TPU v7x, 32 devices: a whole 2x2x4 slice. The times are simulated.
32 devices in a mesh: seq: 16 (over z, x, core), wshard: 2 (over y).
Axes of the slice: x: 2, y: 2, z: 4, core: 2. Of those that a mesh axis runs over, the one named last changes fastest.
Arguments:
- inputs: float32 [2, 4096, 768], P('wshard', 'seq'), may hold values from -6 to 6
- lengths: int32 [2], P('wshard'), may hold values from 1024 to 4096, as said below
- cotangent: float32 [2, 4096, 768], P('wshard', 'seq'), may hold values from -6 to 6
- query_weight: float32 [768, 768], P('wshard'), may hold values from -0.21875 to 0.21875
- query_bias: float32 [768], P('wshard'), may hold values from -2 to 2
- key_weight: float32 [768, 768], P('wshard'), may hold values from -0.21875 to 0.21875
- value_weight: float32 [768, 768], P('wshard'), may hold values from -0.21875 to 0.21875
- value_bias: float32 [768], P('wshard'), may hold values from -2 to 2
- output_weight: float32 [768, 768], P('wshard'), may hold values from -6 to 6
- output_bias: float32 [768], P('wshard'), may hold values from -2 to 2
- first_gain: float32 [768], P('wshard'), may hold values from 0.25 to 1.75
- first_shift: float32 [768], P('wshard'), may hold values from -2 to 2
- up_weight: float32 [768, 3072], P('wshard'), may hold values from -0.21875 to 0.21875
- up_bias: float32 [3072], P('wshard'), may hold values from -2 to 2
- down_weight: float32 [3072, 768], P('wshard'), may hold values from -0.109375 to 0.109375
- down_bias: float32 [768], P('wshard'), may hold values from -2 to 2
- second_gain: float32 [768], P('wshard'), may hold values from 0.25 to 1.75
- second_shift: float32 [768], P('wshard'), may hold values from -2 to 2
Outputs:
- outputs: float32 [2, 4096, 768], P('wshard', 'seq')
- input_grad: float32 [2, 4096, 768], P('wshard', 'seq')
- grad_query_weight: float32 [768, 768], P('wshard')
- grad_query_bias: float32 [768], P('wshard')
- grad_key_weight: float32 [768, 768], P('wshard')
- grad_value_weight: float32 [768, 768], P('wshard')
- grad_value_bias: float32 [768], P('wshard')
- grad_output_weight: float32 [768, 768], P('wshard')
- grad_output_bias: float32 [768], P('wshard')
- grad_first_gain: float32 [768], P('wshard')
- grad_first_shift: float32 [768], P('wshard')
- grad_up_weight: float32 [768, 3072], P('wshard')
- grad_up_bias: float32 [3072], P('wshard')
- grad_down_weight: float32 [3072, 768], P('wshard')
- grad_down_bias: float32 [768], P('wshard')
- grad_second_gain: float32 [768], P('wshard')
- grad_second_shift: float32 [768], P('wshard')
Inputs may be any that keep to these rules, and one draw needn't show every extreme that they name: `lengths`: some sequence has all 4096 positions valid in every draw.
All inputs are finite; a program needn't handle non-finite values.
Results may differ from a plain program's by a relative error of at most 0.024.
Values may be sent and summed in bfloat16 or wider, within the bound.
No kernel may reach another device: no remote copies, remote signals or barrier semaphores. Data moves between devices by JAX's collectives and lax.ppermute only.
A program may use at most 256 MiB of HBM per device.

v0:
```python
from functools import partial

import jax
import jax.numpy as jnp
from jax import lax
from jax.sharding import PartitionSpec as P

HEADS = 12


NEG_FILL = -1e30


def layer_norm(features, norm_gain, norm_shift):
    average = jnp.mean(features, axis=-1, keepdims=True)
    centered = features - average
    variance = jnp.mean(centered * centered, axis=-1, keepdims=True)
    return centered * lax.rsqrt(variance + 1e-12) * norm_gain + norm_shift


def matmul(left_side, right_side):
    return jnp.dot(left_side, right_side, preferred_element_type=jnp.float32)


def left_trans(left_side, right_side):
    return lax.dot_general(
        left_side, right_side, (((0,), (0,)), ((), ())), preferred_element_type=jnp.float32
    )


def right_trans(left_side, right_side):
    return lax.dot_general(
        left_side, right_side, (((1,), (1,)), ((), ())), preferred_element_type=jnp.float32
    )


def sub_block():
    return 512


def fold_keys(running, pieces, query_heads, length):
    key_piece, value_piece = pieces
    piece_rows = key_piece.shape[0]
    block_rows = sub_block()
    block_count = piece_rows // block_rows
    head_count = query_heads.shape[1]
    head_dim = query_heads.shape[2]
    key_blocks = key_piece.reshape(block_count, block_rows, head_count, head_dim)
    value_blocks = value_piece.reshape(block_count, block_rows, head_count, head_dim)
    offsets = jnp.arange(block_count, dtype=jnp.int32) * block_rows

    def one_block(loop_carry, sliced):
        key_block, value_block, offset = sliced
        running_max, weight_sum, running_out = loop_carry
        scores = jnp.einsum(
            "qhd,khd->hqk", query_heads, key_block, preferred_element_type=jnp.float32
        ) * head_dim ** (-0.5)
        key_valid = offset + jnp.arange(block_rows, dtype=jnp.int32) < length
        masked = jnp.where(key_valid[None, None, :], scores, NEG_FILL)
        new_max = jnp.maximum(running_max, jnp.max(masked, axis=-1))
        weights = jnp.where(key_valid[None, None, :], jnp.exp(scores - new_max[..., None]), 0.0)
        rescale = jnp.exp(running_max - new_max)
        weight_sum = weight_sum * rescale + jnp.sum(weights, axis=-1)
        running_out = running_out * rescale[..., None] + jnp.einsum(
            "hqk,khd->hqd",
            weights.astype(jnp.bfloat16),
            value_block,
            preferred_element_type=jnp.float32,
        )
        return ((new_max, weight_sum, running_out), None)

    running, _ = lax.scan(one_block, running, (key_blocks, value_blocks, offsets))
    return running


def key_block_grads(
    query_heads, out_heads, log_sum, delta, key_block, value_block, key_places, length
):
    head_dim = query_heads.shape[2]
    factor = head_dim ** (-0.5)
    key_valid = key_places < length
    scores = (
        jnp.einsum("qhd,khd->hqk", query_heads, key_block, preferred_element_type=jnp.float32)
        * factor
    )
    probabilities = jnp.where(key_valid[None, None, :], jnp.exp(scores - log_sum[..., None]), 0.0)
    value_grad = jnp.einsum(
        "hqk,qhd->khd",
        probabilities.astype(jnp.bfloat16),
        out_heads,
        preferred_element_type=jnp.float32,
    )
    prob_grad = jnp.einsum(
        "qhd,khd->hqk", out_heads, value_block, preferred_element_type=jnp.float32
    )
    score_grad = (probabilities * (prob_grad - delta[..., None])).astype(jnp.bfloat16)
    query_grad = (
        jnp.einsum("hqk,khd->qhd", score_grad, key_block, preferred_element_type=jnp.float32)
        * factor
    )
    key_grad = (
        jnp.einsum("hqk,qhd->khd", score_grad, query_heads, preferred_element_type=jnp.float32)
        * factor
    )
    return (query_grad, key_grad, value_grad)


def body(
    inputs,
    lengths,
    cotangent,
    query_weight,
    query_bias,
    key_weight,
    value_weight,
    value_bias,
    output_weight,
    output_bias,
    first_gain,
    first_shift,
    up_weight,
    up_bias,
    down_weight,
    down_bias,
    second_gain,
    second_shift,
):
    shards = [
        query_weight,
        query_bias,
        key_weight,
        value_weight,
        value_bias,
        output_weight,
        output_bias,
        first_gain,
        first_shift,
        up_weight,
        up_bias,
        down_weight,
        down_bias,
        second_gain,
        second_shift,
    ]
    low_shards = [shard_item.astype(jnp.bfloat16) for shard_item in shards]
    gathered = (
        lax.all_gather(low_shards[0], "wshard", axis=0, tiled=True),
        lax.all_gather(low_shards[1], "wshard", axis=0, tiled=True),
        lax.all_gather(low_shards[2], "wshard", axis=0, tiled=True),
        lax.all_gather(low_shards[3], "wshard", axis=0, tiled=True),
        lax.all_gather(low_shards[4], "wshard", axis=0, tiled=True),
        lax.all_gather(low_shards[5], "wshard", axis=0, tiled=True),
        lax.all_gather(low_shards[6], "wshard", axis=0, tiled=True),
        lax.all_gather(low_shards[7], "wshard", axis=0, tiled=True),
        lax.all_gather(low_shards[8], "wshard", axis=0, tiled=True),
        lax.all_gather(low_shards[9], "wshard", axis=0, tiled=True),
        lax.all_gather(low_shards[10], "wshard", axis=0, tiled=True),
        lax.all_gather(low_shards[11], "wshard", axis=0, tiled=True),
        lax.all_gather(low_shards[12], "wshard", axis=0, tiled=True),
        lax.all_gather(low_shards[13], "wshard", axis=0, tiled=True),
        lax.all_gather(low_shards[14], "wshard", axis=0, tiled=True),
    )
    (
        query_full,
        query_offset,
        key_full,
        value_full,
        value_offset,
        out_full,
        out_offset,
        first_scale,
        first_offset,
        up_full,
        up_offset,
        down_full,
        down_offset,
        second_scale,
        second_offset,
    ) = gathered
    tokens = inputs[0]
    local_rows = tokens.shape[0]
    model_width = tokens.shape[1]
    head_count = HEADS
    head_dim = model_width // head_count
    length = lengths[0]
    my_index = lax.axis_index("seq")
    positions = my_index * local_rows + jnp.arange(local_rows, dtype=jnp.int32)
    low_tokens = tokens.astype(jnp.bfloat16)
    queries = (matmul(low_tokens, query_full) + query_offset.astype(jnp.float32)).astype(
        jnp.bfloat16
    )
    key_rows = matmul(low_tokens, key_full).astype(jnp.bfloat16)
    value_rows = (matmul(low_tokens, value_full) + value_offset.astype(jnp.float32)).astype(
        jnp.bfloat16
    )
    query_heads = queries.reshape(local_rows, head_count, head_dim)
    start_state = (
        jnp.full((head_count, local_rows), NEG_FILL, jnp.float32),
        jnp.zeros((head_count, local_rows), jnp.float32),
        jnp.zeros((head_count, local_rows, head_dim), jnp.float32),
    )
    running_max, weight_sum, running_out = fold_keys(
        start_state,
        (
            lax.all_gather(key_rows, "seq", axis=0, tiled=True),
            lax.all_gather(value_rows, "seq", axis=0, tiled=True),
        ),
        query_heads,
        length,
    )
    log_sum = running_max + jnp.log(weight_sum)
    attended = jnp.transpose(running_out / weight_sum[..., None], (1, 0, 2))
    low_mixed = attended.reshape(local_rows, model_width).astype(jnp.bfloat16)
    branch = matmul(low_mixed, out_full) + out_offset.astype(jnp.float32)
    normed, first_pull = jax.vjp(
        layer_norm,
        tokens + branch,
        first_scale.astype(jnp.float32),
        first_offset.astype(jnp.float32),
    )
    low_normed = normed.astype(jnp.bfloat16)
    pre_act = matmul(low_normed, up_full) + up_offset.astype(jnp.float32)
    activated, gelu_pull = jax.vjp(partial(jax.nn.gelu, approximate=False), pre_act)
    low_act = activated.astype(jnp.bfloat16)
    ffn_out = matmul(low_act, down_full) + down_offset.astype(jnp.float32)
    outputs, second_pull = jax.vjp(
        layer_norm,
        normed + ffn_out,
        second_scale.astype(jnp.float32),
        second_offset.astype(jnp.float32),
    )
    regathered = (
        lax.all_gather(low_shards[0], "wshard", axis=0, tiled=True),
        lax.all_gather(low_shards[1], "wshard", axis=0, tiled=True),
        lax.all_gather(low_shards[2], "wshard", axis=0, tiled=True),
        lax.all_gather(low_shards[3], "wshard", axis=0, tiled=True),
        lax.all_gather(low_shards[4], "wshard", axis=0, tiled=True),
        lax.all_gather(low_shards[5], "wshard", axis=0, tiled=True),
        lax.all_gather(low_shards[6], "wshard", axis=0, tiled=True),
        lax.all_gather(low_shards[7], "wshard", axis=0, tiled=True),
        lax.all_gather(low_shards[8], "wshard", axis=0, tiled=True),
        lax.all_gather(low_shards[9], "wshard", axis=0, tiled=True),
        lax.all_gather(low_shards[10], "wshard", axis=0, tiled=True),
        lax.all_gather(low_shards[11], "wshard", axis=0, tiled=True),
        lax.all_gather(low_shards[12], "wshard", axis=0, tiled=True),
        lax.all_gather(low_shards[13], "wshard", axis=0, tiled=True),
        lax.all_gather(low_shards[14], "wshard", axis=0, tiled=True),
    )
    query_back = regathered[0]
    key_back = regathered[2]
    value_back = regathered[3]
    out_back = regathered[5]
    up_back = regathered[9]
    down_back = regathered[11]
    valid = (positions < length).astype(jnp.float32)
    seed_grad = cotangent[0] * valid[:, None]
    sum_grad, grad_second_gain, grad_second_shift = second_pull(seed_grad)
    ffn_grad = sum_grad.astype(jnp.bfloat16)
    grad_down_weight = left_trans(low_act, ffn_grad)
    grad_down_bias = jnp.sum(ffn_grad.astype(jnp.float32), axis=0)
    (act_grad,) = gelu_pull(right_trans(ffn_grad, down_back))
    pre_grad = act_grad.astype(jnp.bfloat16)
    grad_up_weight = left_trans(low_normed, pre_grad)
    grad_up_bias = jnp.sum(pre_grad.astype(jnp.float32), axis=0)
    normed_grad = right_trans(pre_grad, up_back) + sum_grad
    resid_grad, grad_first_gain, grad_first_shift = first_pull(normed_grad)
    branch_grad = resid_grad.astype(jnp.bfloat16)
    grad_output_weight = left_trans(low_mixed, branch_grad)
    grad_output_bias = jnp.sum(branch_grad.astype(jnp.float32), axis=0)
    mixed_grad = right_trans(branch_grad, out_back).astype(jnp.bfloat16)
    out_heads = mixed_grad.reshape(local_rows, head_count, head_dim)
    delta = jnp.einsum("qhd,qhd->hq", out_heads.astype(jnp.float32), attended)
    all_keys, all_values = (
        lax.all_gather(key_rows, "seq", axis=0, tiled=True),
        lax.all_gather(value_rows, "seq", axis=0, tiled=True),
    )
    seq_rows = all_keys.shape[0]
    block_rows = sub_block()
    block_count = seq_rows // block_rows

    def scan_fn(query_acc, sliced):
        key_block, value_block, offset = sliced
        key_places = offset + jnp.arange(block_rows, dtype=jnp.int32)
        query_part, key_part, value_part = key_block_grads(
            query_heads, out_heads, log_sum, delta, key_block, value_block, key_places, length
        )
        return (
            query_acc + query_part,
            (
                key_part.reshape(block_rows, model_width),
                value_part.reshape(block_rows, model_width),
            ),
        )

    query_acc, (key_parts, value_parts) = lax.scan(
        scan_fn,
        jnp.zeros((local_rows, head_count, head_dim), jnp.float32),
        (
            all_keys.reshape(block_count, block_rows, head_count, head_dim),
            all_values.reshape(block_count, block_rows, head_count, head_dim),
            jnp.arange(block_count, dtype=jnp.int32) * block_rows,
        ),
    )
    key_grad, value_grad = (
        lax.psum_scatter(
            key_parts.reshape(seq_rows, model_width).astype(jnp.bfloat16),
            "seq",
            scatter_dimension=0,
            tiled=True,
        ).astype(jnp.float32),
        lax.psum_scatter(
            value_parts.reshape(seq_rows, model_width).astype(jnp.bfloat16),
            "seq",
            scatter_dimension=0,
            tiled=True,
        ).astype(jnp.float32),
    )
    query_low = query_acc.reshape(local_rows, model_width).astype(jnp.bfloat16)
    key_low = key_grad.astype(jnp.bfloat16)
    value_low = value_grad.astype(jnp.bfloat16)
    grad_query_weight = left_trans(low_tokens, query_low)
    grad_query_bias = jnp.sum(query_low.astype(jnp.float32), axis=0)
    grad_key_weight = left_trans(low_tokens, key_low)
    grad_value_weight = left_trans(low_tokens, value_low)
    grad_value_bias = jnp.sum(value_low.astype(jnp.float32), axis=0)
    input_grad = (
        resid_grad
        + right_trans(query_low, query_back)
        + right_trans(key_low, key_back)
        + right_trans(value_low, value_back)
    )
    parted = (
        lax.psum_scatter(
            grad_query_weight.astype(jnp.bfloat16), "wshard", scatter_dimension=0, tiled=True
        ).astype(jnp.float32),
        lax.psum_scatter(
            grad_query_bias.astype(jnp.bfloat16), "wshard", scatter_dimension=0, tiled=True
        ).astype(jnp.float32),
        lax.psum_scatter(
            grad_key_weight.astype(jnp.bfloat16), "wshard", scatter_dimension=0, tiled=True
        ).astype(jnp.float32),
        lax.psum_scatter(
            grad_value_weight.astype(jnp.bfloat16), "wshard", scatter_dimension=0, tiled=True
        ).astype(jnp.float32),
        lax.psum_scatter(
            grad_value_bias.astype(jnp.bfloat16), "wshard", scatter_dimension=0, tiled=True
        ).astype(jnp.float32),
        lax.psum_scatter(
            grad_output_weight.astype(jnp.bfloat16), "wshard", scatter_dimension=0, tiled=True
        ).astype(jnp.float32),
        lax.psum_scatter(
            grad_output_bias.astype(jnp.bfloat16), "wshard", scatter_dimension=0, tiled=True
        ).astype(jnp.float32),
        lax.psum_scatter(
            grad_first_gain.astype(jnp.bfloat16), "wshard", scatter_dimension=0, tiled=True
        ).astype(jnp.float32),
        lax.psum_scatter(
            grad_first_shift.astype(jnp.bfloat16), "wshard", scatter_dimension=0, tiled=True
        ).astype(jnp.float32),
        lax.psum_scatter(
            grad_up_weight.astype(jnp.bfloat16), "wshard", scatter_dimension=0, tiled=True
        ).astype(jnp.float32),
        lax.psum_scatter(
            grad_up_bias.astype(jnp.bfloat16), "wshard", scatter_dimension=0, tiled=True
        ).astype(jnp.float32),
        lax.psum_scatter(
            grad_down_weight.astype(jnp.bfloat16), "wshard", scatter_dimension=0, tiled=True
        ).astype(jnp.float32),
        lax.psum_scatter(
            grad_down_bias.astype(jnp.bfloat16), "wshard", scatter_dimension=0, tiled=True
        ).astype(jnp.float32),
        lax.psum_scatter(
            grad_second_gain.astype(jnp.bfloat16), "wshard", scatter_dimension=0, tiled=True
        ).astype(jnp.float32),
        lax.psum_scatter(
            grad_second_shift.astype(jnp.bfloat16), "wshard", scatter_dimension=0, tiled=True
        ).astype(jnp.float32),
    )
    totals = (
        lax.psum(parted[0].astype(jnp.bfloat16), "seq").astype(jnp.float32),
        lax.psum(parted[1].astype(jnp.bfloat16), "seq").astype(jnp.float32),
        lax.psum(parted[2].astype(jnp.bfloat16), "seq").astype(jnp.float32),
        lax.psum(parted[3].astype(jnp.bfloat16), "seq").astype(jnp.float32),
        lax.psum(parted[4].astype(jnp.bfloat16), "seq").astype(jnp.float32),
        lax.psum(parted[5].astype(jnp.bfloat16), "seq").astype(jnp.float32),
        lax.psum(parted[6].astype(jnp.bfloat16), "seq").astype(jnp.float32),
        lax.psum(parted[7].astype(jnp.bfloat16), "seq").astype(jnp.float32),
        lax.psum(parted[8].astype(jnp.bfloat16), "seq").astype(jnp.float32),
        lax.psum(parted[9].astype(jnp.bfloat16), "seq").astype(jnp.float32),
        lax.psum(parted[10].astype(jnp.bfloat16), "seq").astype(jnp.float32),
        lax.psum(parted[11].astype(jnp.bfloat16), "seq").astype(jnp.float32),
        lax.psum(parted[12].astype(jnp.bfloat16), "seq").astype(jnp.float32),
        lax.psum(parted[13].astype(jnp.bfloat16), "seq").astype(jnp.float32),
        lax.psum(parted[14].astype(jnp.bfloat16), "seq").astype(jnp.float32),
    )
    return (outputs[None], input_grad[None]) + tuple(totals)


def solution(mesh):
    placed = (
        P("wshard", "seq", None),
        P("wshard"),
        P("wshard", "seq", None),
        P("wshard", None),
        P("wshard"),
        P("wshard", None),
        P("wshard", None),
        P("wshard"),
        P("wshard", None),
        P("wshard"),
        P("wshard"),
        P("wshard"),
        P("wshard", None),
        P("wshard"),
        P("wshard", None),
        P("wshard"),
        P("wshard"),
        P("wshard"),
    )
    return jax.shard_map(
        body,
        mesh=mesh,
        in_specs=placed,
        out_specs=(
            P("wshard", "seq", None),
            P("wshard", "seq", None),
            P("wshard", None),
            P("wshard"),
            P("wshard", None),
            P("wshard", None),
            P("wshard"),
            P("wshard", None),
            P("wshard"),
            P("wshard"),
            P("wshard"),
            P("wshard", None),
            P("wshard"),
            P("wshard", None),
            P("wshard"),
            P("wshard"),
            P("wshard"),
        ),
        check_vma=False,
    )
```

profile of v0, /device:TPU:1, one launch (start us, length us, event | category | flops | bytes accessed | tf_op | source)
XLA Modules:
  0.0 1149.4 jit_solution(9357363706525144808)
XLA Ops:
  11.6 23.4 %all-gather.18.cloned.1.call-done = bf16[768,768]{1,0:T(8,128)(2,1)} async-done(((bf16[384,768]{1,0:T(8,128)(2,1)}), bf16[768,768]{1,0:T(8,128)(2,1)}) %all-gather.18.cloned.1.call-update) | async-done | bytes 1179664 | tf_op jit(solution)/shard_map/all_gather | solution.py:149
  40.9 19.1 %all-gather.24.cloned.1.call-done = bf16[768,768]{1,0:T(8,128)(2,1)} async-done(((bf16[384,768]{1,0:T(8,128)(2,1)}), bf16[768,768]{1,0:T(8,128)(2,1)}) %all-gather.24.cloned.1.call-update) | async-done | bytes 1179664 | tf_op jit(solution)/shard_map/all_gather | solution.py:150
  106.3 43.9 %all-gather.20.cloned.1.call-done = bf16[4096,768]{1,0:T(8,128)(2,1)} async-done(((bf16[256,768]{1,0:T(8,128)(2,1)}), bf16[4096,768]{1,0:T(8,128)(2,1)}) %all-gather.20.cloned.1.call-update) | async-done | bytes 6291472 | tf_op jit(solution)/shard_map/all_gather | solution.py:205
  150.1 8.6 copy.61
  158.7 7.2 copy.106
  170.8 42.5 %all-gather.26.cloned.1.call-done = bf16[4096,768]{1,0:T(8,128)(2,1)} async-done(((bf16[256,768]{1,0:T(8,128)(2,1)}), bf16[4096,768]{1,0:T(8,128)(2,1)}) %all-gather.26.cloned.1.call-update) | async-done | bytes 6291472 | tf_op jit(solution)/shard_map/all_gather | solution.py:206
  213.3 9.1 copy.63
  222.4 7.0 copy.107
  234.3 116.3 %while.30 = (s32[]{:T(128)}, f32[12,256]{1,0:T(8,128)S(1)}, f32[12,256]{1,0:T(8,128)S(1)}, f32[12,256,64]{1,2,0:T(8,128)S(1)}, s32[8]{0:T(128)S(1)}, /*index=5*/...) while((s32[]{:T(128)}, f32[12,256]{1,0:T(8,128)S(1)}, ...), condition=%wide.region_3.4_spmd.clone, body=%wide.region_0.3_spmd.clone.sunk | while | flops 420560896 | bytes 47777976 | solution.py:72
  236.2 5.3 select_reduce_fusion.2
  251.3 5.4 select_reduce_fusion.2
  265.7 5.3 select_reduce_fusion.2
  280.0 5.3 select_reduce_fusion.2
  294.3 5.3 select_reduce_fusion.2
  308.7 5.5 select_reduce_fusion.2
  323.8 5.3 select_reduce_fusion.2
  338.1 5.3 select_reduce_fusion.2
  353.6 11.5 %multiply_convert_fusion.1 = (bf16[256,3072]{1,0:T(8,128)(2,1)S(1)}, f32[256,3072]{1,0:T(8,128)}, f32[256,3072]{1,0:T(8,128)}) fusion(f32[3072]{0:T(1024)} %bitcast.183, bf16[768,3072]{1,0:T(8,128)(2,1)} %all-gather.30.cloned.1.call-done, f32[256,768]{1,0:T(8,128)S(1)} %get-tuple-element.413, f32[768]{0:T(1024)} %reshape.179, f32[768]{0:T(1024)} %reshape.178, ...), kind=kOutput, calls=%fused_computation.55 | convolution fusion | flops 1260847104 | bytes 13389824 | tf_op jit(solution)/shard_map/dot_general | solution.py:22
  384.6 190.5 %while.31 = (s32[]{:T(128)}, f32[256,12,64]{0,2,1:T(8,128)}, bf16[8,512,768]{2,1,0:T(8,128)(2,1)}, bf16[8,512,768]{2,1,0:T(8,128)(2,1)}, bf16[8,512,12,64]{1,3,2...) while((s32[]{:T(128)}, f32[256,12,64]{0,2,1:T(8,128)}, ...), condition=%wide.region_13.14_spmd.clone, body=%wide.region_12.13_spmd.clone.sunk | while | flops 1023738880 | bytes 67037188 | solution.py:295
  419.2 4.9 fusion.139
  578.5 81.1 %reduce-scatter.15.cloned.1.call-done = bf16[256,768]{1,0:T(8,128)(2,1)} async-done(((bf16[4096,768]{1,0:T(8,128)(2,1)}), bf16[256,768]{1,0:T(8,128)(2,1)}) %reduce-scatter.15.cloned.1.call-update) | async-done | bytes 393232 | tf_op jit(solution)/shard_map/reduce_scatter | solution.py:305
  662.7 85.7 %reduce-scatter.17.cloned.1.call-done = bf16[256,768]{1,0:T(8,128)(2,1)} async-done(((bf16[4096,768]{1,0:T(8,128)(2,1)}), bf16[256,768]{1,0:T(8,128)(2,1)}) %reduce-scatter.17.cloned.1.call-update) | async-done | bytes 393232 | tf_op jit(solution)/shard_map/reduce_scatter | solution.py:311
  753.0 5.2 convolution_convert_fusion.1
  763.4 9.6 reduce-scatter.25.cloned.1.call-done
  775.0 22.5 %reduce-scatter.27.cloned.1.call-done = bf16[384,768]{1,0:T(8,128)(2,1)} async-done(((bf16[768,768]{1,0:T(8,128)(2,1)}), bf16[384,768]{1,0:T(8,128)(2,1)}) %reduce-scatter.27.cloned.1.call-update) | async-done | bytes 589840
  799.6 22.5 %reduce-scatter.29.cloned.1.call-done = bf16[384,768]{1,0:T(8,128)(2,1)} async-done(((bf16[768,768]{1,0:T(8,128)(2,1)}), bf16[384,768]{1,0:T(8,128)(2,1)}) %reduce-scatter.29.cloned.1.call-update) | async-done | bytes 589840
  824.2 22.5 %reduce-scatter.19.cloned.1.call-done = bf16[384,768]{1,0:T(8,128)(2,1)} async-done(((bf16[768,768]{1,0:T(8,128)(2,1)}), bf16[384,768]{1,0:T(8,128)(2,1)}) %reduce-scatter.19.cloned.1.call-update) | async-done | bytes 589840 | tf_op jit(solution)/shard_map/reduce_scatter | solution.py:348
  846.6 62.7 %reduce-scatter.21.cloned.1.call-done = bf16[384,3072]{1,0:T(8,128)(2,1)} async-done(((bf16[768,3072]{1,0:T(8,128)(2,1)}), bf16[384,3072]{1,0:T(8,128)(2,1)}) %reduce-scatter.21.cloned.1.call-update) | async-done | bytes 2359312 | tf_op jit(solution)/shard_map/reduce_scatter | solution.py:360
  909.4 62.9 %reduce-scatter.23.cloned.1.call-done = bf16[1536,768]{1,0:T(8,128)(2,1)} async-done(((bf16[3072,768]{1,0:T(8,128)(2,1)}), bf16[1536,768]{1,0:T(8,128)(2,1)}) %reduce-scatter.23.cloned.1.call-update) | async-done | bytes 2359312 | tf_op jit(solution)/shard_map/reduce_scatter | solution.py:366
  977.7 5.4 all-reduce.11
  983.8 59.6 %all-reduce.9 = (bf16[384]{0:T(512)(128)(2,1)S(1)}, bf16[384]{0:T(512)(128)(2,1)S(1)}, bf16[384]{0:T(512)(128)(2,1)S(1)}, bf16[384]{0:T(512)(128)(2,1)S(1)}, bf1...) all-reduce(bf16[384]{0:T(512)(128)(2,1)S(1)} %dynamic-slice.1, ...), channel_id=1, replica_groups=mesh['seq'=16,'wshard'=2] {'seq'}, use_global_device_ids=true, to_apply=%region_20.21 | all-reduce | flops 4608 | bytes 18432 | tf_op jit(solution)/shard_map/psum | solution.py:381
  1051.7 78.3 %all-reduce.14.cloned.1.call-done = (bf16[384,768]{0,1:T(8,128)(2,1)}, bf16[384,768]{0,1:T(8,128)(2,1)}, bf16[384,768]{0,1:T(8,128)(2,1)}, bf16[384,768]{1,0:T(8...) async-done(((bf16[384,768]{0,1:T(8,128)(2,1)}, bf16[384,768]{0,1:T(8,128)(2,1)}, bf16[384,768]{0,1:T(8,128)(2,1)}, bf16[384,768]{1,0:T(8,128)(2,1)}, ...) | async-done | bytes 7077904 | tf_op jit(solution)/shard_map/psum | solution.py:380
  (572 shorter events, 392.9 us)
Async XLA Ops:
  7.2 27.8 %all-gather.18.cloned.1.call-start = ((), (), s32[]{:S(2)}) async-start(), calls=%async_computation.8 | async-start | bytes 1769472 | tf_op jit(solution)/shard_map/all_gather | solution.py:149
  9.6 50.4 %all-gather.24.cloned.1.call-start = ((), (), s32[]{:S(2)}) async-start(), calls=%async_computation.11 | async-start | bytes 1769472 | tf_op jit(solution)/shard_map/all_gather | solution.py:150
  10.5 27.1 %copy-start.55 = (f32[384]{0:T(512)S(1)}, f32[384]{0:T(512)}, u32[]{:S(2)}) copy-start(f32[384]{0:T(512)} %param.29) | copy-start | bytes 4612
  10.5 93.8 %all-gather.22.cloned.1.call-start = ((), (), s32[]{:S(2)}) async-start(), calls=%async_computation.10 | async-start | bytes 1769472 | tf_op jit(solution)/shard_map/all_gather | solution.py:147
  11.5 51.1 %copy-start.30 = (f32[384,768]{1,0:T(8,128)S(1)}, f32[384,768]{1,0:T(8,128)}, u32[]{:S(2)}) copy-start(f32[384,768]{1,0:T(8,128)} %param.30) | copy-start | bytes 3538948
  11.5 138.6 %all-gather.20.cloned.1.call-start = ((), (), s32[]{:S(2)}) async-start(), calls=%async_computation.9 | async-start | bytes 6684672 | tf_op jit(solution)/shard_map/all_gather | solution.py:205
  11.6 92.7 %copy-start.9 = (bf16[256,768]{1,0:T(8,128)(2,1)}, bf16[256,768]{1,0:T(8,128)(2,1)S(1)}, u32[]{:S(2)}) copy-start(bf16[256,768]{1,0:T(8,128)(2,1)S(1)} %bitcast_convert_fusion.5) | copy-start | bytes 1179652
  37.6 175.7 %all-gather.26.cloned.1.call-start = ((), (), s32[]{:S(2)}) async-start(), calls=%async_computation.12 | async-start | bytes 6684672 | tf_op jit(solution)/shard_map/all_gather | solution.py:206
  62.5 288.2 %all-gather.28.cloned.1.call-start = ((), (), s32[]{:S(2)}) async-start(), calls=%async_computation.13 | async-start | bytes 1769472 | tf_op jit(solution)/shard_map/all_gather | solution.py:152
  63.5 290.0 %all-gather.30.cloned.1.call-start = ((), (), s32[]{:S(2)}) async-start(), calls=%async_computation.14 | async-start | bytes 7077888 | tf_op jit(solution)/shard_map/all_gather | solution.py:156
  67.7 13.0 %copy-start.57 = (f32[384]{0:T(512)S(1)}, f32[384]{0:T(512)}, u32[]{:S(2)}) copy-start(f32[384]{0:T(512)} %param.31) | copy-start | bytes 4612
  67.7 16.6 %copy-start.58 = (f32[384]{0:T(512)S(1)}, f32[384]{0:T(512)}, u32[]{:S(2)}) copy-start(f32[384]{0:T(512)} %param.26) | copy-start | bytes 4612
  67.7 19.8 %copy-start.59 = (f32[384]{0:T(512)S(1)}, f32[384]{0:T(512)}, u32[]{:S(2)}) copy-start(f32[384]{0:T(512)} %param.33) | copy-start | bytes 4612
  67.7 23.6 %copy-start.60 = (f32[384]{0:T(512)S(1)}, f32[384]{0:T(512)}, u32[]{:S(2)}) copy-start(f32[384]{0:T(512)} %param.32) | copy-start | bytes 4612
  67.7 28.1 %copy-start.61 = (f32[384]{0:T(512)S(1)}, f32[384]{0:T(512)}, u32[]{:S(2)}) copy-start(f32[384]{0:T(512)} %param.38) | copy-start | bytes 4612
  67.7 31.9 %copy-start.62 = (f32[384]{0:T(512)S(1)}, f32[384]{0:T(512)}, u32[]{:S(2)}) copy-start(f32[384]{0:T(512)} %param.39) | copy-start | bytes 4612
  67.7 297.6 %all-gather.32.cloned.1.call-start = ((), (), s32[]{:S(2)}) async-start(), calls=%async_computation.15 | async-start | bytes 7077888 | tf_op jit(solution)/shard_map/all_gather | solution.py:158
  72.1 587.5 %reduce-scatter.15.cloned.1.call-start = ((), (), s32[]{:S(2)}) async-start(), calls=%async_computation.16 | async-start | bytes 6684672 | tf_op jit(solution)/shard_map/reduce_scatter | solution.py:305
  352.7 26.0 %copy-start.3 = (f32[256,768]{1,0:T(8,128)}, f32[256,768]{1,0:T(8,128)S(1)}, u32[]{:S(2)}) copy-start(f32[256,768]{1,0:T(8,128)S(1)} %get-tuple-element.413) | copy-start | bytes 2359300
  575.1 173.2 %reduce-scatter.17.cloned.1.call-start = ((), (), s32[]{:S(2)}) async-start(), calls=%async_computation.17 | async-start | bytes 6684672 | tf_op jit(solution)/shard_map/reduce_scatter | solution.py:311
  575.7 197.2 %reduce-scatter.25.cloned.1.call-start = ((), (), s32[]{:S(2)}) async-start(), calls=%async_computation.21 | async-start | bytes 1769472
  576.5 83.1 %copy-start.10 = (bf16[256,768]{1,0:T(8,128)(2,1)S(1)}, bf16[256,768]{1,0:T(8,128)(2,1)}, u32[]{:S(2)}) copy-start(bf16[256,768]{1,0:T(8,128)(2,1)} %copy-done.9) | copy-start | bytes 1179652
  578.5 219.0 %reduce-scatter.27.cloned.1.call-start = ((), (), s32[]{:S(2)}) async-start(), calls=%async_computation.22 | async-start | bytes 1769472
  662.6 88.8 %copy-start.17 = (bf16[256,12,64]{0,2,1:T(8,128)(2,1)S(1)}, bf16[256,12,64]{0,2,1:T(8,128)(2,1)}, u32[]{:S(2)}) copy-start(bf16[256,12,64]{0,2,1:T(8,128)(2,1)} %copy-done.16) | copy-start | bytes 1179652
  662.6 88.8 %copy-start.19 = (bf16[256,768]{1,0:T(8,128)(2,1)S(1)}, bf16[256,768]{1,0:T(8,128)(2,1)}, u32[]{:S(2)}) copy-start(bf16[256,768]{1,0:T(8,128)(2,1)} %copy-done.18) | copy-start | bytes 1179652
  662.6 159.5 %reduce-scatter.29.cloned.1.call-start = ((), (), s32[]{:S(2)}) async-start(), calls=%async_computation.23 | async-start | bytes 1769472
  751.3 95.3 %reduce-scatter.19.cloned.1.call-start = ((), (), s32[]{:S(2)}) async-start(), calls=%async_computation.18 | async-start | bytes 1769472 | tf_op jit(solution)/shard_map/reduce_scatter | solution.py:348
  752.9 156.4 %reduce-scatter.21.cloned.1.call-start = ((), (), s32[]{:S(2)}) async-start(), calls=%async_computation.19 | async-start | bytes 7077888 | tf_op jit(solution)/shard_map/reduce_scatter | solution.py:360
  758.2 214.0 %reduce-scatter.23.cloned.1.call-start = ((), (), s32[]{:S(2)}) async-start(), calls=%async_computation.20 | async-start | bytes 7077888 | tf_op jit(solution)/shard_map/reduce_scatter | solution.py:366
  763.3 366.7 %all-reduce.14.cloned.1.call-start = ((), (), s32[]{:S(2)}) async-start(), calls=%async_computation.24 | async-start | bytes 14155776 | tf_op jit(solution)/shard_map/psum | solution.py:380
  972.4 76.3 %copy-start.11 = (bf16[768,768]{1,0:T(8,128)(2,1)S(1)}, bf16[768,768]{1,0:T(8,128)(2,1)}, u32[]{:S(2)}) copy-start(bf16[768,768]{1,0:T(8,128)(2,1)} %all-gather.18.cloned.1.call-done) | copy-start | bytes 3538948
  972.4 76.3 %copy-start.25 = (bf16[256,768]{1,0:T(8,128)(2,1)S(1)}, bf16[256,768]{1,0:T(8,128)(2,1)}, u32[]{:S(2)}) copy-start(bf16[256,768]{1,0:T(8,128)(2,1)} %reduce-scatter.15.cloned.1.call-done) | copy-start | bytes 1179652
  (118 other events, 466.3 us)
Sparse Core Ops, SparseCore 0:
  10.2 24.8 all-gather.17
  37.2 22.7 all-gather.23
  62.1 22.9 all-gather.21
  87.8 62.2 all-gather.19
  152.8 60.4 all-gather.25
  215.3 20.9 all-gather.27
  238.4 62.6 all-gather.29
  302.6 62.6 all-gather.31
  575.2 84.3 reduce-scatter.14
  663.9 84.3 reduce-scatter.16
  751.2 21.7 reduce-scatter.24
  775.7 21.7 reduce-scatter.26
  800.3 21.7 reduce-scatter.28
  824.8 21.7 reduce-scatter.18
  849.4 59.9 reduce-scatter.20
  912.2 59.9 reduce-scatter.22
  977.1 152.9 all-reduce.13
where the time goes:
time: 1160 us; the launch traced here: 1150 us
  waiting for transfers between devices  578 us (50%)
  matrix products  236 us (20%)
  local copies, waits for them, and re-layouts  131 us (11%)
  blocking collectives  95.1 us (8%)
  other arithmetic  89.9 us (8%)
  between operations  17.4 us (1%)
    reduce_scatter x1, waiting for transfers between devices, body(): lax.psum_scatter(value_parts.reshape(seq_rows, model_width).astype(jnp.bf...  85.7 us
    reduce_scatter x1, waiting for transfers between devices, body(): lax.psum_scatter(key_parts.reshape(seq_rows, model_width).astype(jnp.bflo...  81.1 us
    psum x1, waiting for transfers between devices, body(): lax.psum(parted[0].astype(jnp.bfloat16), 'seq').astype(jnp.float32)  78.3 us
    reduce_scatter x1, waiting for transfers between devices, body(): lax.psum_scatter(grad_down_weight.astype(jnp.bfloat16), 'wshard', scatter...  62.9 us
    reduce_scatter x1, waiting for transfers between devices, body(): lax.psum_scatter(grad_up_weight.astype(jnp.bfloat16), 'wshard', scatter_d...  62.7 us
    psum x1, blocking collectives, body(): lax.psum(parted[1].astype(jnp.bfloat16), 'seq').astype(jnp.float32)  59.6 us
    unnamed x20, waiting for transfers between devices  55.2 us
    dynamic_update_slice x24, local copies, waits for them, and re-layouts, body(): lax.scan(scan_fn, jnp.zeros((local_rows, head_count, head_dim), jnp.float...  48.9 us
  transfers between devices with their start and end apart: 17, of which 14 were waited for; matrix products, arithmetic and copies ran while one was open for 20% of the time, Pallas kernels for 0%

commit v1 on v0

v1 whole, which is shorter than its diff:
```python
from functools import partial

import jax
import jax.numpy as jnp
from jax import lax
from jax.experimental import pallas as pl
from jax.experimental.pallas import tpu as pltpu
from jax.sharding import Mesh, PartitionSpec as P

HEADS = 12
ZS = 4
NEG_FILL = -1e30
SWAP = ((0, 1), (1, 0))
F32 = jnp.float32
BF16 = jnp.bfloat16


def layer_norm(features, norm_gain, norm_shift):
    average = jnp.mean(features, axis=-1, keepdims=True)
    centered = features - average
    variance = jnp.mean(centered * centered, axis=-1, keepdims=True)
    return centered * lax.rsqrt(variance + 1e-12) * norm_gain + norm_shift


def matmul(left_side, right_side):
    return jnp.dot(left_side, right_side, preferred_element_type=F32)


def left_trans(left_side, right_side):
    return lax.dot_general(
        left_side, right_side, (((0,), (0,)), ((), ())), preferred_element_type=F32
    )


def right_trans(left_side, right_side):
    return lax.dot_general(
        left_side, right_side, (((1,), (1,)), ((), ())), preferred_element_type=F32
    )


def swap(value, axis):
    return lax.ppermute(value, axis, SWAP)


def key_rows_at(length, blocks, rows, outer, per_outer):
    group = per_outer * rows
    left = length - outer * (ZS * group)
    whole = jnp.clip(left // group, 0, ZS)
    touched = jnp.clip((left + group - 1) // group, 0, ZS)
    return whole, touched


def forward_kernel(meta_ref, q_ref, *refs, blocks, rows):
    kv_refs = refs[:blocks]
    out_ref, log_ref = refs[blocks : blocks + 2]
    value_refs = refs[blocks + 2 :]
    head_dim, query_count = q_ref.shape
    length = meta_ref[0]
    for block in range(blocks):
        for part in range(ZS):
            cut = slice(part * rows, (part + 1) * rows)
            value_refs[block][:, cut] = kv_refs[block][cut, :].T[head_dim:, :]
    query = jnp.concatenate([q_ref[...], jnp.zeros((head_dim, query_count), BF16)], axis=0)

    def step(group, carry, members, masked):
        top, total, acc = carry
        start = pl.multiple_of(group * rows, rows)
        found = []
        for block in members:
            scores = matmul(kv_refs[block][pl.ds(start, rows), :], query)
            if masked:
                place = (meta_ref[1 + block] + group * 4) * rows
                place = place + lax.broadcasted_iota(jnp.int32, scores.shape, 0)
                scores = jnp.where(place < length, scores, NEG_FILL)
            found.append(scores)
        new_top = top
        for scores in found:
            new_top = jnp.maximum(new_top, jnp.max(scores, axis=0, keepdims=True))
        fade = jnp.exp(top - new_top)
        total = total * fade
        acc = acc * fade
        for block, scores in zip(members, found):
            weights = jnp.exp(scores - new_top)
            total = total + jnp.sum(weights, axis=0, keepdims=True)
            acc = acc + matmul(
                value_refs[block][:, pl.ds(start, rows)], weights.astype(BF16)
            )
        return new_top, total, acc

    carry = (
        jnp.full((1, query_count), NEG_FILL, F32),
        jnp.zeros((1, query_count), F32),
        jnp.zeros((head_dim, query_count), F32),
    )
    for first in range(0, blocks, 4):
        members = tuple(range(first, first + 4))
        whole, touched = key_rows_at(length, blocks, rows, meta_ref[1 + first] // 16, 4)
        carry = lax.fori_loop(
            0, whole, lambda g, c: step(g, c, members, False), carry
        )
        carry = lax.fori_loop(
            whole, touched, lambda g, c: step(g, c, members, True), carry
        )
    top, total, acc = carry
    out_ref[...] = acc * (1.0 / total)
    log_ref[0] = top + jnp.log(total)


def attend_forward(meta, queries, kv_blocks):
    blocks = len(kv_blocks)
    block_rows, width = kv_blocks[0].shape
    heads = width // 128
    head_dim = queries.shape[0] // heads
    query_count = queries.shape[1]
    head_rows = pl.BlockSpec((head_dim, query_count), lambda h, m: (h, 0))
    head_cols = pl.BlockSpec((block_rows, 128), lambda h, m: (0, h))
    head_stat = pl.BlockSpec((1, 1, query_count), lambda h, m: (h, 0, 0))
    keys = blocks * block_rows
    return pl.pallas_call(
        partial(forward_kernel, blocks=blocks, rows=block_rows // ZS),
        grid_spec=pltpu.PrefetchScalarGridSpec(
            num_scalar_prefetch=1,
            grid=(heads,),
            in_specs=[head_rows] + [head_cols] * blocks,
            out_specs=[head_rows, head_stat],
            scratch_shapes=[pltpu.VMEM((head_dim, block_rows), BF16)] * blocks,
        ),
        out_shape=[
            jax.ShapeDtypeStruct((heads * head_dim, query_count), F32),
            jax.ShapeDtypeStruct((heads, 1, query_count), F32),
        ],
        compiler_params=pltpu.CompilerParams(vmem_limit_bytes=56 << 20),
        cost_estimate=pl.CostEstimate(
            flops=4 * heads * query_count * keys * head_dim * 4,
            bytes_accessed=keys * width * 2,
            transcendentals=heads * query_count * keys,
        ),
        name="attend_forward",
    )(meta, queries, *kv_blocks)


def backward_kernel(meta_ref, q_ref, go_ref, out_ref, log_ref, *refs, blocks, rows):
    kv_refs = refs[:blocks]
    dq_ref = refs[blocks]
    dkv_refs = refs[blocks + 1 : 2 * blocks + 1]
    key_refs = refs[2 * blocks + 1 : 3 * blocks + 1]
    qn_ref, gn_ref, acc_ref = refs[3 * blocks + 1 :]
    head_dim, query_count = q_ref.shape
    length = meta_ref[0]
    blank = jnp.zeros((head_dim, query_count), BF16)
    for block in range(blocks):
        for part in range(ZS):
            cut = slice(part * rows, (part + 1) * rows)
            key_refs[block][:, cut] = kv_refs[block][cut, :].T[:head_dim, :]
    query = jnp.concatenate([q_ref[...], blank], axis=0)
    grad = jnp.concatenate([blank, go_ref[...]], axis=0)
    qn_ref[...] = query.T
    gn_ref[...] = grad.T
    delta = jnp.sum(go_ref[...].astype(F32) * out_ref[...], axis=0, keepdims=True)
    log_sum = log_ref[0]
    acc_ref[...] = jnp.zeros_like(acc_ref)

    def step(group, members, masked):
        start = pl.multiple_of(group * rows, rows)
        for block in members:
            kv = kv_refs[block][pl.ds(start, rows), :]
            scores = matmul(kv, query)
            prob_grad = matmul(kv, grad)
            prob = jnp.exp(scores - log_sum)
            if masked:
                place = (meta_ref[1 + block] + group * 4) * rows
                place = place + lax.broadcasted_iota(jnp.int32, scores.shape, 0)
                prob = jnp.where(place < length, prob, 0.0)
            score_grad = (prob * (prob_grad - delta)).astype(BF16)
            dkv_refs[block][pl.ds(start, rows), :] = (
                matmul(prob.astype(BF16), gn_ref[...]) + matmul(score_grad, qn_ref[...])
            ).astype(BF16)
            acc_ref[...] += matmul(key_refs[block][:, pl.ds(start, rows)], score_grad)

    def clear(group, members):
        start = pl.multiple_of(group * rows, rows)
        for block in members:
            dkv_refs[block][pl.ds(start, rows), :] = jnp.zeros((rows, 128), BF16)

    def loop(low, high, fn):
        def one(group, carry):
            fn(group)
            return carry

        lax.fori_loop(low, high, one, 0)

    for first in range(0, blocks, 4):
        members = tuple(range(first, first + 4))
        whole, touched = key_rows_at(length, blocks, rows, meta_ref[1 + first] // 16, 4)
        loop(0, whole, lambda g: step(g, members, False))
        loop(whole, touched, lambda g: step(g, members, True))
        loop(touched, ZS, lambda g: clear(g, members))
    dq_ref[...] = (acc_ref[...] * head_dim ** (-0.5)).astype(BF16)


def attend_backward(meta, queries, grads, outs, logs, kv_blocks):
    blocks = len(kv_blocks)
    block_rows, width = kv_blocks[0].shape
    heads = width // 128
    head_dim = queries.shape[0] // heads
    query_count = queries.shape[1]
    head_rows = pl.BlockSpec((head_dim, query_count), lambda h, m: (h, 0))
    head_cols = pl.BlockSpec((block_rows, 128), lambda h, m: (0, h))
    head_stat = pl.BlockSpec((1, 1, query_count), lambda h, m: (h, 0, 0))
    keys = blocks * block_rows
    return pl.pallas_call(
        partial(backward_kernel, blocks=blocks, rows=block_rows // ZS),
        grid_spec=pltpu.PrefetchScalarGridSpec(
            num_scalar_prefetch=1,
            grid=(heads,),
            in_specs=[head_rows, head_rows, head_rows, head_stat] + [head_cols] * blocks,
            out_specs=[head_rows] + [head_cols] * blocks,
            scratch_shapes=[pltpu.VMEM((head_dim, block_rows), BF16)] * blocks
            + [
                pltpu.VMEM((query_count, 128), BF16),
                pltpu.VMEM((query_count, 128), BF16),
                pltpu.VMEM((head_dim, query_count), F32),
            ],
        ),
        out_shape=[jax.ShapeDtypeStruct((heads * head_dim, query_count), BF16)]
        + [jax.ShapeDtypeStruct((block_rows, width), BF16)] * blocks,
        compiler_params=pltpu.CompilerParams(vmem_limit_bytes=56 << 20),
        cost_estimate=pl.CostEstimate(
            flops=10 * heads * query_count * keys * head_dim * 4,
            bytes_accessed=2 * keys * width * 2,
            transcendentals=heads * query_count * keys,
        ),
        name="attend_backward",
    )(meta, queries, grads, outs, logs, *kv_blocks)


def in_order(index, own, other, axis):
    return jnp.where(
        index == 0,
        jnp.concatenate([own, other], axis=axis),
        jnp.concatenate([other, own], axis=axis),
    )


def part_of(value, index, count, axis):
    size = value.shape[axis] // count
    return lax.dynamic_slice_in_dim(value, index * size, size, axis)


def body(
    inputs,
    lengths,
    cotangent,
    query_weight,
    query_bias,
    key_weight,
    value_weight,
    value_bias,
    output_weight,
    output_bias,
    first_gain,
    first_shift,
    up_weight,
    up_bias,
    down_weight,
    down_bias,
    second_gain,
    second_shift,
    *,
    sizes,
):
    count_o, count_w = sizes
    w_at = lax.axis_index("w")
    z_at = lax.axis_index("z")
    c_at = lax.axis_index("c")
    x_at = lax.axis_index("x")
    o_at = lax.axis_index("o")
    tokens = inputs[0]
    local_rows, width = tokens.shape
    head_dim = width // HEADS
    heads = HEADS // ZS
    part = heads * head_dim
    length = lengths[0]

    def gather_w(own):
        if count_w == 2:
            return in_order(w_at, own, swap(own, "w"), 0)
        return lax.all_gather(own, "w", axis=0, tiled=True)

    def gather_w_half(own):
        if count_w == 2:
            got = swap(part_of(own, c_at, 2, 0), "w")
            return in_order(w_at, own, in_order(c_at, got, swap(got, "c"), 0), 0)
        return lax.all_gather(own, "w", axis=0, tiled=True)

    def head_slice(weight):
        return lax.dynamic_slice_in_dim(weight, z_at * part, part, 1).astype(BF16)

    low_tokens = tokens.astype(BF16)
    token_all = lax.all_gather(low_tokens, "z", axis=0, tiled=True)
    own_rows = query_weight.shape[0]
    own_kv = jnp.concatenate(
        [
            head_slice(key_weight).reshape(own_rows, heads, 1, head_dim),
            head_slice(value_weight).reshape(own_rows, heads, 1, head_dim),
        ],
        axis=2,
    ).reshape(own_rows, 2 * part)
    attn_full = gather_w(jnp.concatenate([head_slice(query_weight), own_kv], axis=1))
    query_full = attn_full[:, :part]
    kv_full = attn_full[:, part:]
    small = jnp.concatenate(
        [
            item.astype(BF16).reshape(-1, own_rows)
            for item in (
                query_bias,
                value_bias,
                output_bias,
                first_gain,
                first_shift,
                down_bias,
                second_gain,
                second_shift,
                up_bias,
            )
        ],
        axis=0,
    )
    small_all = lax.all_gather(small, "w", axis=0, tiled=False).astype(F32)
    vectors = [small_all[:, at].reshape(width) for at in range(8)]
    query_offset, value_offset, out_offset, first_scale, first_offset = vectors[:5]
    down_offset, second_scale, second_offset = vectors[5:]
    up_offset = small_all[:, 8:].reshape(-1)
    out_full = gather_w_half(output_weight.astype(BF16))
    up_full = gather_w_half(up_weight.astype(BF16))
    down_full = gather_w_half(down_weight.astype(BF16))

    query_own = lax.dynamic_slice_in_dim(query_offset, z_at * part, part, 0)
    value_own = lax.dynamic_slice_in_dim(value_offset, z_at * part, part, 0)
    kv_own = jnp.concatenate(
        [jnp.zeros((heads, 1, head_dim), F32), value_own.reshape(heads, 1, head_dim)],
        axis=1,
    ).reshape(2 * part)
    queries = (
        lax.dot_general(
            query_full, token_all, (((0,), (1,)), ((), ())), preferred_element_type=F32
        )
        + query_own[:, None]
    ).astype(BF16)
    queries = queries * jnp.array(head_dim ** (-0.5), BF16)
    key_values = (matmul(token_all, kv_full) + kv_own).astype(BF16)
    kv_blocks = [key_values]
    kv_blocks = kv_blocks + [swap(item, "x") for item in kv_blocks]
    kv_blocks = kv_blocks + [swap(item, "c") for item in kv_blocks]
    if count_o == 2:
        kv_blocks = kv_blocks + [swap(item, "o") for item in kv_blocks]
    places = []
    for at in range(len(kv_blocks)):
        o_of = o_at ^ (at >> 2)
        places.append(o_of * 16 + (x_at ^ (at & 1)) * 2 + (c_at ^ ((at >> 1) & 1)))
    meta = jnp.stack([length] + places).astype(jnp.int32)
    attended, logs = attend_forward(meta, queries, kv_blocks)
    low_mixed = lax.all_to_all(attended.astype(BF16), "z", 1, 0, tiled=True)

    branch = left_trans(low_mixed, out_full) + out_offset
    normed, first_pull = jax.vjp(layer_norm, tokens + branch, first_scale, first_offset)
    low_normed = normed.astype(BF16)
    pre_act = matmul(low_normed, up_full) + up_offset
    activated, gelu_pull = jax.vjp(partial(jax.nn.gelu, approximate=False), pre_act)
    low_act = activated.astype(BF16)
    ffn_out = matmul(low_act, down_full) + down_offset
    outputs, second_pull = jax.vjp(
        layer_norm, normed + ffn_out, second_scale, second_offset
    )
    my_index = o_at * 16 + z_at * 4 + x_at * 2 + c_at
    positions = my_index * local_rows + jnp.arange(local_rows, dtype=jnp.int32)
    valid = (positions < length).astype(F32)
    seed_grad = cotangent[0] * valid[:, None]
    sum_grad, grad_second_gain, grad_second_shift = second_pull(seed_grad)
    ffn_grad = sum_grad.astype(BF16)
    grad_down_bias = jnp.sum(ffn_grad.astype(F32), axis=0)
    (act_grad,) = gelu_pull(right_trans(ffn_grad, down_full))
    pre_grad = act_grad.astype(BF16)
    grad_up_bias = jnp.sum(pre_grad.astype(F32), axis=0)
    normed_grad = right_trans(pre_grad, up_full) + sum_grad
    resid_grad, grad_first_gain, grad_first_shift = first_pull(normed_grad)
    branch_grad = resid_grad.astype(BF16)
    grad_output_bias = jnp.sum(branch_grad.astype(F32), axis=0)
    mixed_grad = right_trans(out_full, branch_grad).astype(BF16)
    head_grads = lax.all_to_all(mixed_grad, "z", 0, 1, tiled=True)

    def sum_w(slabs):
        if count_w == 2:
            kept = lax.dynamic_index_in_dim(slabs, w_at, 0, keepdims=False)
            sent = lax.dynamic_index_in_dim(slabs, 1 - w_at, 0, keepdims=False)
            return (kept.astype(F32) + swap(sent, "w").astype(F32)).astype(BF16)
        return lax.psum_scatter(slabs, "w", scatter_dimension=0, tiled=True)[0]

    hidden = low_act.shape[1]
    act_cut = low_act.reshape(local_rows, count_w, 2, hidden // count_w // 2)
    act_own = lax.dynamic_index_in_dim(act_cut, c_at, 2, keepdims=False)
    act_sent = lax.dynamic_index_in_dim(act_cut, 1 - c_at, 2, keepdims=False)
    act_rows = jnp.concatenate([act_own, swap(act_sent, "c")], axis=0)
    ffn_rows = jnp.concatenate([ffn_grad, swap(ffn_grad, "c")], axis=0)
    down_slabs = lax.dot_general(
        act_rows, ffn_rows, (((0,), (0,)), ((), ())), preferred_element_type=F32
    ).astype(BF16)
    pre_own = part_of(pre_grad, c_at, 2, 1)
    pre_rows = jnp.concatenate([pre_own, swap(part_of(pre_grad, 1 - c_at, 2, 1), "c")], axis=0)
    normed_rows = jnp.concatenate([low_normed, swap(low_normed, "c")], axis=0)
    up_slabs = left_trans(normed_rows, pre_rows).astype(BF16)
    up_slabs = up_slabs.reshape(count_w, own_rows, hidden // 2)
    branch_rows = jnp.concatenate(
        [part_of(branch_grad, c_at, 2, 1), swap(part_of(branch_grad, 1 - c_at, 2, 1), "c")],
        axis=0,
    )
    mixed_rows = jnp.concatenate([low_mixed, swap(low_mixed, "c")], axis=1)
    out_slabs = matmul(mixed_rows, branch_rows).astype(BF16)
    out_slabs = out_slabs.reshape(count_w, own_rows, width // 2)
    line = ("o", "z", "x")
    down_sum = lax.psum(sum_w(down_slabs), line)
    up_sum = lax.psum(sum_w(up_slabs), line)
    out_sum = lax.psum(sum_w(out_slabs), line)
    total_down = in_order(c_at, down_sum, swap(down_sum, "c"), 0).astype(F32)
    total_up = in_order(c_at, up_sum, swap(up_sum, "c"), 1).astype(F32)
    total_out = in_order(c_at, out_sum, swap(out_sum, "c"), 1).astype(F32)

    query_low, *kv_parts = attend_backward(
        meta, queries, head_grads, attended, logs, kv_blocks
    )

    def add_pair(kept, got):
        return (kept.astype(F32) + got.astype(F32)).astype(BF16)

    if count_o == 2:
        kv_parts = [add_pair(kv_parts[at], swap(kv_parts[at + 4], "o")) for at in range(4)]
    kv_parts = [add_pair(kv_parts[at], swap(kv_parts[at + 2], "c")) for at in range(2)]
    kv_low = add_pair(kv_parts[0], swap(kv_parts[1], "x"))
    token_part = (
        lax.dot_general(
            query_low, query_full, (((0,), (1,)), ((), ())), preferred_element_type=F32
        )
        + right_trans(kv_low, kv_full)
    ).astype(BF16)
    token_grad = lax.psum_scatter(token_part, "z", scatter_dimension=0, tiled=True)
    input_grad = resid_grad + token_grad.astype(F32)
    attn_part = jnp.concatenate(
        [
            lax.dot_general(
                token_all, query_low, (((0,), (1,)), ((), ())), preferred_element_type=F32
            ),
            left_trans(token_all, kv_low),
        ],
        axis=1,
    ).astype(BF16)
    attn_own = sum_w(attn_part.reshape(count_w, own_rows, 3 * part))
    attn_own = lax.psum(attn_own, ("o", "x", "c"))
    attn_all = lax.all_gather(attn_own, "z", axis=0, tiled=False).astype(F32)
    total_query = jnp.transpose(attn_all[:, :, :part], (1, 0, 2)).reshape(own_rows, width)
    pairs = attn_all[:, :, part:].reshape(ZS, own_rows, heads, 2, head_dim)
    pairs = jnp.transpose(pairs, (3, 1, 0, 2, 4)).reshape(2, own_rows, width)
    total_key, total_value = pairs[0], pairs[1]

    query_sum = jnp.sum(query_low.astype(F32), axis=1)
    value_sum = jnp.sum(kv_low.astype(F32), axis=0).reshape(heads, 2, head_dim)[:, 1]
    blank = jnp.zeros((width,), F32)
    grad_query_bias = lax.dynamic_update_slice_in_dim(blank, query_sum, z_at * part, 0)
    grad_value_bias = lax.dynamic_update_slice_in_dim(
        blank, value_sum.reshape(part), z_at * part, 0
    )
    packed = jnp.concatenate(
        [
            item.reshape(-1, 128)
            for item in (
                grad_query_bias,
                grad_value_bias,
                grad_output_bias,
                grad_first_gain,
                grad_first_shift,
                grad_down_bias,
                grad_second_gain,
                grad_second_shift,
                grad_up_bias,
            )
        ],
        axis=0,
    )
    packed = lax.psum(packed, ("o", "z", "x", "c", "w"))
    each = width // 128
    totals = [
        part_of(packed[at * each : (at + 1) * each].reshape(width), w_at, count_w, 0)
        for at in range(8)
    ]
    total_up_bias = part_of(packed[8 * each :].reshape(-1), w_at, count_w, 0)
    return (
        outputs[None],
        input_grad[None],
        total_query,
        totals[0],
        total_key,
        total_value,
        totals[1],
        total_out,
        totals[2],
        totals[3],
        totals[4],
        total_up,
        total_up_bias,
        total_down,
        totals[5],
        totals[6],
        totals[7],
    )


def solution(mesh):
    count_s = mesh.shape["seq"]
    count_w = mesh.shape["wshard"]
    count_o = count_s // 16
    fine = Mesh(
        mesh.devices.reshape(count_o, ZS, 2, 2, count_w), ("o", "z", "x", "c", "w")
    )
    seq = ("o", "z", "x", "c")
    rows = P("w", seq, None)
    matrix = P("w", None)
    vector = P("w")
    placed = (
        rows,
        vector,
        rows,
        matrix,
        vector,
        matrix,
        matrix,
        vector,
        matrix,
        vector,
        vector,
        vector,
        matrix,
        vector,
        matrix,
        vector,
        vector,
        vector,
    )
    return jax.shard_map(
        partial(body, sizes=(count_o, count_w)),
        mesh=fine,
        in_specs=placed,
        out_specs=(
            rows,
            rows,
            matrix,
            vector,
            matrix,
            matrix,
            vector,
            matrix,
            vector,
            vector,
            vector,
            matrix,
            vector,
            matrix,
            vector,
            vector,
            vector,
        ),
        check_vma=False,
    )
```

time: 1160 us -> 599 us (0.52)
  waiting for transfers between devices: 578 us -> 260 us
  matrix products: 236 us -> 48.3 us
  local copies, waits for them, and re-layouts: 131 us -> 56.7 us
  Pallas kernels: 0 us -> 49.1 us
  other arithmetic: 89.9 us -> 45.8 us
  starting transfers between devices: 0.96 us -> 44 us
  blocking collectives: 95.1 us -> 74.7 us
    reduce_scatter x5 -> x1, waiting for transfers between devices: 315 us -> 27.7 us  [body(): lax.psum_scatter(token_part, 'z', scatter_dimension=0, tiled=True)]
    dot_general x62 -> x8, matrix products: 211 us -> 29.9 us  [the longest x4 22.7 us: matmul(): return jnp.dot(left_side, right_side, preferred_element_type=F32)]
    all_gather x8 -> x2, waiting for transfers between devices: 129 us -> 39 us  [the longest x1 39 us: body(): attn_all = lax.all_gather(attn_own, 'z', axis=0, tiled=False).astype(F32)]
    ppermute x0 -> x26, waiting for transfers between devices: none -> 82.1 us  [swap(): return lax.ppermute(value, axis, SWAP)]
    unnamed x20 -> x5, waiting for transfers between devices: 55.2 us -> 0.08 us
    pallas_call x0 -> x2, Pallas kernels: none -> 49.1 us  [the longest x1 28.7 us: attend_backward(): pl.pallas_call(partial(backward_kernel, blocks=blocks, rows=block_rows //...]
    dynamic_update_slice x24 -> x2, local copies, waits for them, and re-layouts: 48.9 us -> 0.43 us  [the longest x1 0.25 us: body(): lax.dynamic_update_slice_in_dim(blank, query_sum, z_at * part, 0)]
    unnamed x170 -> x125, local copies, waits for them, and re-layouts: 46.2 us -> 6.42 us
  transfers between devices with their start and end apart: 17 -> 33, of which waited for: 14 -> 11; matrix products, arithmetic and copies ran while one was open for 20% -> 24% of each run, Pallas kernels for 0% -> 8%
where the time goes in v1:
time: 599 us; the launch traced here: 594 us
  waiting for transfers between devices  260 us (43%)
  blocking collectives  74.7 us (12%)
  local copies, waits for them, and re-layouts  56.7 us (9%)
  Pallas kernels  49.1 us (8%)
  matrix products  48.3 us (8%)
  other arithmetic  45.8 us (8%)
  starting transfers between devices  44 us (7%)
  between operations  15.7 us (3%)
    ppermute x26, waiting for transfers between devices, swap(): return lax.ppermute(value, axis, SWAP)  82.1 us
    psum x1, waiting for transfers between devices, body(): out_sum = lax.psum(sum_w(out_slabs), line)  79.7 us
    psum x1, blocking collectives, body(): packed = lax.psum(packed, ('o', 'z', 'x', 'c', 'w'))  43.7 us
    all_gather x1, waiting for transfers between devices, body(): attn_all = lax.all_gather(attn_own, 'z', axis=0, tiled=False).astype(F32)  39 us
    ppermute x26, starting transfers between devices, swap(): return lax.ppermute(value, axis, SWAP)  35.4 us
    all_gather x1, blocking collectives, body(): small_all = lax.all_gather(small, 'w', axis=0, tiled=False).astype(F32)  31 us
    pallas_call x1, Pallas kernels, attend_backward(): pl.pallas_call(partial(backward_kernel, blocks=blocks, rows=block_rows //...  28.7 us
    psum x1, waiting for transfers between devices, body(): attn_own = lax.psum(attn_own, ('o', 'x', 'c'))  27.9 us
  transfers between devices with their start and end apart: 33, of which 11 were waited for; matrix products, arithmetic and copies ran while one was open for 24% of the time, Pallas kernels for 8%

profile of v1, /device:TPU:1, one launch (start us, length us, event | category | flops | bytes accessed | tf_op | source)
XLA Modules:
  0.0 594.2 jit_solution(97744072320791034)
XLA Ops:
  18.1 31.0 %all-gather.1 = bf16[2,12,384]{2,1,0:T(8,128)(2,1)S(1)} all-gather(bf16[1,12,384]{2,1,0:T(8,128)(2,1)S(1)} %bitcast.148), channel_id=2, replica_groups=mesh['o'=1,'z'=4,'x'=2,'c'=2,'w'=2] {'w'}, dimensions={0}, use_global_device_ids=true | all-gather | bytes 27648 | tf_op jit(solution)/shard_map/all_gather | solution.py:329
  50.7 4.0 convert_element_type.228
  56.2 3.6 fusion.16.refs_0_
  66.8 11.2 %collective-permute-done.1.refs_1_ = bf16[1024,384]{1,0:T(8,128)(2,1)} collective-permute-done((bf16[1024,384]{1,0:T(8,128)(2,1)}, bf16[1024,384]{1,0:T(8,128)(2,1)}, u32[]{:S(2)}, u32[]{:S(2)}) %collective-permute-start.1) | collective-permute-done | bytes 786464 | tf_op jit(solution)/shard_map/ppermute | solution.py:42
  80.1 14.2 %collective-permute-done.4 = bf16[192,768]{1,0:T(8,128)(2,1)S(1)} collective-permute-done((bf16[192,768]{1,0:T(8,128)(2,1)S(1)}, bf16[192,768]{1,0:T(8,128)(2,1)S(1)}, u32[]{:S(2)}, u32[]{:S(2)}) %collective-permute-start.4) | collective-permute-done | bytes 294944 | tf_op jit(solution)/shard_map/ppermute | solution.py:42
  106.3 20.3 %attend_forward.1 = (f32[192,1024]{1,0:T(8,128)}, f32[3,1,1024]{2,1,0:T(1,128)}) custom-call(s32[5]{0:T(128)} %stack.19.meta_ref, bf16[192,1024]{1,0:T(8,128)(2,1)} %fusion.20.q_ref, bf16[1024,384]{1,0:T(8,128)(2,1)} %fusion.16.refs_0_, bf16[1024,384]{1,0:T(8,128)(2,1)} %collective-permute-done.1.refs_1_, bf16[1024,384]{1,0:T(8,128)(2,1)} %collective-permute-done.2.refs_2_, ...), custom_call_target="tpu_custom_call" | custom-call | flops 12884901888 | bytes 3145728 | tf_op jit(solution)/shard_map/attend_forward/pallas_call | solution.py:119
  128.6 4.7 all-to-all-start
  133.4 3.9 maximum_select_fusion.3
  137.3 4.1 maximum_select_fusion.2
  141.4 3.5 all-to-all-done
  149.2 11.5 %multiply_convert_fusion = (bf16[256,3072]{1,0:T(8,128)(2,1)}, f32[256,3072]{1,0:T(8,128)}, f32[256,3072]{1,0:T(8,128)}) fusion(f32[3072]{0:T(1024)S(1)} %copy-done.40, bf16[256,768]{1,0:T(8,128)(2,1)} %fusion.31, bf16[384,3072]{1,0:T(8,128)(2,1)S(1)} %copy-done.17, bf16[384,3072]{1,0:T(8,128)(2,1)S(1)} %copy-done.7, pred[]{:T(512)S(6)} %eq.4), kind=kOutput, calls=%fused_computation.9 | convolution fusion | flops 1281097728 | bytes 12988417 | tf_op jit(solution)/shard_map/dot_general | solution.py:26
  160.7 4.1 reshape.281
  164.8 5.8 fusion.60
  174.1 8.3 %convert_reduce_fusion = (f32[3072]{0:T(1024)}, bf16[256,3072]{1,0:T(8,128)(2,1)S(1)}) fusion(f32[256,3072]{1,0:T(8,128)S(1)} %copy-done.58, f32[256,3072]{1,0:T(8,128)} %get-tuple-element.113, bf16[256,768]{1,0:T(8,128)(2,1)} %get-tuple-element.83, bf16[1536,768]{1,0:T(8,128)(2,1)S(1)} %copy-done.19, bf16[1536,768]{1,0:T(8,128)(2,1)S(1)} %copy-done.10, ...), kind=kOutput, calls=%fused_computation.6 | convolution fusion | flops 1241773056 | bytes 12988417 | tf_op jit(solution)/shard_map/dot_general | solution.py:36
  187.3 3.5 all-to-all-start.1
  194.5 4.9 constant_dynamic-slice_fusion.1
  199.4 13.0 %copy.67 = bf16[256,2,1,768]{0,3,1,2:T(8,128)(2,1)} copy(bf16[256,2,1,768]{3,2,1,0:T(2,128)(2,1)} %get-tuple-element.97) | data formatting | bytes 1572864 | tf_op jit(solution)/shard_map/jit(dynamic_index_in_dim)/dynamic_slice | solution.py:402
  212.4 2.9 copy.66
  217.9 28.7 %attend_backward.1 = (bf16[192,1024]{1,0:T(8,128)(2,1)}, bf16[1024,384]{1,0:T(8,128)(2,1)}, bf16[1024,384]{1,0:T(8,128)(2,1)}, bf16[1024,384]{1,0:T(8,128)(2,1)}, bf16[1024,384]{1,0:T(8,128)(2,1)}) custom-call(s32[5]{0:T(128)} %stack.19.meta_ref, bf16[192,1024]{1,0:T(8,128)(2,1)} %fusion.20.q_ref, bf16[192,1024]{1,0:T(8,128)(2,1)} %bitcast.147, ...), custom_call_target="tpu_custom_call" | custom-call | flops 32212254720 | bytes 6291456 | tf_op jit(solution)/shard_map/attend_backward/pallas_call | solution.py:211
  246.8 13.9 %collective-permute-start.16 = (bf16[384,384]{1,0:T(8,128)(2,1)S(1)}, bf16[384,384]{1,0:T(8,128)(2,1)S(1)}, u32[]{:S(2)}, u32[]{:S(2)}) collective-permute-start(bf16[384,384]{1,0:T(8,128)(2,1)S(1)} %dynamic-slice_bitcast_fusion.3), channel_id=1, source_target_pairs={{0,1},{1,0},{2,3},{3,2},{4,5},{5,4},{6,7},{7,6},{8,9},{9,8},{10,11... | collective-permute-start | bytes 884744 | tf_op jit(solution)/shard_map/ppermute | solution.py:42
  262.2 5.4 collective-permute-done.16
  279.1 9.3 %collective-permute-done.12 = bf16[1024,384]{1,0:T(8,128)(2,1)S(1)} collective-permute-done((bf16[1024,384]{1,0:T(8,128)(2,1)S(1)}, bf16[1024,384]{1,0:T(8,128)(2,1)S(1)}, u32[]{:S(2)}, u32[]{:S(2)}) %collective-permute-start.12) | collective-permute-done | bytes 786464 | tf_op jit(solution)/shard_map/ppermute | solution.py:42
  291.3 8.4 %collective-permute-done.20 = bf16[384,1536]{1,0:T(8,128)(2,1)S(1)} collective-permute-done((bf16[384,1536]{1,0:T(8,128)(2,1)S(1)}, bf16[384,1536]{1,0:T(8,128)(2,1)S(1)}, u32[]{:S(2)}, u32[]{:S(2)}) %collective-permute-start.20) | collective-permute-done | bytes 1179680 | tf_op jit(solution)/shard_map/ppermute | solution.py:42
  301.0 33.5 %collective-permute-done.13 = bf16[384,576]{0,1:T(8,128)(2,1)S(1)} collective-permute-done((bf16[384,576]{0,1:T(8,128)(2,1)S(1)}, bf16[384,576]{0,1:T(8,128)(2,1)S(1)}, u32[]{:S(2)}, u32[]{:S(2)}) %collective-permute-start.13) | collective-permute-done | bytes 442400 | tf_op jit(solution)/shard_map/ppermute | solution.py:42
  335.7 2.9 fusion.8
  341.5 27.9 %all-reduce.5.cloned.1.call-done = bf16[1,384,576]{1,2,0:T(8,128)(2,1)} async-done(((bf16[1,384,576]{1,2,0:T(8,128)(2,1)}), bf16[1,384,576]{1,2,0:T(8,128)(2,1)}) %all-reduce.5.cloned.1.call-update) | async-done | bytes 442384 | tf_op jit(solution)/shard_map/psum | solution.py:457
  370.6 43.7 %psum.36 = f32[72,128]{1,0:T(8,128)S(1)} all-reduce(f32[72,128]{1,0:T(8,128)S(1)} %concatenate.123), channel_id=1, replica_groups=mesh['o'=1,'z'=4,'x'=2,'c'=2,'w'=2] {'o','z','x','c','w'}, use_global_device_ids=true, to_apply=%region_19.20 | all-reduce | flops 9216 | bytes 73728 | tf_op jit(solution)/shard_map/psum | solution.py:488
  414.3 79.7 %all-reduce.7.cloned.1.call-done = (bf16[384,384]{1,0:T(8,128)(2,1)}, bf16[384,1536]{1,0:T(8,128)(2,1)}, bf16[768,768]{1,0:T(8,128)(2,1)}) async-done(((bf16[384,384]{1,0:T(8,128)(2,1)}, bf16[384,1536]{1,0:T(8,128)(2,1)}, bf16[768,768]{1,0:T(8,128)(2,1)}), (bf16[384,384]{1,0:T(8,128)(2,1)}, bf16[384,1536]{1,0:T(8,128)(2,1)}, bf16[768,768]{1,0:T(8,128)(2,1)})) %all-reduce.7.cloned.1.call-update) | async-done | bytes 2654224 | tf_op jit(solution)/shard_map/psum | solution.py:423
  503.4 27.7 %reduce-scatter.2.cloned.1.call-done = bf16[256,768]{1,0:T(8,128)(2,1)} async-done(((bf16[1024,768]{1,0:T(8,128)(2,1)}), bf16[256,768]{1,0:T(8,128)(2,1)}) %reduce-scatter.2.cloned.1.call-update) | async-done | bytes 393232 | tf_op jit(solution)/shard_map/reduce_scatter | solution.py:445
  533.1 39.0 %all-gather.7.cloned.1.call-done = bf16[4,384,576]{1,2,0:T(8,128)(2,1)} async-done(((bf16[1,384,576]{1,2,0:T(8,128)(2,1)}), bf16[4,384,576]{1,2,0:T(8,128)(2,1)}) %all-gather.7.cloned.1.call-update) | async-done | bytes 1769488 | tf_op jit(solution)/shard_map/all_gather | solution.py:458
  578.2 4.7 fusion.6
  582.8 4.6 fusion.7
  (301 shorter events, 94.5 us)
Async XLA Ops:
  7.2 49.0 %all-gather.5.cloned.1.call-start = ((), (), s32[]{:S(2)}) async-start(), calls=%async_computation.3 | async-start | bytes 1966080 | tf_op jit(solution)/shard_map/all_gather | solution.py:300
  11.5 43.2 %collective-permute-start = (bf16[384,576]{0,1:T(8,128)(2,1)S(1)}, bf16[384,576]{0,1:T(8,128)(2,1)}, u32[]{:S(2)}, u32[]{:S(2)}) collective-permute-start(bf16[384,576]{0,1:T(8,128)(2,1)S(1)} %pad_maximum_fusion), channel_id=1, source_target_pairs={{0,1},{1,0},{2,3},{3,2},{4,5},{5,4},{6,7},{7,6},{8,9},{9,8},{10,11... | collective-permute-start | bytes 1327112 | tf_op jit(solution)/shard_map/ppermute | solution.py:42
  17.5 86.8 %collective-permute-start.6 = (bf16[192,3072]{1,0:T(8,128)(2,1)}, bf16[192,3072]{1,0:T(8,128)(2,1)}, u32[]{:S(2)}, u32[]{:S(2)}) collective-permute-start(bf16[192,3072]{1,0:T(8,128)(2,1)} %constant_dynamic-slice_fusion.7), channel_id=1, source_target_pairs={{0,1},{1,0},{2,3},{3,2},{4,5},{5,4},{6,7},{7,6},{8,9},{9,8},{10,11... | collective-permute-start | bytes 3538952 | tf_op jit(solution)/shard_map/ppermute | solution.py:42
  59.8 18.2 %collective-permute-start.1 = (bf16[1024,384]{1,0:T(8,128)(2,1)}, bf16[1024,384]{1,0:T(8,128)(2,1)}, u32[]{:S(2)}, u32[]{:S(2)}) collective-permute-start(bf16[1024,384]{1,0:T(8,128)(2,1)} %fusion.16.refs_0_), channel_id=1, source_target_pairs={{0,4},{4,0},{1,5},{5,1},{2,6},{6,2},{3,7},{7,3},{8,12},{12,8},{9,1... | collective-permute-start | bytes 2359304 | tf_op jit(solution)/shard_map/ppermute | solution.py:42
  62.0 42.3 %collective-permute-start.8 = (bf16[768,768]{1,0:T(8,128)(2,1)}, bf16[768,768]{1,0:T(8,128)(2,1)}, u32[]{:S(2)}, u32[]{:S(2)}) collective-permute-start(bf16[768,768]{1,0:T(8,128)(2,1)} %constant_dynamic-slice_fusion.6), channel_id=1, source_target_pairs={{0,1},{1,0},{2,3},{3,2},{4,5},{5,4},{6,7},{7,6},{8,9},{9,8},{10,11... | collective-permute-start | bytes 3538952 | tf_op jit(solution)/shard_map/ppermute | solution.py:42
  64.2 30.1 %collective-permute-start.4 = (bf16[192,768]{1,0:T(8,128)(2,1)S(1)}, bf16[192,768]{1,0:T(8,128)(2,1)S(1)}, u32[]{:S(2)}, u32[]{:S(2)}) collective-permute-start(bf16[192,768]{1,0:T(8,128)(2,1)S(1)} %constant_dynamic-slice_fusion.8), channel_id=1, source_target_pairs={{0,1},{1,0},{2,3},{3,2},{4,5},{5,4},{6,7},{7,6},{8,9},{9,8},{10,11... | collective-permute-start | bytes 884744 | tf_op jit(solution)/shard_map/ppermute | solution.py:42
  64.5 41.8 %collective-permute-start.2 = (bf16[1024,384]{1,0:T(8,128)(2,1)}, bf16[1024,384]{1,0:T(8,128)(2,1)}, u32[]{:S(2)}, u32[]{:S(2)}) collective-permute-start(bf16[1024,384]{1,0:T(8,128)(2,1)} %fusion.16.refs_0_), channel_id=1, source_target_pairs={{0,2},{2,0},{1,3},{3,1},{4,6},{6,4},{5,7},{7,5},{8,10},{10,8},{9,1... | collective-permute-start | bytes 2359304 | tf_op jit(solution)/shard_map/ppermute | solution.py:42
  78.0 28.2 %collective-permute-start.3 = (bf16[1024,384]{1,0:T(8,128)(2,1)}, bf16[1024,384]{1,0:T(8,128)(2,1)}, u32[]{:S(2)}, u32[]{:S(2)}) collective-permute-start(bf16[1024,384]{1,0:T(8,128)(2,1)} %collective-permute-done.1.refs_1_), channel_id=1, source_target_pairs={{0,2},{2,0},{1,3},{3,1},{4,6},{6,4},{5,7},{7,5},{8,10},{10,8},{9,1... | collective-permute-start | bytes 2359304 | tf_op jit(solution)/shard_map/ppermute | solution.py:42
  94.3 9.1 %collective-permute-start.5 = (bf16[192,768]{1,0:T(8,128)(2,1)S(1)}, bf16[192,768]{1,0:T(8,128)(2,1)S(1)}, u32[]{:S(2)}, u32[]{:S(2)}) collective-permute-start(bf16[192,768]{1,0:T(8,128)(2,1)S(1)} %collective-permute-done.4), channel_id=1, source_target_pairs={{0,2},{2,0},{1,3},{3,1},{4,6},{6,4},{5,7},{7,5},{8,10},{10,8},{9,1... | collective-permute-start | bytes 884744 | tf_op jit(solution)/shard_map/ppermute | solution.py:42
  104.4 32.9 %collective-permute-start.7 = (bf16[192,3072]{1,0:T(8,128)(2,1)}, bf16[192,3072]{1,0:T(8,128)(2,1)}, u32[]{:S(2)}, u32[]{:S(2)}) collective-permute-start(bf16[192,3072]{1,0:T(8,128)(2,1)} %collective-permute-done.6), channel_id=1, source_target_pairs={{0,2},{2,0},{1,3},{3,1},{4,6},{6,4},{5,7},{7,5},{8,10},{10,8},{9,1... | collective-permute-start | bytes 3538952 | tf_op jit(solution)/shard_map/ppermute | solution.py:42
  104.4 28.9 %collective-permute-start.9 = (bf16[768,768]{1,0:T(8,128)(2,1)}, bf16[768,768]{1,0:T(8,128)(2,1)}, u32[]{:S(2)}, u32[]{:S(2)}) collective-permute-start(bf16[768,768]{1,0:T(8,128)(2,1)} %collective-permute-done.8), channel_id=1, source_target_pairs={{0,2},{2,0},{1,3},{3,1},{4,6},{6,4},{5,7},{7,5},{8,10},{10,8},{9,1... | collective-permute-start | bytes 3538952 | tf_op jit(solution)/shard_map/ppermute | solution.py:42
  128.6 16.3 %all-to-all-start = ((bf16[192,4,256]{2,0,1:T(8,128)(2,1)}), bf16[192,4,256]{2,0,1:T(8,128)(2,1)}, u32[]{:S(2)}, u32[]{:S(2)}) async-start(bf16[192,4,256]{2,0,1:T(8,128)(2,1)} %bitcast.126), calls=%async_computation | async-start | bytes 786432 | tf_op jit(solution)/shard_map/all_to_all | solution.py:363
  144.9 70.4 %collective-permute-start.14 = (bf16[768,256]{1,0:T(8,128)(2,1)}, bf16[768,256]{1,0:T(8,128)(2,1)}, u32[]{:S(2)}, u32[]{:S(2)}) collective-permute-start(bf16[768,256]{1,0:T(8,128)(2,1)} %bitcast.11), channel_id=1, source_target_pairs={{0,2},{2,0},{1,3},{3,1},{4,6},{6,4},{5,7},{7,5},{8,10},{10,8},{9,1... | collective-permute-start | bytes 1179656 | tf_op jit(solution)/shard_map/ppermute | solution.py:42
  149.1 120.6 %collective-permute-start.18 = (bf16[256,768]{1,0:T(8,128)(2,1)}, bf16[256,768]{1,0:T(8,128)(2,1)}, u32[]{:S(2)}, u32[]{:S(2)}) collective-permute-start(bf16[256,768]{1,0:T(8,128)(2,1)} %fusion.31), channel_id=1, source_target_pairs={{0,2},{2,0},{1,3},{3,1},{4,6},{6,4},{5,7},{7,5},{8,10},{10,8},{9,1... | collective-permute-start | bytes 1179656 | tf_op jit(solution)/shard_map/ppermute | solution.py:42
  173.6 100.9 %collective-permute-start.23 = (bf16[256,768]{1,0:T(8,128)(2,1)}, bf16[256,768]{1,0:T(8,128)(2,1)}, u32[]{:S(2)}, u32[]{:S(2)}) collective-permute-start(bf16[256,768]{1,0:T(8,128)(2,1)} %get-tuple-element.83), channel_id=1, source_target_pairs={{0,2},{2,0},{1,3},{3,1},{4,6},{6,4},{5,7},{7,5},{8,10},{10,8},{9,1... | collective-permute-start | bytes 1179656 | tf_op jit(solution)/shard_map/ppermute | solution.py:42
  187.3 29.8 %all-to-all-start.1 = ((bf16[4,192,256]{2,1,0:T(8,128)(2,1)}), bf16[4,192,256]{2,1,0:T(8,128)(2,1)S(1)}, u32[]{:S(2)}, u32[]{:S(2)}) async-start(bf16[4,192,256]{2,1,0:T(8,128)(2,1)} %bitcast.15), calls=%async_computation.1 | async-start | bytes 786432 | tf_op jit(solution)/shard_map/all_to_all | solution.py:390
  190.8 178.7 %all-reduce.5.cloned.1.call-start = ((), (), s32[]{:S(2)}) async-start(), calls=%async_computation.5 | async-start | bytes 884736 | tf_op jit(solution)/shard_map/psum | solution.py:457
  191.6 23.7 %collective-permute-start.15 = (bf16[256,384]{1,0:T(8,128)(2,1)}, bf16[256,384]{1,0:T(8,128)(2,1)}, u32[]{:S(2)}, u32[]{:S(2)}) collective-permute-start(bf16[256,384]{1,0:T(8,128)(2,1)} %get-tuple-element.102), channel_id=1, source_target_pairs={{0,2},{2,0},{1,3},{3,1},{4,6},{6,4},{5,7},{7,5},{8,10},{10,8},{9,1... | collective-permute-start | bytes 589832 | tf_op jit(solution)/shard_map/ppermute | solution.py:42
  194.1 76.0 %collective-permute-start.19 = (bf16[256,1536]{1,0:T(8,128)(2,1)}, bf16[256,1536]{1,0:T(8,128)(2,1)}, u32[]{:S(2)}, u32[]{:S(2)}) collective-permute-start(bf16[256,1536]{1,0:T(8,128)(2,1)} %get-tuple-element.99), channel_id=1, source_target_pairs={{0,2},{2,0},{1,3},{3,1},{4,6},{6,4},{5,7},{7,5},{8,10},{10,8},{9,1... | collective-permute-start | bytes 2359304 | tf_op jit(solution)/shard_map/ppermute | solution.py:42
  246.7 22.8 %collective-permute-start.11 = (bf16[1024,384]{1,0:T(8,128)(2,1)}, bf16[1024,384]{1,0:T(8,128)(2,1)S(1)}, u32[]{:S(2)}, u32[]{:S(2)}) collective-permute-start(bf16[1024,384]{1,0:T(8,128)(2,1)} %get-tuple-element.30), channel_id=1, source_target_pairs={{0,2},{2,0},{1,3},{3,1},{4,6},{6,4},{5,7},{7,5},{8,10},{10,8},{9,1... | collective-permute-start | bytes 2359304 | tf_op jit(solution)/shard_map/ppermute | solution.py:42
  246.8 20.8 %collective-permute-start.16 = (bf16[384,384]{1,0:T(8,128)(2,1)S(1)}, bf16[384,384]{1,0:T(8,128)(2,1)S(1)}, u32[]{:S(2)}, u32[]{:S(2)}) collective-permute-start(bf16[384,384]{1,0:T(8,128)(2,1)S(1)} %dynamic-slice_bitcast_fusion.3), channel_id=1, source_target_pairs={{0,1},{1,0},{2,3},{3,2},{4,5},{5,4},{6,7},{7,6},{8,9},{9,8},{10,11... | collective-permute-start | bytes 884744 | tf_op jit(solution)/shard_map/ppermute | solution.py:42
  269.5 9.6 %collective-permute-start.10 = (bf16[1024,384]{1,0:T(8,128)(2,1)S(1)}, bf16[1024,384]{1,0:T(8,128)(2,1)S(1)}, u32[]{:S(2)}, u32[]{:S(2)}) collective-permute-start(bf16[1024,384]{1,0:T(8,128)(2,1)S(1)} %copy-done.57), channel_id=1, source_target_pairs={{0,2},{2,0},{1,3},{3,1},{4,6},{6,4},{5,7},{7,5},{8,10},{10,8},{9,1... | collective-permute-start | bytes 2359304 | tf_op jit(solution)/shard_map/ppermute | solution.py:42
  269.7 18.7 %collective-permute-start.12 = (bf16[1024,384]{1,0:T(8,128)(2,1)S(1)}, bf16[1024,384]{1,0:T(8,128)(2,1)S(1)}, u32[]{:S(2)}, u32[]{:S(2)}) collective-permute-start(bf16[1024,384]{1,0:T(8,128)(2,1)S(1)} %add_convert_fusion.3), channel_id=1, source_target_pairs={{0,4},{4,0},{1,5},{5,1},{2,6},{6,2},{3,7},{7,3},{8,12},{12,8},{9,1... | collective-permute-start | bytes 2359304 | tf_op jit(solution)/shard_map/ppermute | solution.py:42
  272.9 26.8 %collective-permute-start.20 = (bf16[384,1536]{1,0:T(8,128)(2,1)S(1)}, bf16[384,1536]{1,0:T(8,128)(2,1)S(1)}, u32[]{:S(2)}, u32[]{:S(2)}) collective-permute-start(bf16[384,1536]{1,0:T(8,128)(2,1)S(1)} %dynamic-slice_bitcast_fusion.1), channel_id=1, source_target_pairs={{0,1},{1,0},{2,3},{3,2},{4,5},{5,4},{6,7},{7,6},{8,9},{9,8},{10,11... | collective-permute-start | bytes 3538952 | tf_op jit(solution)/shard_map/ppermute | solution.py:42
  278.1 57.6 %collective-permute-start.24 = (bf16[768,768]{1,0:T(8,128)(2,1)}, bf16[768,768]{1,0:T(8,128)(2,1)}, u32[]{:S(2)}, u32[]{:S(2)}) collective-permute-start(bf16[768,768]{1,0:T(8,128)(2,1)} %dynamic-slice_bitcast_fusion), channel_id=1, source_target_pairs={{0,1},{1,0},{2,3},{3,2},{4,5},{5,4},{6,7},{7,6},{8,9},{9,8},{10,11... | collective-permute-start | bytes 3538952 | tf_op jit(solution)/shard_map/ppermute | solution.py:42
  289.8 44.7 %collective-permute-start.13 = (bf16[384,576]{0,1:T(8,128)(2,1)S(1)}, bf16[384,576]{0,1:T(8,128)(2,1)S(1)}, u32[]{:S(2)}, u32[]{:S(2)}) collective-permute-start(bf16[384,576]{0,1:T(8,128)(2,1)S(1)} %dynamic-slice_bitcast_fusion.2), channel_id=1, source_target_pairs={{0,1},{1,0},{2,3},{3,2},{4,5},{5,4},{6,7},{7,6},{8,9},{9,8},{10,11... | collective-permute-start | bytes 1327112 | tf_op jit(solution)/shard_map/ppermute | solution.py:42
  335.4 158.6 %all-reduce.7.cloned.1.call-start = ((), (), s32[]{:S(2)}) async-start(), calls=%async_computation.7 | async-start | bytes 5308416 | tf_op jit(solution)/shard_map/psum | solution.py:423
  338.6 192.5 %reduce-scatter.2.cloned.1.call-start = ((), (), s32[]{:S(2)}) async-start(), calls=%async_computation.4 | async-start | bytes 1966080 | tf_op jit(solution)/shard_map/reduce_scatter | solution.py:445
  341.5 230.6 %all-gather.7.cloned.1.call-start = ((), (), s32[]{:S(2)}) async-start(), calls=%async_computation.6 | async-start | bytes 2211840 | tf_op jit(solution)/shard_map/all_gather | solution.py:458
  494.0 7.2 %collective-permute-start.17 = (bf16[384,384]{1,0:T(8,128)(2,1)}, bf16[384,384]{1,0:T(8,128)(2,1)S(1)}, u32[]{:S(2)}, u32[]{:S(2)}) collective-permute-start(bf16[384,384]{1,0:T(8,128)(2,1)} %get-tuple-element.79), channel_id=1, source_target_pairs={{0,2},{2,0},{1,3},{3,1},{4,6},{6,4},{5,7},{7,5},{8,10},{10,8},{9,1... | collective-permute-start | bytes 884744 | tf_op jit(solution)/shard_map/ppermute | solution.py:42
  494.8 83.4 %collective-permute-start.21 = (bf16[384,1536]{1,0:T(8,128)(2,1)}, bf16[384,1536]{1,0:T(8,128)(2,1)}, u32[]{:S(2)}, u32[]{:S(2)}) collective-permute-start(bf16[384,1536]{1,0:T(8,128)(2,1)} %get-tuple-element.80), channel_id=1, source_target_pairs={{0,2},{2,0},{1,3},{3,1},{4,6},{6,4},{5,7},{7,5},{8,10},{10,8},{9,1... | collective-permute-start | bytes 3538952 | tf_op jit(solution)/shard_map/ppermute | solution.py:42
  500.7 82.1 %collective-permute-start.25 = (bf16[768,768]{1,0:T(8,128)(2,1)}, bf16[768,768]{1,0:T(8,128)(2,1)}, u32[]{:S(2)}, u32[]{:S(2)}) collective-permute-start(bf16[768,768]{1,0:T(8,128)(2,1)} %get-tuple-element.81), channel_id=1, source_target_pairs={{0,2},{2,0},{1,3},{3,1},{4,6},{6,4},{5,7},{7,5},{8,10},{10,8},{9,1... | collective-permute-start | bytes 3538952 | tf_op jit(solution)/shard_map/ppermute | solution.py:42
  (60 other events, 768.8 us)
Sparse Core Ops, SparseCore 0:
  10.2 39.0 all-gather.4
  335.5 33.8 all-reduce.4
  374.5 119.4 all-reduce.6
  496.9 34.2 reduce-scatter.1
  532.6 39.4 all-gather.6

commit v2 on v1

--- a/solution.py
+++ b/solution.py
@@ -15,21 +15,8 @@
 BF16 = jnp.bfloat16
 
 
-def layer_norm(features, norm_gain, norm_shift):
-    average = jnp.mean(features, axis=-1, keepdims=True)
-    centered = features - average
-    variance = jnp.mean(centered * centered, axis=-1, keepdims=True)
-    return centered * lax.rsqrt(variance + 1e-12) * norm_gain + norm_shift
-
-
 def matmul(left_side, right_side):
     return jnp.dot(left_side, right_side, preferred_element_type=F32)
-
-
-def left_trans(left_side, right_side):
-    return lax.dot_general(
-        left_side, right_side, (((0,), (0,)), ((), ())), preferred_element_type=F32
-    )
 
 
 def right_trans(left_side, right_side):
@@ -232,6 +219,433 @@
         ),
         name="attend_backward",
     )(meta, queries, grads, outs, logs, *kv_blocks)
+
+
+def project_kernel(tokens_ref, weight_ref, bias_ref, query_ref, kv_ref, turned_ref):
+    part = query_ref.shape[0]
+    tokens = tokens_ref[...]
+    kv = matmul(tokens, weight_ref[:, : 2 * part]) + bias_ref[:, : 2 * part]
+    kv_ref[...] = kv.astype(BF16)
+    query = matmul(tokens, weight_ref[:, 2 * part :]) + bias_ref[:, 2 * part :]
+    query = query.astype(BF16) * jnp.array((part // 3) ** (-0.5), BF16)
+    query_ref[...] = query.T
+    turned_ref[...] = tokens.T
+
+
+def project(tokens, weight, bias):
+    rows, width = tokens.shape
+    part = weight.shape[1] // 3
+    return pl.pallas_call(
+        project_kernel,
+        out_shape=[
+            jax.ShapeDtypeStruct((part, rows), BF16),
+            jax.ShapeDtypeStruct((rows, 2 * part), BF16),
+            jax.ShapeDtypeStruct((width, rows), BF16),
+        ],
+        compiler_params=pltpu.CompilerParams(vmem_limit_bytes=40 << 20),
+        name="project",
+    )(tokens, weight, bias)
+
+
+def middle_kernel(meta_ref, mixed_ref, tokens_ref, seed_ref, vec_ref, upoff_ref, *refs, counts, chunk):
+    pieces = refs[: sum(counts)]
+    (
+        outputs_ref,
+        resid_ref,
+        mgrad_ref,
+        act_ref,
+        pre_ref,
+        ffn_ref,
+        normed_ref,
+        branch_ref,
+        small_ref,
+        upsum_ref,
+        out_w,
+        up_w,
+        down_w,
+        slope_ref,
+        sems,
+    ) = refs[sum(counts) :]
+    groups = []
+    at = 0
+    for count, target in zip(counts, (out_w, up_w, down_w)):
+        group = []
+        for piece in range(count):
+            source = pieces[at]
+            unit = source.shape[0] if piece else source.shape[0] // 2
+            if count == 1:
+                place = target
+            else:
+                start = pl.multiple_of(meta_ref[1 + piece] * unit, unit)
+                place = target.at[pl.ds(start, source.shape[0]), :]
+            copy = pltpu.make_async_copy(source, place, sems.at[at])
+            copy.start()
+            group.append(copy)
+            at += 1
+        groups.append(group)
+    rows, width = tokens_ref.shape
+    hidden = upoff_ref.shape[1]
+
+    def mean(value):
+        return jnp.mean(value, axis=-1, keepdims=True)
+
+    def norm(value):
+        centered = value - mean(value)
+        scale = lax.rsqrt(mean(centered * centered) + 1e-12)
+        return centered * scale, scale
+
+    def norm_back(grad, normal, scale):
+        return scale * (grad - mean(grad) - normal * mean(grad * normal))
+
+    def column(value):
+        return jnp.sum(value, axis=0, keepdims=True)
+
+    mixed = mixed_ref[...].T
+    for copy in groups[0]:
+        copy.wait()
+    first_n, first_r = norm(tokens_ref[...] + (matmul(mixed, out_w[...]) + vec_ref[2:3, :]))
+    normed = first_n * vec_ref[3:4, :] + vec_ref[4:5, :]
+    low = normed.astype(BF16)
+    normed_ref[...] = low.T
+    for copy in groups[1] + groups[2]:
+        copy.wait()
+    acc = None
+    for at in range(0, hidden, chunk):
+        cut = slice(at, at + chunk)
+        pre_act = matmul(low, up_w[:, cut]) + upoff_ref[:, cut]
+        phi = 0.5 + 0.5 * lax.erf(pre_act * (0.5**0.5))
+        act = (pre_act * phi).astype(BF16)
+        slope_ref[:, cut] = phi + pre_act * (
+            jnp.exp(-0.5 * pre_act * pre_act) * 0.3989422804014327
+        )
+        act_ref[cut, :] = act.T
+        term = matmul(act, down_w[cut, :])
+        acc = term if acc is None else acc + term
+    second_n, second_r = norm(normed + (acc + vec_ref[5:6, :]))
+    outputs_ref[...] = second_n * vec_ref[6:7, :] + vec_ref[7:8, :]
+    place = lax.broadcasted_iota(jnp.int32, (rows, 1), 0)
+    seed = jnp.where(place < meta_ref[0], seed_ref[...], 0.0)
+    sum_grad = norm_back(seed * vec_ref[6:7, :], second_n, second_r)
+    ffn = sum_grad.astype(BF16)
+    ffn_ref[...] = ffn
+    small_ref[3:4, :] = column(ffn.astype(F32))
+    small_ref[4:5, :] = column(seed * second_n)
+    small_ref[5:6, :] = column(seed)
+    acc = sum_grad
+    for at in range(0, hidden, chunk):
+        cut = slice(at, at + chunk)
+        pre = (right_trans(ffn, down_w[cut, :]) * slope_ref[:, cut]).astype(BF16)
+        pre_ref[:, cut] = pre
+        upsum_ref[:, cut] = column(pre.astype(F32))
+        acc = acc + right_trans(pre, up_w[:, cut])
+    small_ref[1:2, :] = column(acc * first_n)
+    small_ref[2:3, :] = column(acc)
+    resid = norm_back(acc * vec_ref[3:4, :], first_n, first_r)
+    resid_ref[...] = resid
+    branch = resid.astype(BF16)
+    branch_ref[...] = branch
+    small_ref[0:1, :] = column(branch.astype(F32))
+    small_ref[6:8, :] = jnp.zeros((2, width), F32)
+    mgrad_ref[...] = right_trans(out_w[...], branch).astype(BF16)
+
+
+def middle(meta, mixed, tokens, seed, vec, upoff, pieces, *, chunk=1024):
+    rows, width = tokens.shape
+    hidden = upoff.shape[1]
+    in_vmem = pl.BlockSpec(memory_space=pltpu.VMEM)
+    in_place = pl.BlockSpec(memory_space=pl.ANY)
+    flat = [item for group in pieces for item in group]
+    return pl.pallas_call(
+        partial(middle_kernel, counts=tuple(len(group) for group in pieces), chunk=chunk),
+        grid_spec=pltpu.PrefetchScalarGridSpec(
+            num_scalar_prefetch=1,
+            grid=(),
+            in_specs=[in_vmem] * 5 + [in_place] * len(flat),
+            out_specs=[in_vmem] * 10,
+            scratch_shapes=[
+                pltpu.VMEM((width, width), BF16),
+                pltpu.VMEM((width, hidden), BF16),
+                pltpu.VMEM((hidden, width), BF16),
+                pltpu.VMEM((rows, hidden), F32),
+                pltpu.SemaphoreType.DMA((len(flat),)),
+            ],
+        ),
+        out_shape=[
+            jax.ShapeDtypeStruct((rows, width), F32),
+            jax.ShapeDtypeStruct((rows, width), F32),
+            jax.ShapeDtypeStruct((width, rows), BF16),
+            jax.ShapeDtypeStruct((hidden, rows), BF16),
+            jax.ShapeDtypeStruct((rows, hidden), BF16),
+            jax.ShapeDtypeStruct((rows, width), BF16),
+            jax.ShapeDtypeStruct((width, rows), BF16),
+            jax.ShapeDtypeStruct((rows, width), BF16),
+            jax.ShapeDtypeStruct((8, width), F32),
+            jax.ShapeDtypeStruct((1, hidden), F32),
+        ],
+        compiler_params=pltpu.CompilerParams(vmem_limit_bytes=56 << 20),
+        name="middle",
+    )(meta, mixed, tokens, seed, vec, upoff, *flat)
+
+
+def down_kernel(meta_ref, act_ref, ffn_ref, *refs):
+    value = matmul(act_ref[...], ffn_ref[...])
+    if len(refs) == 2:
+        value = value + refs[0][...].astype(F32)
+    refs[-1][...] = value.astype(BF16)
+
+
+def down_slab(meta, act, ffn, count, got=None):
+    rows, width = ffn.shape
+    block = act.shape[0] // count
+    whole = pl.BlockSpec((block, width), lambda i, m: (0, 0))
+    return pl.pallas_call(
+        down_kernel,
+        grid_spec=pltpu.PrefetchScalarGridSpec(
+            num_scalar_prefetch=1,
+            grid=(1,),
+            in_specs=[
+                pl.BlockSpec((block, rows), lambda i, m: (m[0] * 2 + m[1], 0)),
+                pl.BlockSpec((rows, width), lambda i, m: (0, 0)),
+            ]
+            + ([] if got is None else [whole]),
+            out_specs=whole,
+        ),
+        out_shape=jax.ShapeDtypeStruct((block, width), BF16),
+        compiler_params=pltpu.CompilerParams(vmem_limit_bytes=24 << 20),
+        name="down_slab",
+    )(meta, act, ffn, *(() if got is None else (got,)))
+
+
+def up_kernel(meta_ref, normed_ref, pre_ref, mixed_ref, branch_ref, *refs, small):
+    out_ref = refs[-1]
+    first = pre_ref.shape[1]
+    second = first + branch_ref.shape[1]
+    got = None
+    if small:
+        small_ref, upsum_ref = refs[:2]
+        refs = refs[2:]
+    if len(refs) == 2:
+        got = refs[0]
+
+    def put(value, rows, columns):
+        if got is not None:
+            value = value + got[rows, columns].astype(F32)
+        out_ref[rows, columns] = value.astype(BF16)
+
+    every = slice(0, out_ref.shape[0])
+    put(matmul(normed_ref[...], pre_ref[...]), every, slice(0, first))
+    put(matmul(mixed_ref[...], branch_ref[...]), every, slice(first, second))
+    if small:
+        lanes = slice(second, second + 128)
+        groups = small_ref.shape[1] // 128
+        lines = upsum_ref.shape[1] // 128
+        values = [small_ref[:, at * 128 : (at + 1) * 128] for at in range(groups)]
+        values += [upsum_ref[:, at * 128 : (at + 1) * 128] for at in range(lines)]
+        used = 8 * groups + lines
+        total = out_ref.shape[0]
+        values += [jnp.zeros((total - used, 128), F32)]
+        put(jnp.concatenate(values, axis=0), every, lanes)
+
+
+def up_slab(meta, normed, pre, mixed, branch, small, count_w, got=None):
+    width, rows = normed.shape
+    hidden = pre.shape[1]
+    block = width // count_w
+    columns = hidden // 2 + width // 2 + (128 if small else 0)
+    whole = pl.BlockSpec((block, columns), lambda i, m: (0, 0))
+    specs = [
+        pl.BlockSpec((block, rows), lambda i, m: (m[0], 0)),
+        pl.BlockSpec((rows, hidden // 2), lambda i, m: (0, m[1])),
+        pl.BlockSpec((block, rows), lambda i, m: (m[0], 0)),
+        pl.BlockSpec((rows, width // 2), lambda i, m: (0, m[1])),
+    ]
+    extra = []
+    if small:
+        specs += [
+            pl.BlockSpec((8, width // count_w), lambda i, m: (0, m[0])),
+            pl.BlockSpec((1, hidden // count_w), lambda i, m: (0, m[0])),
+        ]
+        extra += list(small)
+    if got is not None:
+        specs.append(whole)
+        extra.append(got)
+    return pl.pallas_call(
+        partial(up_kernel, small=bool(small)),
+        grid_spec=pltpu.PrefetchScalarGridSpec(
+            num_scalar_prefetch=1, grid=(1,), in_specs=specs, out_specs=whole
+        ),
+        out_shape=jax.ShapeDtypeStruct((block, columns), BF16),
+        compiler_params=pltpu.CompilerParams(vmem_limit_bytes=24 << 20),
+        name="up_slab",
+    )(meta, normed, pre, mixed, branch, *extra)
+
+
+def head_kernel(meta_ref, turned_ref, query_ref, kv_ref, *refs):
+    block = turned_ref.shape[0]
+    part = query_ref.shape[0]
+    out_ref = refs[-1]
+
+    def put(value, rows, columns):
+        if len(refs) == 2:
+            value = value + refs[0][rows, columns].astype(F32)
+        out_ref[rows, columns] = value.astype(BF16)
+
+    kv = kv_ref[...]
+    query = query_ref[...]
+    turned = turned_ref[...]
+    rows = slice(0, block)
+    put(matmul(turned, kv), rows, slice(0, 2 * part))
+    put(right_trans(turned, query), rows, slice(2 * part, 3 * part))
+    rest = slice(block, block + 16)
+    ones = jnp.ones((16, kv.shape[0]), BF16)
+    put(matmul(ones, kv), rest, slice(0, 2 * part))
+    put(right_trans(ones, query), rest, slice(2 * part, 3 * part))
+
+
+def head_slab(meta, turned, query, kv, count, got=None):
+    width, rows = turned.shape
+    part = query.shape[0]
+    block = width // count
+    whole = pl.BlockSpec((block + 16, 3 * part), lambda i, m: (0, 0))
+    return pl.pallas_call(
+        head_kernel,
+        grid_spec=pltpu.PrefetchScalarGridSpec(
+            num_scalar_prefetch=1,
+            grid=(1,),
+            in_specs=[
+                pl.BlockSpec((block, rows), lambda i, m: (m[0] * 2 + m[1], 0)),
+                pl.BlockSpec((part, rows), lambda i, m: (0, 0)),
+                pl.BlockSpec((rows, 2 * part), lambda i, m: (0, 0)),
+            ]
+            + ([] if got is None else [whole]),
+            out_specs=whole,
+        ),
+        out_shape=jax.ShapeDtypeStruct((block + 16, 3 * part), BF16),
+        compiler_params=pltpu.CompilerParams(vmem_limit_bytes=24 << 20),
+        name="head_slab",
+    )(meta, turned, query, kv, *(() if got is None else (got,)))
+
+
+def token_kernel(query_ref, kv_ref, weight_ref, out_ref):
+    part = query_ref.shape[0]
+    out_ref[...] = (
+        right_trans(kv_ref[...], weight_ref[:, : 2 * part])
+        + right_trans(query_ref[...].T, weight_ref[:, 2 * part :])
+    ).astype(BF16)
+
+
+def token_part(query, kv, weight):
+    return pl.pallas_call(
+        token_kernel,
+        out_shape=jax.ShapeDtypeStruct((kv.shape[0], weight.shape[0]), BF16),
+        compiler_params=pltpu.CompilerParams(vmem_limit_bytes=32 << 20),
+        name="token_part",
+    )(query, kv, weight)
+
+
+def down_finish_kernel(meta_ref, *refs):
+    block = refs[0].shape[0]
+    c_at, x_at = meta_ref[0], meta_ref[1]
+    for at in range(4):
+        place = (c_at ^ (at >> 1)) * 2 + (x_at ^ (at & 1))
+        start = pl.multiple_of(place * block, 8)
+        refs[4][pl.ds(start, block), :] = refs[at][...].astype(F32)
+
+
+def down_finish(meta, pieces):
+    block, width = pieces[0].shape
+    in_vmem = pl.BlockSpec(memory_space=pltpu.VMEM)
+    return pl.pallas_call(
+        down_finish_kernel,
+        grid_spec=pltpu.PrefetchScalarGridSpec(
+            num_scalar_prefetch=1, grid=(), in_specs=[in_vmem] * 4, out_specs=in_vmem
+        ),
+        out_shape=jax.ShapeDtypeStruct((4 * block, width), F32),
+        compiler_params=pltpu.CompilerParams(vmem_limit_bytes=32 << 20),
+        name="down_finish",
+    )(meta, *pieces)
+
+
+def up_finish_kernel(meta_ref, *refs, first):
+    pieces = refs[:4]
+    up_ref, out_ref, *rest = refs[4:]
+    block = pieces[0].shape[0]
+    c_at, x_at = meta_ref[0], meta_ref[1]
+    second = first + out_ref.shape[1] // 2
+    for at in range(4):
+        start = pl.multiple_of((x_at ^ (at & 1)) * block, 8)
+        core = c_at ^ (at >> 1)
+        up_ref[pl.ds(start, block), pl.ds(pl.multiple_of(core * first, 128), first)] = (
+            pieces[at][:, :first].astype(F32)
+        )
+        width = second - first
+        out_ref[pl.ds(start, block), pl.ds(pl.multiple_of(core * width, 128), width)] = (
+            pieces[at][:, first:second].astype(F32)
+        )
+        if rest and at < 2:
+            rest[0][pl.ds(start, block), :] = pieces[at][:, second:].astype(F32)
+
+
+def up_finish(meta, pieces, hidden, width):
+    block, columns = pieces[0].shape
+    in_vmem = pl.BlockSpec(memory_space=pltpu.VMEM)
+    shapes = [(2 * block, hidden), (2 * block, width)]
+    if columns > hidden // 2 + width // 2:
+        shapes.append((2 * block, 128))
+    return pl.pallas_call(
+        partial(up_finish_kernel, first=hidden // 2),
+        grid_spec=pltpu.PrefetchScalarGridSpec(
+            num_scalar_prefetch=1,
+            grid=(),
+            in_specs=[in_vmem] * 4,
+            out_specs=[in_vmem] * len(shapes),
+        ),
+        out_shape=[jax.ShapeDtypeStruct(shape, F32) for shape in shapes],
+        compiler_params=pltpu.CompilerParams(vmem_limit_bytes=40 << 20),
+        name="up_finish",
+    )(meta, *pieces)
+
+
+def head_finish_kernel(meta_ref, own_ref, got_ref, query_ref, key_ref, value_ref, bias_ref, *, part):
+    block = own_ref.shape[1] - 16
+    head_dim = part // 3
+    for at, source in enumerate((own_ref, got_ref)):
+        start = pl.multiple_of((meta_ref[0] ^ at) * block, 8)
+        rows = pl.ds(start, block)
+        keys, values, queries = [], [], []
+        for z in range(ZS):
+            item = source[z].astype(F32)
+            for head in range(3):
+                low = head * 2 * head_dim
+                keys.append(item[:, low : low + head_dim])
+                values.append(item[:, low + head_dim : low + 2 * head_dim])
+            queries.append(item[:, 2 * part :])
+        key = jnp.concatenate(keys, axis=1)
+        value = jnp.concatenate(values, axis=1)
+        query = jnp.concatenate(queries, axis=1)
+        query_ref[rows, :] = query[:block]
+        key_ref[rows, :] = key[:block]
+        value_ref[rows, :] = value[:block]
+        if at == 0:
+            bias_ref[0:8, :] = query[block : block + 8]
+            bias_ref[8:16, :] = value[block : block + 8]
+
+
+def head_finish(meta, own, got):
+    _, block, columns = own.shape
+    rows = 2 * (block - 16)
+    width = ZS * columns // 3
+    in_vmem = pl.BlockSpec(memory_space=pltpu.VMEM)
+    return pl.pallas_call(
+        partial(head_finish_kernel, part=columns // 3),
+        grid_spec=pltpu.PrefetchScalarGridSpec(
+            num_scalar_prefetch=1, grid=(), in_specs=[in_vmem] * 2, out_specs=[in_vmem] * 4
+        ),
+        out_shape=[jax.ShapeDtypeStruct((rows, width), F32)] * 3
+        + [jax.ShapeDtypeStruct((16, width), F32)],
+        compiler_params=pltpu.CompilerParams(vmem_limit_bytes=40 << 20),
+        name="head_finish",
+    )(meta, own, got)
 
 
 def in_order(index, own, other, axis):
@@ -282,16 +696,7 @@
     part = heads * head_dim
     length = lengths[0]
 
-    def gather_w(own):
-        if count_w == 2:
-            return in_order(w_at, own, swap(own, "w"), 0)
-        return lax.all_gather(own, "w", axis=0, tiled=True)
-
-    def gather_w_half(own):
-        if count_w == 2:
-            got = swap(part_of(own, c_at, 2, 0), "w")
-            return in_order(w_at, own, in_order(c_at, got, swap(got, "c"), 0), 0)
-        return lax.all_gather(own, "w", axis=0, tiled=True)
+    hold = lax.optimization_barrier
 
     def head_slice(weight):
         return lax.dynamic_slice_in_dim(weight, z_at * part, part, 1).astype(BF16)
@@ -299,19 +704,16 @@
     low_tokens = tokens.astype(BF16)
     token_all = lax.all_gather(low_tokens, "z", axis=0, tiled=True)
     own_rows = query_weight.shape[0]
-    own_kv = jnp.concatenate(
-        [
-            head_slice(key_weight).reshape(own_rows, heads, 1, head_dim),
-            head_slice(value_weight).reshape(own_rows, heads, 1, head_dim),
-        ],
-        axis=2,
-    ).reshape(own_rows, 2 * part)
-    attn_full = gather_w(jnp.concatenate([head_slice(query_weight), own_kv], axis=1))
-    query_full = attn_full[:, :part]
-    kv_full = attn_full[:, part:]
+    key_own = head_slice(key_weight)
+    value_own = head_slice(value_weight)
+    own_kv = []
+    for head in range(heads):
+        cut = slice(head * head_dim, (head + 1) * head_dim)
+        own_kv += [key_own[:, cut], value_own[:, cut]]
+    attn_own = jnp.concatenate(own_kv + [head_slice(query_weight)], axis=1)
     small = jnp.concatenate(
         [
-            item.astype(BF16).reshape(-1, own_rows)
+            item.astype(BF16)
             for item in (
                 query_bias,
                 value_bias,
@@ -323,32 +725,34 @@
                 second_shift,
                 up_bias,
             )
-        ],
-        axis=0,
-    )
-    small_all = lax.all_gather(small, "w", axis=0, tiled=False).astype(F32)
-    vectors = [small_all[:, at].reshape(width) for at in range(8)]
-    query_offset, value_offset, out_offset, first_scale, first_offset = vectors[:5]
-    down_offset, second_scale, second_offset = vectors[5:]
-    up_offset = small_all[:, 8:].reshape(-1)
-    out_full = gather_w_half(output_weight.astype(BF16))
-    up_full = gather_w_half(up_weight.astype(BF16))
-    down_full = gather_w_half(down_weight.astype(BF16))
-
-    query_own = lax.dynamic_slice_in_dim(query_offset, z_at * part, part, 0)
-    value_own = lax.dynamic_slice_in_dim(value_offset, z_at * part, part, 0)
-    kv_own = jnp.concatenate(
-        [jnp.zeros((heads, 1, head_dim), F32), value_own.reshape(heads, 1, head_dim)],
-        axis=1,
-    ).reshape(2 * part)
-    queries = (
-        lax.dot_general(
-            query_full, token_all, (((0,), (1,)), ((), ())), preferred_element_type=F32
-        )
-        + query_own[:, None]
-    ).astype(BF16)
-    queries = queries * jnp.array(head_dim ** (-0.5), BF16)
-    key_values = (matmul(token_all, kv_full) + kv_own).astype(BF16)
+        ]
+    ).reshape(-1, 3 * part)
+    attn_pack = jnp.concatenate([attn_own, small], axis=0)
+    if count_w == 2:
+        attn_got = swap(attn_pack, "w")
+        attn_full = in_order(w_at, attn_own, attn_got[:own_rows], 0)
+        small_all = in_order(w_at, small[None], attn_got[None, own_rows:], 0)
+    else:
+        attn_all = lax.all_gather(attn_pack, "w", axis=0, tiled=False)
+        attn_full = attn_all[:, :own_rows].reshape(width, 3 * part)
+        small_all = attn_all[:, own_rows:]
+    small_all = small_all.astype(F32).reshape(count_w, -1, own_rows)
+    vec = jnp.transpose(small_all[:, :8], (1, 0, 2)).reshape(8, width)
+    up_offset = small_all[:, 8:].reshape(1, -1)
+    attn_pack, output_weight, up_weight, down_weight = hold(
+        (attn_pack, output_weight, up_weight, down_weight)
+    )
+    low_weights = [item.astype(BF16) for item in (output_weight, up_weight, down_weight)]
+    if count_w == 2:
+        got_weights = [swap(part_of(item, c_at, 2, 0), "w") for item in low_weights]
+    else:
+        got_weights = [lax.all_gather(item, "w", axis=0, tiled=True) for item in low_weights]
+
+    own_bias = lax.dynamic_slice_in_dim(vec[:2], z_at * part, part, 1)
+    value_bias_own = own_bias[1].reshape(heads, 1, head_dim)
+    kv_bias = jnp.concatenate([jnp.zeros_like(value_bias_own), value_bias_own], axis=1)
+    bias_row = jnp.concatenate([kv_bias.reshape(1, 2 * part), own_bias[:1]], axis=1)
+    queries, key_values, turned = project(token_all, attn_full, bias_row)
     kv_blocks = [key_values]
     kv_blocks = kv_blocks + [swap(item, "x") for item in kv_blocks]
     kv_blocks = kv_blocks + [swap(item, "c") for item in kv_blocks]
@@ -360,138 +764,125 @@
         places.append(o_of * 16 + (x_at ^ (at & 1)) * 2 + (c_at ^ ((at >> 1) & 1)))
     meta = jnp.stack([length] + places).astype(jnp.int32)
     attended, logs = attend_forward(meta, queries, kv_blocks)
+    attended, *got_weights = hold((attended, *got_weights))
     low_mixed = lax.all_to_all(attended.astype(BF16), "z", 1, 0, tiled=True)
-
-    branch = left_trans(low_mixed, out_full) + out_offset
-    normed, first_pull = jax.vjp(layer_norm, tokens + branch, first_scale, first_offset)
-    low_normed = normed.astype(BF16)
-    pre_act = matmul(low_normed, up_full) + up_offset
-    activated, gelu_pull = jax.vjp(partial(jax.nn.gelu, approximate=False), pre_act)
-    low_act = activated.astype(BF16)
-    ffn_out = matmul(low_act, down_full) + down_offset
-    outputs, second_pull = jax.vjp(
-        layer_norm, normed + ffn_out, second_scale, second_offset
-    )
+    if count_w == 2:
+        pieces = [
+            (own, got, swap(got, "c")) for own, got in zip(low_weights, got_weights)
+        ]
+    else:
+        pieces = [(item,) for item in got_weights]
+
     my_index = o_at * 16 + z_at * 4 + x_at * 2 + c_at
-    positions = my_index * local_rows + jnp.arange(local_rows, dtype=jnp.int32)
-    valid = (positions < length).astype(F32)
-    seed_grad = cotangent[0] * valid[:, None]
-    sum_grad, grad_second_gain, grad_second_shift = second_pull(seed_grad)
-    ffn_grad = sum_grad.astype(BF16)
-    grad_down_bias = jnp.sum(ffn_grad.astype(F32), axis=0)
-    (act_grad,) = gelu_pull(right_trans(ffn_grad, down_full))
-    pre_grad = act_grad.astype(BF16)
-    grad_up_bias = jnp.sum(pre_grad.astype(F32), axis=0)
-    normed_grad = right_trans(pre_grad, up_full) + sum_grad
-    resid_grad, grad_first_gain, grad_first_shift = first_pull(normed_grad)
-    branch_grad = resid_grad.astype(BF16)
-    grad_output_bias = jnp.sum(branch_grad.astype(F32), axis=0)
-    mixed_grad = right_trans(out_full, branch_grad).astype(BF16)
+    rest = jnp.clip(length - my_index * local_rows, 0, local_rows)
+    other = 2 * (1 - w_at)
+    spots = jnp.stack([rest, 2 * w_at, other + c_at, other + 1 - c_at]).astype(jnp.int32)
+    (
+        outputs,
+        resid_grad,
+        mixed_grad,
+        act_turned,
+        pre_grad,
+        ffn_grad,
+        normed_turned,
+        branch_grad,
+        small_sum,
+        upsum,
+    ) = middle(spots, low_mixed, tokens, cotangent[0], vec, up_offset, pieces)
     head_grads = lax.all_to_all(mixed_grad, "z", 0, 1, tiled=True)
-
-    def sum_w(slabs):
+    hidden = pre_grad.shape[1]
+
+    def add_pair(kept, got):
+        return (kept.astype(F32) + got.astype(F32)).astype(BF16)
+
+    def halve(value, axis, bit, perm, dim):
+        got = lax.ppermute(part_of(value, 1 - bit, 2, dim), axis, perm)
+        return add_pair(part_of(value, bit, 2, dim), got)
+
+    def unite(value, axis, bit, perm, dim):
+        return in_order(bit, value, lax.ppermute(value, axis, perm), dim)
+
+    near = ((0, 1), (1, 0), (2, 3), (3, 2))
+    far = ((0, 2), (2, 0), (1, 3), (3, 1))
+
+    def sum_line(value):
+        if count_o == 2:
+            value = add_pair(value, swap(value, "o"))
+        value = halve(value, "x", x_at, SWAP, 0)
+        value = halve(value, "z", z_at & 1, near, 0)
+        value = halve(value, "z", z_at >> 1, far, 0)
+        value = unite(value, "z", z_at >> 1, far, 0)
+        return unite(value, "z", z_at & 1, near, 0)
+
+    def four_pieces(value):
+        got = swap(value, "x")
+        return [value, got, swap(value, "c"), swap(got, "c")]
+
+    def pick(w, c):
+        return jnp.stack([jnp.asarray(w), jnp.asarray(c)]).astype(jnp.int32)
+
+    def core_sum(slab):
         if count_w == 2:
-            kept = lax.dynamic_index_in_dim(slabs, w_at, 0, keepdims=False)
-            sent = lax.dynamic_index_in_dim(slabs, 1 - w_at, 0, keepdims=False)
-            return (kept.astype(F32) + swap(sent, "w").astype(F32)).astype(BF16)
-        return lax.psum_scatter(slabs, "w", scatter_dimension=0, tiled=True)[0]
-
-    hidden = low_act.shape[1]
-    act_cut = low_act.reshape(local_rows, count_w, 2, hidden // count_w // 2)
-    act_own = lax.dynamic_index_in_dim(act_cut, c_at, 2, keepdims=False)
-    act_sent = lax.dynamic_index_in_dim(act_cut, 1 - c_at, 2, keepdims=False)
-    act_rows = jnp.concatenate([act_own, swap(act_sent, "c")], axis=0)
-    ffn_rows = jnp.concatenate([ffn_grad, swap(ffn_grad, "c")], axis=0)
-    down_slabs = lax.dot_general(
-        act_rows, ffn_rows, (((0,), (0,)), ((), ())), preferred_element_type=F32
-    ).astype(BF16)
-    pre_own = part_of(pre_grad, c_at, 2, 1)
-    pre_rows = jnp.concatenate([pre_own, swap(part_of(pre_grad, 1 - c_at, 2, 1), "c")], axis=0)
-    normed_rows = jnp.concatenate([low_normed, swap(low_normed, "c")], axis=0)
-    up_slabs = left_trans(normed_rows, pre_rows).astype(BF16)
-    up_slabs = up_slabs.reshape(count_w, own_rows, hidden // 2)
-    branch_rows = jnp.concatenate(
-        [part_of(branch_grad, c_at, 2, 1), swap(part_of(branch_grad, 1 - c_at, 2, 1), "c")],
-        axis=0,
-    )
-    mixed_rows = jnp.concatenate([low_mixed, swap(low_mixed, "c")], axis=1)
-    out_slabs = matmul(mixed_rows, branch_rows).astype(BF16)
-    out_slabs = out_slabs.reshape(count_w, own_rows, width // 2)
-    line = ("o", "z", "x")
-    down_sum = lax.psum(sum_w(down_slabs), line)
-    up_sum = lax.psum(sum_w(up_slabs), line)
-    out_sum = lax.psum(sum_w(out_slabs), line)
-    total_down = in_order(c_at, down_sum, swap(down_sum, "c"), 0).astype(F32)
-    total_up = in_order(c_at, up_sum, swap(up_sum, "c"), 1).astype(F32)
-    total_out = in_order(c_at, out_sum, swap(out_sum, "c"), 1).astype(F32)
+            got_far = swap(slab(pick(1 - w_at, 1 - c_at)), "c")
+            got_near = swap(slab(pick(1 * w_at, 1 - c_at)), "c")
+            return slab(pick(1 - w_at, c_at), got_far), slab(pick(1 * w_at, c_at), got_near)
+        got = [swap(slab(pick(w, 1 - c_at)), "c") for w in range(count_w)]
+        return (jnp.stack([slab(pick(w, c_at), got[w]) for w in range(count_w)]),)
+
+    def y_sum(sums):
+        if count_w == 2:
+            return add_pair(sums[1], swap(sums[0], "w"))
+        return lax.psum_scatter(sums[0], "w", scatter_dimension=0, tiled=True)[0]
+
+    smalls = (small_sum, upsum) if count_w == 2 else ()
+    down_sums = core_sum(
+        lambda m, got=None: down_slab(m, act_turned, ffn_grad, 2 * count_w, got)
+    )
+    up_sums = core_sum(
+        lambda m, got=None: up_slab(
+            m, normed_turned, pre_grad, low_mixed, branch_grad, smalls, count_w, got
+        )
+    )
+    down_sums, up_sums, head_grads = hold((down_sums, up_sums, head_grads))
+    down_sum = sum_line(y_sum(down_sums))
+    up_sum = sum_line(y_sum(up_sums))
+    spot = jnp.stack([c_at, x_at]).astype(jnp.int32)
+    total_down = down_finish(spot, four_pieces(down_sum))
+    total_up, total_out, *small_total = up_finish(spot, four_pieces(up_sum), hidden, width)
 
     query_low, *kv_parts = attend_backward(
         meta, queries, head_grads, attended, logs, kv_blocks
     )
-
-    def add_pair(kept, got):
-        return (kept.astype(F32) + got.astype(F32)).astype(BF16)
-
     if count_o == 2:
         kv_parts = [add_pair(kv_parts[at], swap(kv_parts[at + 4], "o")) for at in range(4)]
     kv_parts = [add_pair(kv_parts[at], swap(kv_parts[at + 2], "c")) for at in range(2)]
     kv_low = add_pair(kv_parts[0], swap(kv_parts[1], "x"))
-    token_part = (
-        lax.dot_general(
-            query_low, query_full, (((0,), (1,)), ((), ())), preferred_element_type=F32
-        )
-        + right_trans(kv_low, kv_full)
-    ).astype(BF16)
-    token_grad = lax.psum_scatter(token_part, "z", scatter_dimension=0, tiled=True)
+    token_sum = token_part(query_low, kv_low, attn_full)
+    token_grad = lax.psum_scatter(token_sum, "z", scatter_dimension=0, tiled=True)
     input_grad = resid_grad + token_grad.astype(F32)
-    attn_part = jnp.concatenate(
-        [
-            lax.dot_general(
-                token_all, query_low, (((0,), (1,)), ((), ())), preferred_element_type=F32
-            ),
-            left_trans(token_all, kv_low),
-        ],
-        axis=1,
-    ).astype(BF16)
-    attn_own = sum_w(attn_part.reshape(count_w, own_rows, 3 * part))
-    attn_own = lax.psum(attn_own, ("o", "x", "c"))
-    attn_all = lax.all_gather(attn_own, "z", axis=0, tiled=False).astype(F32)
-    total_query = jnp.transpose(attn_all[:, :, :part], (1, 0, 2)).reshape(own_rows, width)
-    pairs = attn_all[:, :, part:].reshape(ZS, own_rows, heads, 2, head_dim)
-    pairs = jnp.transpose(pairs, (3, 1, 0, 2, 4)).reshape(2, own_rows, width)
-    total_key, total_value = pairs[0], pairs[1]
-
-    query_sum = jnp.sum(query_low.astype(F32), axis=1)
-    value_sum = jnp.sum(kv_low.astype(F32), axis=0).reshape(heads, 2, head_dim)[:, 1]
-    blank = jnp.zeros((width,), F32)
-    grad_query_bias = lax.dynamic_update_slice_in_dim(blank, query_sum, z_at * part, 0)
-    grad_value_bias = lax.dynamic_update_slice_in_dim(
-        blank, value_sum.reshape(part), z_at * part, 0
-    )
-    packed = jnp.concatenate(
-        [
-            item.reshape(-1, 128)
-            for item in (
-                grad_query_bias,
-                grad_value_bias,
-                grad_output_bias,
-                grad_first_gain,
-                grad_first_shift,
-                grad_down_bias,
-                grad_second_gain,
-                grad_second_shift,
-                grad_up_bias,
-            )
-        ],
-        axis=0,
-    )
-    packed = lax.psum(packed, ("o", "z", "x", "c", "w"))
-    each = width // 128
-    totals = [
-        part_of(packed[at * each : (at + 1) * each].reshape(width), w_at, count_w, 0)
-        for at in range(8)
-    ]
-    total_up_bias = part_of(packed[8 * each :].reshape(-1), w_at, count_w, 0)
+    head_sum = y_sum(
+        core_sum(lambda m, got=None: head_slab(m, turned, query_low, kv_low, 2 * count_w, got))
+    )
+    head_sum = add_pair(head_sum, swap(head_sum, "x"))
+    if count_o == 2:
+        head_sum = add_pair(head_sum, swap(head_sum, "o"))
+    head_two = unite(head_sum[None], "z", z_at & 1, near, 0)
+    head_four = unite(head_two, "z", z_at >> 1, far, 0)
+    total_query, total_key, total_value, head_bias = head_finish(
+        spot, head_four, swap(head_four, "c")
+    )
+    totals = [part_of(head_bias[at], w_at, count_w, 0) for at in (0, 8)]
+    if count_w == 2:
+        groups = own_rows // 128
+        table = small_total[0][: 8 * groups].reshape(groups, 8, 128)
+        totals += [table[:, at].reshape(own_rows) for at in range(6)]
+        lines = hidden // count_w // 128
+        total_up_bias = small_total[0][8 * groups : 8 * groups + lines].reshape(-1)
+    else:
+        every = ("o", "z", "x", "c", "w")
+        small_sum, upsum = lax.psum((small_sum, upsum), every)
+        totals += [part_of(small_sum[at], w_at, count_w, 0) for at in range(6)]
+        total_up_bias = part_of(upsum[0], w_at, count_w, 0)
     return (
         outputs[None],
         input_grad[None],

time: 599 us -> 454 us (0.76)
  blocking collectives: 74.7 us -> 0 us
  Pallas kernels: 49.1 us -> 120 us
  waiting for transfers between devices: 260 us -> 196 us
  matrix products: 48.3 us -> 0 us
  local copies, waits for them, and re-layouts: 56.7 us -> 32.3 us
  other arithmetic: 45.8 us -> 26.9 us
  starting transfers between devices: 44 us -> 54.9 us
    psum x2 -> x0, waiting for transfers between devices: 108 us -> none  [the longest x1 79.7 us: body(): out_sum = lax.psum(sum_w(out_slabs), line)]
    ppermute x0 -> x12, waiting for transfers between devices: none -> 82.4 us  [the longest x6 50.2 us: halve(): got = lax.ppermute(part_of(value, 1 - bit, 2, dim), axis, perm)]
    pallas_call x0 -> x18, Pallas kernels: none -> 58 us  [the longest x1 15.4 us: middle(): pl.pallas_call(partial(middle_kernel, counts=tuple((len(group) for group...]
    dot_general x15 -> x0, matrix products: 48.3 us -> none  [the longest x4 22.7 us: matmul(): return jnp.dot(left_side, right_side, preferred_element_type=F32)]
    psum x1 -> x0, blocking collectives: 43.7 us -> none  [body(): packed = lax.psum(packed, ('o', 'z', 'x', 'c', 'w'))]
    all_gather x1 -> x0, waiting for transfers between devices: 39 us -> none  [body(): attn_all = lax.all_gather(attn_own, 'z', axis=0, tiled=False).astype(F32)]
    all_gather x1 -> x0, blocking collectives: 31 us -> none  [body(): small_all = lax.all_gather(small, 'w', axis=0, tiled=False).astype(F32)]
    reduce_scatter x1, waiting for transfers between devices: 27.7 us -> 0.01 us  [body(): lax.psum_scatter(token_sum, 'z', scatter_dimension=0, tiled=True)]
  transfers between devices with their start and end apart: 33 -> 46, of which waited for: 11 -> 18; matrix products, arithmetic and copies ran while one was open for 24% -> 9% of each run, Pallas kernels for 8% -> 21%
where the time goes in v2:
time: 454 us; the launch traced here: 446 us
  waiting for transfers between devices  196 us (43%)
  Pallas kernels  120 us (26%)
  starting transfers between devices  54.9 us (12%)
  local copies, waits for them, and re-layouts  32.3 us (7%)
  other arithmetic  26.9 us (6%)
  between operations  16 us (4%)
    ppermute x30, waiting for transfers between devices, swap(): return lax.ppermute(value, axis, SWAP)  73.1 us
    ppermute x6, waiting for transfers between devices, halve(): got = lax.ppermute(part_of(value, 1 - bit, 2, dim), axis, perm)  50.2 us
    ppermute x30, starting transfers between devices, swap(): return lax.ppermute(value, axis, SWAP)  37.8 us
    pallas_call x1, Pallas kernels, attend_backward(): pl.pallas_call(partial(backward_kernel, blocks=blocks, rows=block_rows //...  36.6 us
    ppermute x6, waiting for transfers between devices, unite(): return in_order(bit, value, lax.ppermute(value, axis, perm), dim)  32.1 us
    pallas_call x1, Pallas kernels, attend_forward(): pl.pallas_call(partial(forward_kernel, blocks=blocks, rows=block_rows //...  25.2 us
    all_gather x1, waiting for transfers between devices, body(): token_all = lax.all_gather(low_tokens, 'z', axis=0, tiled=True)  20.9 us
    unnamed x102, local copies, waits for them, and re-layouts  16.5 us
  transfers between devices with their start and end apart: 46, of which 18 were waited for; matrix products, arithmetic and copies ran while one was open for 9% of the time, Pallas kernels for 21%

profile of v2, /device:TPU:1, one launch (start us, length us, event | category | flops | bytes accessed | tf_op | source)
XLA Modules:
  0.0 445.9 jit_solution(8332735138140266667)
XLA Ops:
  15.7 11.2 %collective-permute-done = bf16[392,576]{1,0:T(8,128)(2,1)S(1)} collective-permute-done((bf16[392,576]{1,0:T(8,128)(2,1)S(1)}, bf16[392,576]{1,0:T(8,128)(2,1)S(1)}, u32[]{:S(2)}, u32[]{:S(2)}) %collective-permute-start) | collective-permute-done | bytes 451616 | tf_op jit(solution)/shard_map/ppermute | solution.py:29
  28.5 20.9 %all-gather.2.cloned.1.call-done.tokens_ref = bf16[1024,768]{1,0:T(8,128)(2,1)} async-done(((bf16[256,768]{1,0:T(8,128)(2,1)}), bf16[1024,768]{1,0:T(8,128)(2,1)}) %all-gather.2.cloned.1.call-update) | async-done | bytes 1572880 | tf_op jit(solution)/shard_map/all_gather | solution.py:705
  55.3 16.1 %collective-permute-done.1.refs_1_ = bf16[1024,384]{1,0:T(8,128)(2,1)} collective-permute-done((bf16[1024,384]{1,0:T(8,128)(2,1)S(1)}, bf16[1024,384]{1,0:T(8,128)(2,1)}, u32[]{:S(2)}, u32[]{:S(2)}) %collective-permute-start.1) | collective-permute-done | bytes 786464 | tf_op jit(solution)/shard_map/ppermute | solution.py:29
  73.1 4.1 convert_element_type.190.refs_3_
  77.2 2.5 constant_dynamic-slice_fusion.9
  82.0 4.0 convert_element_type.191.refs_6_
  89.9 25.2 %attend_forward.1 = (f32[192,1024]{1,0:T(8,128)}, f32[3,1,1024]{2,1,0:T(1,128)}) custom-call(s32[5]{0:T(128)} %stack.98.meta_ref, bf16[192,1024]{1,0:T(8,128)(2,1)} %copy-done.30, bf16[1024,384]{1,0:T(8,128)(2,1)} %copy-done.29, bf16[1024,384]{1,0:T(8,128)(2,1)} %collective-permute-done.1.refs_1_, bf16[1024,384]{1,0:T(8,128)(2,1)} %collective-permute-done.2.refs_2_, ...), custom_call_target="tpu_custom_call" | custom-call | flops 12884901888 | bytes 3145728 | tf_op jit(solution)/shard_map/attend_forward/pallas_call | solution.py:106
  115.1 24.1 %collective-permute-done.6.refs_7_ = bf16[768,768]{1,0:T(8,128)(2,1)} collective-permute-done((bf16[768,768]{1,0:T(8,128)(2,1)S(1)}, bf16[768,768]{1,0:T(8,128)(2,1)}, u32[]{:S(2)}, u32[]{:S(2)}) %collective-permute-start.6) | collective-permute-done | bytes 1179680 | tf_op jit(solution)/shard_map/ppermute | solution.py:29
  141.9 3.6 all-to-all-start
  148.3 8.5 %all-to-all-done = bf16[192,4,256]{2,0,1:T(8,128)(2,1)S(1)} async-done(((bf16[192,4,256]{2,0,1:T(8,128)(2,1)}), bf16[192,4,256]{2,0,1:T(8,128)(2,1)S(1)}, u32[]{:S(2)}, u32[]{:S(2)}) %all-to-all-start) | async-done | bytes 393248 | tf_op jit(solution)/shard_map/all_to_all | solution.py:768
  157.6 15.4 %middle.1 = (f32[256,768]{1,0:T(8,128)}, f32[256,768]{1,0:T(8,128)}, bf16[768,256]{1,0:T(8,128)(2,1)}, bf16[3072,256]{1,0:T(8,128)(2,1)}, bf16[256,3072]{1,0:T(8...) custom-call(s32[4]{0:T(128)} %pad_add_fusion.meta_ref, ...), custom_call_target="tpu_custom_call" | custom-call | tf_op jit(solution)/shard_map/middle/pallas_call | solution.py:358
  189.3 3.5 all-to-all-start.1
  193.1 10.9 %all-to-all-done.1 = bf16[4,192,256]{2,1,0:T(8,128)(2,1)S(1)} async-done(((bf16[4,192,256]{2,1,0:T(8,128)(2,1)}), bf16[4,192,256]{2,1,0:T(8,128)(2,1)S(1)}, u32[]{:S(2)}, u32[]{:S(2)}) %all-to-all-start.1) | async-done | bytes 393248 | tf_op jit(solution)/shard_map/all_to_all | solution.py:792
  209.6 3.6 down_slab.5
  213.2 2.5 up_slab.7
  216.9 3.7 up_slab.5
  222.1 36.6 %attend_backward.1 = (bf16[192,1024]{1,0:T(8,128)(2,1)}, bf16[1024,384]{1,0:T(8,128)(2,1)}, bf16[1024,384]{1,0:T(8,128)(2,1)}, bf16[1024,384]{1,0:T(8,128)(2,1)}, bf16[1024,384]{1,0:T(8,128)(2,1)}) custom-call(s32[5]{0:T(128)} %stack.98.meta_ref, bf16[192,1024]{1,0:T(8,128)(2,1)} %copy-done.30, bf16[192,1024]{1,0:T(8,128)(2,1)} %bitcast.58, ...), custom_call_target="tpu_custom_call" | custom-call | flops 32212254720 | bytes 6291456 | tf_op jit(solution)/shard_map/attend_backward/pallas_call | solution.py:198
  269.5 11.3 %collective-permute-done.24 = bf16[384,2048]{1,0:T(8,128)(2,1)} collective-permute-done((bf16[384,2048]{1,0:T(8,128)(2,1)}, bf16[384,2048]{1,0:T(8,128)(2,1)}, u32[]{:S(2)}, u32[]{:S(2)}) %collective-permute-start.24) | collective-permute-done | bytes 1572896 | tf_op jit(solution)/shard_map/ppermute | solution.py:29
  293.0 2.5 collective-permute-start.17
  302.0 12.0 %collective-permute-done.25 = bf16[192,2048]{1,0:T(8,128)(2,1)} collective-permute-done((bf16[192,2048]{1,0:T(8,128)(2,1)}, bf16[192,2048]{1,0:T(8,128)(2,1)}, u32[]{:S(2)}, u32[]{:S(2)}) %collective-permute-start.25) | collective-permute-done | bytes 786464 | tf_op jit(solution)/shard_map/ppermute | solution.py:799
  318.4 25.3 %collective-permute-done.26 = bf16[96,2048]{1,0:T(8,128)(2,1)S(1)} collective-permute-done((bf16[96,2048]{1,0:T(8,128)(2,1)S(1)}, bf16[96,2048]{1,0:T(8,128)(2,1)S(1)}, u32[]{:S(2)}, u32[]{:S(2)}) %collective-permute-start.26) | collective-permute-done | bytes 393248 | tf_op jit(solution)/shard_map/ppermute | solution.py:799
  346.4 11.5 %collective-permute-done.27 = bf16[48,2048]{1,0:T(8,128)(2,1)S(1)} collective-permute-done((bf16[48,2048]{1,0:T(8,128)(2,1)S(1)}, bf16[48,2048]{1,0:T(8,128)(2,1)S(1)}, u32[]{:S(2)}, u32[]{:S(2)}) %collective-permute-start.27) | collective-permute-done | bytes 196640 | tf_op jit(solution)/shard_map/ppermute | solution.py:799
  360.0 4.2 collective-permute-done.37
  364.3 5.2 %collective-permute-done.28 = bf16[48,2048]{1,0:T(8,128)(2,1)S(1)} collective-permute-done((bf16[48,2048]{1,0:T(8,128)(2,1)S(1)}, bf16[48,2048]{1,0:T(8,128)(2,1)S(1)}, u32[]{:S(2)}, u32[]{:S(2)}) %collective-permute-start.28) | collective-permute-done | bytes 196640 | tf_op jit(solution)/shard_map/ppermute | solution.py:803
  371.8 15.7 %collective-permute-done.38 = bf16[192,768]{1,0:T(8,128)(2,1)S(1)} collective-permute-done((bf16[192,768]{1,0:T(8,128)(2,1)S(1)}, bf16[192,768]{1,0:T(8,128)(2,1)S(1)}, u32[]{:S(2)}, u32[]{:S(2)}) %collective-permute-start.38) | collective-permute-done | bytes 294944 | tf_op jit(solution)/shard_map/ppermute | solution.py:803
  388.9 7.0 %collective-permute-done.29 = bf16[96,2048]{1,0:T(8,128)(2,1)S(1)} collective-permute-done((bf16[96,2048]{1,0:T(8,128)(2,1)S(1)}, bf16[96,2048]{1,0:T(8,128)(2,1)S(1)}, u32[]{:S(2)}, u32[]{:S(2)}) %collective-permute-start.29) | collective-permute-done | bytes 393248 | tf_op jit(solution)/shard_map/ppermute | solution.py:803
  400.1 7.6 %collective-permute-start.41 = (bf16[384,768]{1,0:T(8,128)(2,1)S(1)}, bf16[384,768]{1,0:T(8,128)(2,1)}, u32[]{:S(2)}, u32[]{:S(2)}) collective-permute-start(bf16[384,768]{1,0:T(8,128)(2,1)S(1)} %collective-permute-done.39.refs_1_), channel_id=1, source_target_pairs={{0,2},{2,0},{1,3},{3,1},{4,6},{6,4},{5,7},{7,5},{8,10},{10,8},{9,1... | collective-permute-start | bytes 1769480 | tf_op jit(solution)/shard_map/ppermute | solution.py:29
  407.7 8.2 %collective-permute-done.30.refs_1_ = bf16[192,2048]{1,0:T(8,128)(2,1)} collective-permute-done((bf16[192,2048]{1,0:T(8,128)(2,1)S(1)}, bf16[192,2048]{1,0:T(8,128)(2,1)}, u32[]{:S(2)}, u32[]{:S(2)}) %collective-permute-start.30) | collective-permute-done | bytes 786464 | tf_op jit(solution)/shard_map/ppermute | solution.py:29
  415.8 4.6 %collective-permute-start.32 = (bf16[192,2048]{1,0:T(8,128)(2,1)}, bf16[192,2048]{1,0:T(8,128)(2,1)}, u32[]{:S(2)}, u32[]{:S(2)}) collective-permute-start(bf16[192,2048]{1,0:T(8,128)(2,1)} %collective-permute-done.30.refs_1_), channel_id=1, source_target_pairs={{0,2},{2,0},{1,3},{3,1},{4,6},{6,4},{5,7},{7,5},{8,10},{10,8},{9,1... | collective-permute-start | bytes 2359304 | tf_op jit(solution)/shard_map/ppermute | solution.py:29
  420.5 4.3 down_finish.1
  424.8 4.1 head_finish.1
  432.3 5.1 %up_finish.1 = (f32[384,3072]{1,0:T(8,128)}, f32[384,768]{1,0:T(8,128)}, f32[384,128]{1,0:T(8,128)S(1)}) custom-call(s32[2]{0:T(128)S(1)} %pad_add_fusion.1.meta_ref, bf16[192,2048]{1,0:T(8,128)(2,1)S(1)} %maximum_select_fusion.2.refs_0_, bf16[192,2048]{1,0:T(8,128)(2,1)} %collective-permute-done.30.refs_1_, ...), custom_call_target="tpu_custom_call" | custom-call | tf_op jit(solution)/shard_map/up_finish/pallas_call | solution.py:595
  (263 shorter events, 105.1 us)
Async XLA Ops:
  7.3 42.1 %all-gather.2.cloned.1.call-start = ((), (), s32[]{:S(2)}) async-start(), calls=%async_computation.3 | async-start | bytes 1966080 | tf_op jit(solution)/shard_map/all_gather | solution.py:705
  53.1 18.4 %collective-permute-start.1 = (bf16[1024,384]{1,0:T(8,128)(2,1)S(1)}, bf16[1024,384]{1,0:T(8,128)(2,1)}, u32[]{:S(2)}, u32[]{:S(2)}) collective-permute-start(bf16[1024,384]{1,0:T(8,128)(2,1)S(1)} %get-tuple-element.57.refs_0_), channel_id=1, source_target_pairs={{0,4},{4,0},{1,5},{5,1},{2,6},{6,2},{3,7},{7,3},{8,12},{12,8},{9,1... | collective-permute-start | bytes 2359304 | tf_op jit(solution)/shard_map/ppermute | solution.py:29
  54.2 35.7 %collective-permute-start.2 = (bf16[1024,384]{1,0:T(8,128)(2,1)S(1)}, bf16[1024,384]{1,0:T(8,128)(2,1)}, u32[]{:S(2)}, u32[]{:S(2)}) collective-permute-start(bf16[1024,384]{1,0:T(8,128)(2,1)S(1)} %get-tuple-element.57.refs_0_), channel_id=1, source_target_pairs={{0,2},{2,0},{1,3},{3,1},{4,6},{6,4},{5,7},{7,5},{8,10},{10,8},{9,1... | collective-permute-start | bytes 2359304 | tf_op jit(solution)/shard_map/ppermute | solution.py:29
  71.4 18.5 %collective-permute-start.3 = (bf16[1024,384]{1,0:T(8,128)(2,1)}, bf16[1024,384]{1,0:T(8,128)(2,1)}, u32[]{:S(2)}, u32[]{:S(2)}) collective-permute-start(bf16[1024,384]{1,0:T(8,128)(2,1)} %collective-permute-done.1.refs_1_), channel_id=1, source_target_pairs={{0,2},{2,0},{1,3},{3,1},{4,6},{6,4},{5,7},{7,5},{8,10},{10,8},{9,1... | collective-permute-start | bytes 2359304 | tf_op jit(solution)/shard_map/ppermute | solution.py:29
  79.7 35.4 %collective-permute-start.5 = (bf16[192,3072]{1,0:T(8,128)(2,1)}, bf16[192,3072]{1,0:T(8,128)(2,1)}, u32[]{:S(2)}, u32[]{:S(2)}) collective-permute-start(bf16[192,3072]{1,0:T(8,128)(2,1)} %constant_dynamic-slice_fusion.9), channel_id=1, source_target_pairs={{0,1},{1,0},{2,3},{3,2},{4,5},{5,4},{6,7},{7,6},{8,9},{9,8},{10,11... | collective-permute-start | bytes 3538952 | tf_op jit(solution)/shard_map/ppermute | solution.py:29
  81.7 33.4 %collective-permute-start.4 = (bf16[192,768]{1,0:T(8,128)(2,1)}, bf16[192,768]{1,0:T(8,128)(2,1)}, u32[]{:S(2)}, u32[]{:S(2)}) collective-permute-start(bf16[192,768]{1,0:T(8,128)(2,1)} %constant_dynamic-slice_fusion.10), channel_id=1, source_target_pairs={{0,1},{1,0},{2,3},{3,2},{4,5},{5,4},{6,7},{7,6},{8,9},{9,8},{10,11... | collective-permute-start | bytes 884744 | tf_op jit(solution)/shard_map/ppermute | solution.py:29
  87.3 51.8 %collective-permute-start.6 = (bf16[768,768]{1,0:T(8,128)(2,1)S(1)}, bf16[768,768]{1,0:T(8,128)(2,1)}, u32[]{:S(2)}, u32[]{:S(2)}) collective-permute-start(bf16[768,768]{1,0:T(8,128)(2,1)S(1)} %constant_dynamic-slice_fusion.8), channel_id=1, source_target_pairs={{0,1},{1,0},{2,3},{3,2},{4,5},{5,4},{6,7},{7,6},{8,9},{9,8},{10,11... | collective-permute-start | bytes 3538952 | tf_op jit(solution)/shard_map/ppermute | solution.py:29
  139.2 17.6 %collective-permute-start.8 = (bf16[192,3072]{1,0:T(8,128)(2,1)}, bf16[192,3072]{1,0:T(8,128)(2,1)}, u32[]{:S(2)}, u32[]{:S(2)}) collective-permute-start(bf16[192,3072]{1,0:T(8,128)(2,1)} %collective-permute-done.5.refs_4_), channel_id=1, source_target_pairs={{0,2},{2,0},{1,3},{3,1},{4,6},{6,4},{5,7},{7,5},{8,10},{10,8},{9,1... | collective-permute-start | bytes 3538952 | tf_op jit(solution)/shard_map/ppermute | solution.py:29
  181.1 32.1 %collective-permute-start.13 = (bf16[384,2048]{1,0:T(8,128)(2,1)}, bf16[384,2048]{1,0:T(8,128)(2,1)}, u32[]{:S(2)}, u32[]{:S(2)}) collective-permute-start(bf16[384,2048]{1,0:T(8,128)(2,1)} %up_slab.6), channel_id=1, source_target_pairs={{0,2},{2,0},{1,3},{3,1},{4,6},{6,4},{5,7},{7,5},{8,10},{10,8},{9,1... | collective-permute-start | bytes 4718600 | tf_op jit(solution)/shard_map/ppermute | solution.py:29
  184.7 32.2 %collective-permute-start.12 = (bf16[384,2048]{1,0:T(8,128)(2,1)}, bf16[384,2048]{1,0:T(8,128)(2,1)}, u32[]{:S(2)}, u32[]{:S(2)}) collective-permute-start(bf16[384,2048]{1,0:T(8,128)(2,1)} %up_slab.4), channel_id=1, source_target_pairs={{0,2},{2,0},{1,3},{3,1},{4,6},{6,4},{5,7},{7,5},{8,10},{10,8},{9,1... | collective-permute-start | bytes 4718600 | tf_op jit(solution)/shard_map/ppermute | solution.py:29
  186.8 18.1 %collective-permute-start.11 = (bf16[768,768]{1,0:T(8,128)(2,1)}, bf16[768,768]{1,0:T(8,128)(2,1)}, u32[]{:S(2)}, u32[]{:S(2)}) collective-permute-start(bf16[768,768]{1,0:T(8,128)(2,1)} %down_slab.6), channel_id=1, source_target_pairs={{0,2},{2,0},{1,3},{3,1},{4,6},{6,4},{5,7},{7,5},{8,10},{10,8},{9,1... | collective-permute-start | bytes 3538952 | tf_op jit(solution)/shard_map/ppermute | solution.py:29
  189.3 20.3 %collective-permute-start.10 = (bf16[768,768]{1,0:T(8,128)(2,1)}, bf16[768,768]{1,0:T(8,128)(2,1)}, u32[]{:S(2)}, u32[]{:S(2)}) collective-permute-start(bf16[768,768]{1,0:T(8,128)(2,1)} %down_slab.4), channel_id=1, source_target_pairs={{0,2},{2,0},{1,3},{3,1},{4,6},{6,4},{5,7},{7,5},{8,10},{10,8},{9,1... | collective-permute-start | bytes 3538952 | tf_op jit(solution)/shard_map/ppermute | solution.py:29
  192.8 237.2 %reduce-scatter.2.cloned.1.call-start = ((), (), s32[]{:S(2)}) async-start(), calls=%async_computation.4 | async-start | bytes 1966080 | tf_op jit(solution)/shard_map/reduce_scatter | solution.py:861
  220.6 46.0 %collective-permute-start.33 = (bf16[768,768]{1,0:T(8,128)(2,1)}, bf16[768,768]{1,0:T(8,128)(2,1)}, u32[]{:S(2)}, u32[]{:S(2)}) collective-permute-start(bf16[768,768]{1,0:T(8,128)(2,1)} %down_slab.5), channel_id=1, source_target_pairs={{0,1},{1,0},{2,3},{3,2},{4,5},{5,4},{6,7},{7,6},{8,9},{9,8},{10,11... | collective-permute-start | bytes 3538952 | tf_op jit(solution)/shard_map/ppermute | solution.py:29
  221.8 59.0 %collective-permute-start.24 = (bf16[384,2048]{1,0:T(8,128)(2,1)}, bf16[384,2048]{1,0:T(8,128)(2,1)}, u32[]{:S(2)}, u32[]{:S(2)}) collective-permute-start(bf16[384,2048]{1,0:T(8,128)(2,1)} %up_slab.5), channel_id=1, source_target_pairs={{0,1},{1,0},{2,3},{3,2},{4,5},{5,4},{6,7},{7,6},{8,9},{9,8},{10,11... | collective-permute-start | bytes 4718600 | tf_op jit(solution)/shard_map/ppermute | solution.py:29
  260.7 25.4 %collective-permute-start.14 = (bf16[1024,384]{1,0:T(8,128)(2,1)}, bf16[1024,384]{1,0:T(8,128)(2,1)}, u32[]{:S(2)}, u32[]{:S(2)}) collective-permute-start(bf16[1024,384]{1,0:T(8,128)(2,1)} %get-tuple-element.80), channel_id=1, source_target_pairs={{0,2},{2,0},{1,3},{3,1},{4,6},{6,4},{5,7},{7,5},{8,10},{10,8},{9,1... | collective-permute-start | bytes 2359304 | tf_op jit(solution)/shard_map/ppermute | solution.py:29
  265.4 20.7 %collective-permute-start.16 = (bf16[1024,384]{1,0:T(8,128)(2,1)}, bf16[1024,384]{1,0:T(8,128)(2,1)}, u32[]{:S(2)}, u32[]{:S(2)}) collective-permute-start(bf16[1024,384]{1,0:T(8,128)(2,1)} %add_convert_fusion.4), channel_id=1, source_target_pairs={{0,4},{4,0},{1,5},{5,1},{2,6},{6,2},{3,7},{7,3},{8,12},{12,8},{9,1... | collective-permute-start | bytes 2359304 | tf_op jit(solution)/shard_map/ppermute | solution.py:29
  269.1 28.0 %collective-permute-start.34 = (bf16[384,768]{1,0:T(8,128)(2,1)}, bf16[384,768]{1,0:T(8,128)(2,1)}, u32[]{:S(2)}, u32[]{:S(2)}) collective-permute-start(bf16[384,768]{1,0:T(8,128)(2,1)} %constant_dynamic-slice_fusion.2), channel_id=1, source_target_pairs={{0,4},{4,0},{1,5},{5,1},{2,6},{6,2},{3,7},{7,3},{8,12},{12,8},{9,1... | collective-permute-start | bytes 1769480 | tf_op jit(solution)/shard_map/ppermute | solution.py:799
  284.8 29.1 %collective-permute-start.25 = (bf16[192,2048]{1,0:T(8,128)(2,1)}, bf16[192,2048]{1,0:T(8,128)(2,1)}, u32[]{:S(2)}, u32[]{:S(2)}) collective-permute-start(bf16[192,2048]{1,0:T(8,128)(2,1)} %constant_dynamic-slice_fusion.5), channel_id=1, source_target_pairs={{0,4},{4,0},{1,5},{5,1},{2,6},{6,2},{3,7},{7,3},{8,12},{12,8},{9,1... | collective-permute-start | bytes 2359304 | tf_op jit(solution)/shard_map/ppermute | solution.py:799
  298.5 18.3 %collective-permute-start.35 = (bf16[192,768]{1,0:T(8,128)(2,1)S(1)}, bf16[192,768]{1,0:T(8,128)(2,1)S(1)}, u32[]{:S(2)}, u32[]{:S(2)}) collective-permute-start(bf16[192,768]{1,0:T(8,128)(2,1)S(1)} %constant_dynamic-slice_fusion.1), channel_id=1, source_target_pairs={{0,8},{8,0},{16,24},{24,16},{1,9},{9,1},{17,25},{25,17},{2,10},{10... | collective-permute-start | bytes 884744 | tf_op jit(solution)/shard_map/ppermute | solution.py:799
  315.4 28.3 %collective-permute-start.26 = (bf16[96,2048]{1,0:T(8,128)(2,1)S(1)}, bf16[96,2048]{1,0:T(8,128)(2,1)S(1)}, u32[]{:S(2)}, u32[]{:S(2)}) collective-permute-start(bf16[96,2048]{1,0:T(8,128)(2,1)S(1)} %constant_dynamic-slice_fusion.4), channel_id=1, source_target_pairs={{0,8},{8,0},{16,24},{24,16},{1,9},{9,1},{17,25},{25,17},{2,10},{10... | collective-permute-start | bytes 1179656 | tf_op jit(solution)/shard_map/ppermute | solution.py:799
  315.6 42.4 %collective-permute-start.20 = (bf16[208,576]{1,0:T(8,128)(2,1)S(1)}, bf16[208,576]{1,0:T(8,128)(2,1)S(1)}, u32[]{:S(2)}, u32[]{:S(2)}) collective-permute-start(bf16[208,576]{1,0:T(8,128)(2,1)S(1)} %add_convert_fusion.10), channel_id=1, source_target_pairs={{0,4},{4,0},{1,5},{5,1},{2,6},{6,2},{3,7},{7,3},{8,12},{12,8},{9,1... | collective-permute-start | bytes 718856 | tf_op jit(solution)/shard_map/ppermute | solution.py:29
  316.9 27.0 %collective-permute-start.36 = (bf16[96,768]{1,0:T(8,128)(2,1)S(1)}, bf16[96,768]{1,0:T(8,128)(2,1)S(1)}, u32[]{:S(2)}, u32[]{:S(2)}) collective-permute-start(bf16[96,768]{1,0:T(8,128)(2,1)S(1)} %constant_dynamic-slice_fusion), channel_id=1, source_target_pairs={{0,16},{16,0},{8,24},{24,8},{1,17},{17,1},{9,25},{25,9},{2,18},{18... | collective-permute-start | bytes 442376 | tf_op jit(solution)/shard_map/ppermute | solution.py:799
  344.0 20.1 %collective-permute-start.37 = (bf16[96,768]{1,0:T(8,128)(2,1)S(1)}, bf16[96,768]{1,0:T(8,128)(2,1)S(1)}, u32[]{:S(2)}, u32[]{:S(2)}) collective-permute-start(bf16[96,768]{1,0:T(8,128)(2,1)S(1)} %add_convert_fusion.12), channel_id=1, source_target_pairs={{0,16},{16,0},{8,24},{24,8},{1,17},{17,1},{9,25},{25,9},{2,18},{18... | collective-permute-start | bytes 442376 | tf_op jit(solution)/shard_map/ppermute | solution.py:803
  364.2 23.3 %collective-permute-start.38 = (bf16[192,768]{1,0:T(8,128)(2,1)S(1)}, bf16[192,768]{1,0:T(8,128)(2,1)S(1)}, u32[]{:S(2)}, u32[]{:S(2)}) collective-permute-start(bf16[192,768]{1,0:T(8,128)(2,1)S(1)} %maximum_select_fusion.6), channel_id=1, source_target_pairs={{0,8},{8,0},{16,24},{24,16},{1,9},{9,1},{17,25},{25,17},{2,10},{10... | collective-permute-start | bytes 884744 | tf_op jit(solution)/shard_map/ppermute | solution.py:803
  369.6 26.3 %collective-permute-start.29 = (bf16[96,2048]{1,0:T(8,128)(2,1)S(1)}, bf16[96,2048]{1,0:T(8,128)(2,1)S(1)}, u32[]{:S(2)}, u32[]{:S(2)}) collective-permute-start(bf16[96,2048]{1,0:T(8,128)(2,1)S(1)} %maximum_select_fusion.5), channel_id=1, source_target_pairs={{0,8},{8,0},{16,24},{24,16},{1,9},{9,1},{17,25},{25,17},{2,10},{10... | collective-permute-start | bytes 1179656 | tf_op jit(solution)/shard_map/ppermute | solution.py:803
  369.9 27.5 %collective-permute-start.22 = (bf16[2,208,576]{2,1,0:T(8,128)(2,1)S(1)}, bf16[2,208,576]{2,1,0:T(8,128)(2,1)S(1)}, u32[]{:S(2)}, u32[]{:S(2)}) collective-permute-start(bf16[2,208,576]{2,1,0:T(8,128)(2,1)S(1)} %maximum_select_fusion.4), channel_id=1, source_target_pairs={{0,16},{16,0},{8,24},{24,8},{1,17},{17,1},{9,25},{25,9},{2,18},{18... | collective-permute-start | bytes 1437704 | tf_op jit(solution)/shard_map/ppermute | solution.py:803
  396.1 19.8 %collective-permute-start.30 = (bf16[192,2048]{1,0:T(8,128)(2,1)S(1)}, bf16[192,2048]{1,0:T(8,128)(2,1)}, u32[]{:S(2)}, u32[]{:S(2)}) collective-permute-start(bf16[192,2048]{1,0:T(8,128)(2,1)S(1)} %maximum_select_fusion.2.refs_0_), channel_id=1, source_target_pairs={{0,4},{4,0},{1,5},{5,1},{2,6},{6,2},{3,7},{7,3},{8,12},{12,8},{9,1... | collective-permute-start | bytes 2359304 | tf_op jit(solution)/shard_map/ppermute | solution.py:29
  397.6 27.2 %collective-permute-start.23 = (bf16[4,208,576]{2,1,0:T(8,128)(2,1)S(1)}, bf16[4,208,576]{2,1,0:T(8,128)(2,1)}, u32[]{:S(2)}, u32[]{:S(2)}) collective-permute-start(bf16[4,208,576]{2,1,0:T(8,128)(2,1)S(1)} %maximum_select_fusion.own_ref), channel_id=1, source_target_pairs={{0,2},{2,0},{1,3},{3,1},{4,6},{6,4},{5,7},{7,5},{8,10},{10,8},{9,1... | collective-permute-start | bytes 2875400 | tf_op jit(solution)/shard_map/ppermute | solution.py:29
  400.0 20.5 %collective-permute-start.40 = (bf16[384,768]{1,0:T(8,128)(2,1)S(1)}, bf16[384,768]{1,0:T(8,128)(2,1)}, u32[]{:S(2)}, u32[]{:S(2)}) collective-permute-start(bf16[384,768]{1,0:T(8,128)(2,1)S(1)} %maximum_select_fusion.3.refs_0_), channel_id=1, source_target_pairs={{0,2},{2,0},{1,3},{3,1},{4,6},{6,4},{5,7},{7,5},{8,10},{10,8},{9,1... | collective-permute-start | bytes 1769480 | tf_op jit(solution)/shard_map/ppermute | solution.py:29
  400.1 20.4 %collective-permute-start.41 = (bf16[384,768]{1,0:T(8,128)(2,1)S(1)}, bf16[384,768]{1,0:T(8,128)(2,1)}, u32[]{:S(2)}, u32[]{:S(2)}) collective-permute-start(bf16[384,768]{1,0:T(8,128)(2,1)S(1)} %collective-permute-done.39.refs_1_), channel_id=1, source_target_pairs={{0,2},{2,0},{1,3},{3,1},{4,6},{6,4},{5,7},{7,5},{8,10},{10,8},{9,1... | collective-permute-start | bytes 1769480 | tf_op jit(solution)/shard_map/ppermute | solution.py:29
  407.6 24.7 %collective-permute-start.31 = (bf16[192,2048]{1,0:T(8,128)(2,1)S(1)}, bf16[192,2048]{1,0:T(8,128)(2,1)}, u32[]{:S(2)}, u32[]{:S(2)}) collective-permute-start(bf16[192,2048]{1,0:T(8,128)(2,1)S(1)} %maximum_select_fusion.2.refs_0_), channel_id=1, source_target_pairs={{0,2},{2,0},{1,3},{3,1},{4,6},{6,4},{5,7},{7,5},{8,10},{10,8},{9,1... | collective-permute-start | bytes 2359304 | tf_op jit(solution)/shard_map/ppermute | solution.py:29
  (61 other events, 395.6 us)
Sparse Core Ops, SparseCore 0:
  10.3 39.0 all-gather.1
  295.7 48.4 reduce-scatter.1

commit v3 on v2

v3 whole, which is shorter than its diff:
```python
from functools import partial

import jax
import jax.numpy as jnp
from jax import lax
from jax.experimental import pallas as pl
from jax.experimental.pallas import tpu as pltpu
from jax.sharding import Mesh, PartitionSpec as P

HEADS = 12
ZS = 4
NEG_FILL = -1e30
SWAP = ((0, 1), (1, 0))
F32 = jnp.float32
BF16 = jnp.bfloat16


def matmul(left_side, right_side):
    return jnp.dot(left_side, right_side, preferred_element_type=F32)


def right_trans(left_side, right_side):
    return lax.dot_general(
        left_side, right_side, (((1,), (1,)), ((), ())), preferred_element_type=F32
    )


def work(units):
    return pl.CostEstimate(flops=int(units * 1e3), bytes_accessed=1, transcendentals=0)


def swap(value, axis):
    return lax.ppermute(value, axis, SWAP)


def touched_groups(length, rows, outer):
    group = 4 * rows
    left = length - outer * (ZS * group)
    return jnp.clip((left + group - 1) // group, 0, ZS)


def with_mask(kv, place, length):
    at = place + lax.broadcasted_iota(jnp.int32, kv.shape, 0)
    lane = lax.broadcasted_iota(jnp.int32, kv.shape, 1)
    fill = jnp.where(at < length, 0.0, jnp.where(lane == 0, NEG_FILL, 0.0))
    return jnp.concatenate([kv, fill.astype(BF16)], axis=1)


def forward_kernel(meta_ref, q_ref, *refs, blocks, rows):
    kv_refs = refs[:blocks]
    out_ref = refs[blocks]
    piece_refs = refs[blocks + 1 : blocks + 1 + ZS]
    log_ref = refs[blocks + 1 + ZS]
    value_refs = refs[blocks + 2 + ZS : 2 * blocks + 2 + ZS]
    low_ref = refs[-1]
    head_dim, query_count = q_ref.shape
    length, z_at = meta_ref[0], meta_ref[1]
    for block in range(blocks):
        for part in range(ZS):
            cut = slice(part * rows, (part + 1) * rows)
            value_refs[block][:, cut] = kv_refs[block][cut, :].T[head_dim:, :]
    query = jnp.concatenate(
        [
            q_ref[...],
            jnp.zeros((head_dim, query_count), BF16),
            jnp.ones((128, query_count), BF16),
        ],
        axis=0,
    )

    def step(group, carry, members):
        top, total, acc = carry
        start = pl.multiple_of(group * rows, rows)
        found = []
        for block in members:
            place = (meta_ref[2 + block] + group * 4) * rows
            kv = with_mask(kv_refs[block][pl.ds(start, rows), :], place, length)
            found.append(matmul(kv, query))
        new_top = top
        for scores in found:
            new_top = jnp.maximum(new_top, jnp.max(scores, axis=0, keepdims=True))
        fade = jnp.exp(top - new_top)
        total = total * fade
        acc = acc * fade
        for block, scores in zip(members, found):
            weights = jnp.exp(scores - new_top)
            total = total + jnp.sum(weights, axis=0, keepdims=True)
            acc = acc + matmul(
                value_refs[block][:, pl.ds(start, rows)], weights.astype(BF16)
            )
        return new_top, total, acc

    carry = (
        jnp.full((1, query_count), NEG_FILL, F32),
        jnp.zeros((1, query_count), F32),
        jnp.zeros((head_dim, query_count), F32),
    )
    for first in range(0, blocks, 4):
        members = tuple(range(first, first + 4))
        count = touched_groups(length, rows, meta_ref[2 + first] // 16)
        carry = lax.fori_loop(0, count, lambda g, c: step(g, c, members), carry)
    top, total, acc = carry
    out = acc * (1.0 / total)
    out_ref[...] = out
    low_ref[...] = out.astype(BF16)
    size = query_count // ZS
    for at in range(ZS):
        start = pl.multiple_of((z_at ^ at) * size, 128)
        piece_refs[at][...] = low_ref[:, pl.ds(start, size)]
    log_ref[0] = top + jnp.log(total)


def attend_forward(meta, queries, kv_blocks, first, head_dim):
    blocks = len(kv_blocks)
    block_rows, columns = kv_blocks[0].shape
    heads = columns // 128
    query_count = queries.shape[1]
    size = query_count // ZS
    head_rows = pl.BlockSpec((head_dim, query_count), lambda i, m: (i, 0))
    return pl.pallas_call(
        partial(forward_kernel, blocks=blocks, rows=block_rows // ZS),
        grid_spec=pltpu.PrefetchScalarGridSpec(
            num_scalar_prefetch=1,
            grid=(heads,),
            in_specs=[pl.BlockSpec((head_dim, query_count), lambda i, m: (i + first, 0))]
            + [pl.BlockSpec((block_rows, 128), lambda i, m: (0, i))] * blocks,
            out_specs=[head_rows]
            + [pl.BlockSpec((head_dim, size), lambda i, m: (i, 0))] * ZS
            + [pl.BlockSpec((1, 1, query_count), lambda i, m: (i, 0, 0))],
            scratch_shapes=[pltpu.VMEM((head_dim, block_rows), BF16)] * blocks
            + [pltpu.VMEM((head_dim, query_count), BF16)],
        ),
        out_shape=[jax.ShapeDtypeStruct((heads * head_dim, query_count), F32)]
        + [jax.ShapeDtypeStruct((heads * head_dim, size), BF16)] * ZS
        + [jax.ShapeDtypeStruct((heads, 1, query_count), F32)],
        compiler_params=pltpu.CompilerParams(vmem_limit_bytes=40 << 20),
        cost_estimate=work(8 * heads),
        name="attend_forward",
    )(meta, queries, *kv_blocks)


def backward_kernel(meta_ref, q_ref, out_ref, log_ref, *refs, blocks, rows):
    piece_refs = refs[:ZS]
    kv_refs = refs[ZS : ZS + blocks]
    refs = refs[ZS + blocks :]
    dq_ref = refs[0]
    pairs = refs[1 : 1 + blocks // 2]
    key_refs = refs[1 + blocks // 2 : 1 + blocks // 2 + blocks]
    go_ref, qn_ref, gn_ref, acc_ref = refs[1 + blocks // 2 + blocks :]
    head_dim, query_count = q_ref.shape
    length, z_at = meta_ref[0], meta_ref[1]
    block_rows = ZS * rows
    size = query_count // ZS
    for at in range(ZS):
        start = pl.multiple_of((z_at ^ at) * size, 128)
        go_ref[:, pl.ds(start, size)] = piece_refs[at][...]
    blank = jnp.zeros((head_dim, query_count), BF16)
    for block in range(blocks):
        for part in range(ZS):
            cut = slice(part * rows, (part + 1) * rows)
            key_refs[block][:, cut] = kv_refs[block][cut, :].T[:head_dim, :]
    grads = go_ref[...]
    query = jnp.concatenate([q_ref[...], blank], axis=0)
    grad = jnp.concatenate([blank, grads], axis=0)
    qn_ref[...] = query.T
    gn_ref[...] = grad.T
    query = jnp.concatenate([query, jnp.ones((128, query_count), BF16)], axis=0)
    delta = jnp.sum(grads.astype(F32) * out_ref[...], axis=0, keepdims=True)
    log_sum = log_ref[0]
    acc_ref[...] = jnp.zeros_like(acc_ref)

    def step(group, members):
        start = pl.multiple_of(group * rows, rows)
        for block in members:
            kv = kv_refs[block][pl.ds(start, rows), :]
            place = (meta_ref[2 + block] + group * 4) * rows
            scores = matmul(with_mask(kv, place, length), query)
            prob_grad = matmul(kv, grad)
            prob = jnp.exp(scores - log_sum)
            score_grad = (prob * (prob_grad - delta)).astype(BF16)
            pairs[block // 2][pl.ds(start + (block & 1) * block_rows, rows), :] = (
                matmul(prob.astype(BF16), gn_ref[...]) + matmul(score_grad, qn_ref[...])
            ).astype(BF16)
            acc_ref[...] += matmul(key_refs[block][:, pl.ds(start, rows)], score_grad)

    def clear(group, members):
        start = pl.multiple_of(group * rows, rows)
        for block in members:
            pairs[block // 2][pl.ds(start + (block & 1) * block_rows, rows), :] = jnp.zeros(
                (rows, 128), BF16
            )

    def loop(low, high, fn):
        def one(group, carry):
            fn(group)
            return carry

        lax.fori_loop(low, high, one, 0)

    for first in range(0, blocks, 4):
        members = tuple(range(first, first + 4))
        count = touched_groups(length, rows, meta_ref[2 + first] // 16)
        loop(0, count, lambda g: step(g, members))
        loop(count, ZS, lambda g: clear(g, members))
    dq_ref[...] = (acc_ref[...] * head_dim ** (-0.5)).astype(BF16)


def attend_backward(meta, queries, grads, out, log_sum, kv_blocks, first, head_dim):
    blocks = len(kv_blocks)
    block_rows, columns = kv_blocks[0].shape
    heads = columns // 128
    query_count = queries.shape[1]
    size = query_count // ZS
    head_rows = pl.BlockSpec((head_dim, query_count), lambda i, m: (i, 0))
    return pl.pallas_call(
        partial(backward_kernel, blocks=blocks, rows=block_rows // ZS),
        grid_spec=pltpu.PrefetchScalarGridSpec(
            num_scalar_prefetch=1,
            grid=(heads,),
            in_specs=[
                pl.BlockSpec((head_dim, query_count), lambda i, m: (i + first, 0)),
                head_rows,
                pl.BlockSpec((1, 1, query_count), lambda i, m: (i, 0, 0)),
            ]
            + [pl.BlockSpec((head_dim, size), lambda i, m: (i + first, 0))] * ZS
            + [pl.BlockSpec((block_rows, 128), lambda i, m: (0, i))] * blocks,
            out_specs=[head_rows]
            + [pl.BlockSpec((2 * block_rows, 128), lambda i, m: (0, i))] * (blocks // 2),
            scratch_shapes=[pltpu.VMEM((head_dim, block_rows), BF16)] * blocks
            + [
                pltpu.VMEM((head_dim, query_count), BF16),
                pltpu.VMEM((query_count, 128), BF16),
                pltpu.VMEM((query_count, 128), BF16),
                pltpu.VMEM((head_dim, query_count), F32),
            ],
        ),
        out_shape=[jax.ShapeDtypeStruct((heads * head_dim, query_count), BF16)]
        + [jax.ShapeDtypeStruct((2 * block_rows, columns), BF16)] * (blocks // 2),
        compiler_params=pltpu.CompilerParams(vmem_limit_bytes=48 << 20),
        cost_estimate=work(12 * heads),
        name="attend_backward",
    )(meta, queries, out, log_sum, *grads, *kv_blocks)


def project_kernel(tokens_ref, weight_ref, bias_ref, query_ref, *refs):
    kv_refs, turned_ref = refs[:-1], refs[-1]
    part = query_ref.shape[0]
    tokens = tokens_ref[...]
    split = 2 * part
    kv = matmul(tokens, weight_ref[:, :split]) + bias_ref[:, :split]
    kv = kv.astype(BF16)
    low = 0
    for ref in kv_refs:
        ref[...] = kv[:, low : low + ref.shape[1]]
        low += ref.shape[1]
    query = matmul(tokens, weight_ref[:, split:]) + bias_ref[:, split:]
    scale = (part * ZS // HEADS) ** (-0.5)
    query_ref[...] = (query.astype(BF16) * jnp.array(scale, BF16)).T
    turned_ref[...] = tokens.T


def project(tokens, weight, bias, counts):
    rows, width = tokens.shape
    part = weight.shape[1] // 3
    return pl.pallas_call(
        project_kernel,
        out_shape=[jax.ShapeDtypeStruct((part, rows), BF16)]
        + [jax.ShapeDtypeStruct((rows, 128 * count), BF16) for count in counts]
        + [jax.ShapeDtypeStruct((width, rows), BF16)],
        compiler_params=pltpu.CompilerParams(vmem_limit_bytes=40 << 20),
        cost_estimate=work(2),
        name="project",
    )(tokens, weight, bias)


def middle_kernel(meta_ref, tokens_ref, seed_ref, vec_ref, upoff_ref, *refs, groups, shared):
    mixed_refs = [refs[at * ZS : (at + 1) * ZS] for at in range(len(groups))]
    refs = refs[ZS * len(groups) :]
    weight_refs = refs[: 5 if shared else 3]
    refs = refs[len(weight_refs) :]
    outputs_ref, resid_ref = refs[:2]
    mgrad_refs = refs[2 : 2 + ZS]
    (
        send_ref,
        keep_ref,
        small_ref,
        out_w,
        up_w,
        down_w,
        slope_ref,
        wide_ref,
        tall_ref,
        sems,
    ) = refs[2 + ZS :]
    w_at, core, z_at = meta_ref[1], meta_ref[2], meta_ref[3]
    moves = [[], [], []]
    if shared:
        outs, ups, downs, got, pair = weight_refs
        count_o, count_u, count_d = outs.shape[0], ups.shape[0], downs.shape[0]
        for kind, (source, target) in enumerate(((outs, out_w), (ups, up_w), (downs, down_w))):
            start = pl.multiple_of(w_at * source.shape[0], source.shape[0])
            moves[kind].append((source, target.at[pl.ds(start, source.shape[0]), :]))
        lanes = got.shape[1]
        for source, which in ((got, core), (pair, 1 - core)):
            half = count_o // 2
            start = pl.multiple_of(((1 - w_at) * 2 + which) * half, half)
            moves[0].append((source.at[pl.ds(0, half), :], out_w.at[pl.ds(start, half), :]))
            low = half
            start = pl.multiple_of((1 - w_at) * count_u, count_u)
            for block in range(up_w.shape[1] // 2 // lanes):
                lane = pl.multiple_of(which * (up_w.shape[1] // 2) + block * lanes, 128)
                moves[1].append(
                    (
                        source.at[pl.ds(low, count_u), :],
                        up_w.at[pl.ds(start, count_u), pl.ds(lane, lanes)],
                    )
                )
                low += count_u
            half = count_d // 2
            start = pl.multiple_of(((1 - w_at) * 2 + which) * half, half)
            moves[2].append((source.at[pl.ds(low, half), :], down_w.at[pl.ds(start, half), :]))
    else:
        for kind, pair in enumerate(zip(weight_refs, (out_w, up_w, down_w))):
            moves[kind].append(pair)
    copies = []
    at = 0
    for kind in range(3):
        made = []
        for source, target in moves[kind]:
            made.append(pltpu.make_async_copy(source, target, sems.at[at]))
            made[-1].start()
            at += 1
        copies.append(made)
    rows, width = tokens_ref.shape
    hidden = upoff_ref.shape[1]
    part = width // ZS
    head_dim = width // HEADS
    quarter = hidden // 4

    def mean(value):
        return jnp.mean(value, axis=-1, keepdims=True)

    def norm(value):
        centered = value - mean(value)
        scale = lax.rsqrt(mean(centered * centered) + 1e-12)
        return centered * scale, scale

    def norm_back(grad, normal, scale):
        return scale * (grad - mean(grad) - normal * mean(grad * normal))

    def column(value):
        return jnp.sum(value, axis=0, keepdims=True)

    normed_at = 2 * quarter
    mixed_at = normed_at + width
    branch_at = mixed_at + width
    act_at = 5 * quarter
    for (first, count), pieces in zip(groups, mixed_refs):
        size = count * head_dim
        for at in range(ZS):
            low = mixed_at + (z_at ^ at) * part + first * head_dim
            send_ref[pl.ds(pl.multiple_of(low, head_dim), size), :] = pieces[at][...]
    mixed = send_ref[mixed_at:branch_at, :].T
    for copy in copies[0]:
        copy.wait()
    first_n, first_r = norm(tokens_ref[...] + (matmul(mixed, out_w[...]) + vec_ref[2:3, :]))
    normed = first_n * vec_ref[3:4, :] + vec_ref[4:5, :]
    low = normed.astype(BF16)
    send_ref[normed_at:mixed_at, :] = low.T
    for copy in copies[1] + copies[2]:
        copy.wait()
    quarters = []
    for half in range(2):
        for kept in (False, True):
            at = half * 2 * quarter + (core if kept else 1 - core) * quarter
            quarters.append((half, kept, pl.multiple_of(at, quarter)))
    acc = None
    for at, (half, kept, start) in enumerate(quarters):
        cut = pl.ds(start, quarter)
        pre_act = matmul(low, up_w[:, cut]) + upoff_ref[:, cut]
        phi = 0.5 + 0.5 * lax.erf(pre_act * (0.5**0.5))
        act = (pre_act * phi).astype(BF16)
        slope_ref[:, at * quarter : (at + 1) * quarter] = phi + pre_act * (
            jnp.exp(-0.5 * pre_act * pre_act) * 0.3989422804014327
        )
        target, base = (keep_ref, 0) if kept else (send_ref, act_at)
        target[base + half * quarter : base + (half + 1) * quarter, :] = act.T
        term = matmul(act, down_w[cut, :])
        acc = term if acc is None else acc + term
    second_n, second_r = norm(normed + (acc + vec_ref[5:6, :]))
    outputs_ref[...] = second_n * vec_ref[6:7, :] + vec_ref[7:8, :]
    place = lax.broadcasted_iota(jnp.int32, (rows, 1), 0)
    seed = jnp.where(place < meta_ref[0], seed_ref[...], 0.0)
    sum_grad = norm_back(seed * vec_ref[6:7, :], second_n, second_r)
    ffn = sum_grad.astype(BF16)
    for at in range(width // 256):
        low_row = act_at + 2 * quarter + at * rows
        send_ref[low_row : low_row + rows, :] = ffn[:, at * 256 : (at + 1) * 256]
    small_ref[3:4, :] = column(ffn.astype(F32))
    small_ref[4:5, :] = column(seed * second_n)
    small_ref[5:6, :] = column(seed)
    acc = sum_grad
    for at, (half, kept, start) in enumerate(quarters):
        cut = pl.ds(start, quarter)
        pre = right_trans(ffn, down_w[cut, :]) * slope_ref[:, at * quarter : (at + 1) * quarter]
        pre = pre.astype(BF16)
        target, base = (keep_ref, 2 * quarter) if kept else (send_ref, 0)
        for block in range(quarter // 256):
            row = base + (half * (quarter // 256) + block) * rows
            target[row : row + rows, :] = pre[:, block * 256 : (block + 1) * 256]
        sums = column(pre.astype(F32))
        line = 8 + half * (2 * quarter // width) + (core if kept else 1 - core)
        small_ref[pl.ds(line, 1), :] = sums
        acc = acc + right_trans(pre, up_w[:, cut])
    small_ref[1:2, :] = column(acc * first_n)
    small_ref[2:3, :] = column(acc)
    resid = norm_back(acc * vec_ref[3:4, :], first_n, first_r)
    resid_ref[...] = resid
    branch = resid.astype(BF16)
    wide_ref[...] = branch
    side = width // 2
    for target, base, which in (
        (send_ref, branch_at, 1 - core),
        (keep_ref, 4 * quarter, core),
    ):
        values = wide_ref[:, pl.ds(pl.multiple_of(which * side, 128), side)]
        target[base : base + rows, :] = values[:, :256]
        target[base + rows : base + 2 * rows, : side - 256] = values[:, 256:]
        target[base + rows : base + 2 * rows, side - 256 :] = jnp.zeros(
            (rows, 512 - side), BF16
        )
    small_ref[0:1, :] = column(branch.astype(F32))
    small_ref[6:8, :] = jnp.zeros((2, width), F32)
    small_ref[12:16, :] = jnp.zeros((4, width), F32)
    gap = branch_at + 2 * rows
    send_ref[gap:act_at, :] = jnp.zeros((act_at - gap, 256), BF16)
    tall_ref[...] = right_trans(out_w[...], branch).astype(BF16)
    for at in range(ZS):
        start = pl.multiple_of((z_at ^ at) * part, part)
        mgrad_refs[at][...] = tall_ref[pl.ds(start, part), :]


def middle(meta, mixed, groups, tokens, seed, vec, upoff, weights):
    rows, width = tokens.shape
    hidden = upoff.shape[1]
    in_vmem = pl.BlockSpec(memory_space=pltpu.VMEM)
    in_place = pl.BlockSpec(memory_space=pl.ANY)
    flat = [item for group in mixed for item in group]
    part = jax.ShapeDtypeStruct((width // ZS, rows), BF16)
    return pl.pallas_call(
        partial(middle_kernel, groups=groups, shared=len(weights) == 5),
        grid_spec=pltpu.PrefetchScalarGridSpec(
            num_scalar_prefetch=1,
            grid=(),
            in_specs=[in_vmem] * (4 + len(flat)) + [in_place] * len(weights),
            out_specs=[in_vmem] * (5 + ZS),
            scratch_shapes=[
                pltpu.VMEM((width, width), BF16),
                pltpu.VMEM((width, hidden), BF16),
                pltpu.VMEM((hidden, width), BF16),
                pltpu.VMEM((rows, hidden), F32),
                pltpu.VMEM((rows, width), BF16),
                pltpu.VMEM((width, rows), BF16),
                pltpu.SemaphoreType.DMA((11,)),
            ],
        ),
        out_shape=[jax.ShapeDtypeStruct((rows, width), F32)] * 2
        + [part] * ZS
        + [
            jax.ShapeDtypeStruct((2 * hidden, 256), BF16),
            jax.ShapeDtypeStruct((hidden + 2 * rows, 256), BF16),
            jax.ShapeDtypeStruct((16, width), F32),
        ],
        compiler_params=pltpu.CompilerParams(vmem_limit_bytes=56 << 20),
        cost_estimate=work(15),
        name="middle",
    )(meta, tokens, seed, vec, upoff, *flat, *weights)


def down_kernel(meta_ref, keep_ref, got_ref, own_ffn_ref, got_ffn_ref, out_ref):
    keep, got = keep_ref[...], got_ref[...]
    rows = keep.shape[1]
    for at in range(out_ref.shape[1] // 256):
        cut = slice(at * rows, (at + 1) * rows)
        value = matmul(keep, own_ffn_ref[cut, :]) + matmul(got, got_ffn_ref[cut, :])
        out_ref[:, at * 256 : (at + 1) * 256] = value.astype(BF16)


def down_slab(meta, keep, send, got):
    block = send.shape[0] // 8
    kept = pl.BlockSpec((block, send.shape[1]), lambda i, m: (m[0], 0))
    act = pl.BlockSpec((block, send.shape[1]), lambda i, m: (5 + m[0], 0))
    ffn = pl.BlockSpec((block, send.shape[1]), lambda i, m: (7, 0))
    return pl.pallas_call(
        down_kernel,
        grid_spec=pltpu.PrefetchScalarGridSpec(
            num_scalar_prefetch=1,
            grid=(1,),
            in_specs=[kept, act, ffn, ffn],
            out_specs=pl.BlockSpec((block, block), lambda i, m: (0, 0)),
        ),
        out_shape=jax.ShapeDtypeStruct((block, block), BF16),
        compiler_params=pltpu.CompilerParams(vmem_limit_bytes=24 << 20),
        cost_estimate=work(2),
        name="down_slab",
    )(meta, keep, got, send, got)


def up_kernel(meta_ref, keep_ref, send_ref, got_ref, own_small_ref, got_small_ref, *refs):
    out_refs, table_ref = refs[:2], refs[2]
    rows = send_ref.shape[1]
    width = own_small_ref.shape[1]
    block = width // 4
    side = width // 2
    normed_at = 2 * width
    branch_at = normed_at + 2 * width
    x_at = meta_ref[0]
    pre_keep = 2 * width
    for w in range(2):
        small = own_small_ref[...] + got_small_ref[...]
        table_ref[...] = jnp.zeros_like(table_ref)
        for at in range(side // 128):
            low = w * side + at * 128
            table_ref[at * 8 : (at + 1) * 8, :] = small[:8, low : low + 128]
        base = side // 128 * 8
        for at in range(2 * width // 128):
            line = 8 + 2 * w + at // (width // 128)
            low = at % (width // 128) * 128
            table_ref[base + at : base + at + 1, :] = small[line : line + 1, low : low + 128]
        for out_ref, which in zip(out_refs, (1 - x_at, x_at)):
            start = pl.multiple_of(which * block, block)
            target = slice(w * block, (w + 1) * block)
            own = send_ref[pl.ds(normed_at + w * side + start, block), :]
            got = got_ref[pl.ds(normed_at + w * side + start, block), :]
            for at in range(normed_at // rows):
                cut = slice(at * rows, (at + 1) * rows)
                value = matmul(own, keep_ref[pre_keep + at * rows : pre_keep + (at + 1) * rows, :])
                value = value + matmul(got, got_ref[cut, :])
                out_ref[target, at * 256 : (at + 1) * 256] = value.astype(BF16)
            own = send_ref[pl.ds(normed_at + width + w * side + start, block), :]
            got = got_ref[pl.ds(normed_at + width + w * side + start, block), :]
            lane = normed_at // rows * 256
            for at in range(2):
                mine = 4 * width + at * rows
                theirs = branch_at + at * rows
                value = matmul(own, keep_ref[mine : mine + rows, :])
                value = value + matmul(got, got_ref[theirs : theirs + rows, :])
                value = value[:, : min(256, side - at * 256)].astype(BF16)
                out_ref[target, lane : lane + value.shape[1]] = value
                lane += value.shape[1]
            out_ref[target, lane : lane + 128] = table_ref[pl.ds(start, block), :].astype(BF16)


def up_slabs(meta, keep, send, got, own_small, got_small):
    width = own_small.shape[1]
    columns = 2 * width + width // 2 + 128
    first = pl.BlockSpec((5 * width, send.shape[1]), lambda i, m: (0, 0))

    def whole(value):
        return pl.BlockSpec(value.shape, lambda i, m: (0, 0))

    return pl.pallas_call(
        up_kernel,
        grid_spec=pltpu.PrefetchScalarGridSpec(
            num_scalar_prefetch=1,
            grid=(1,),
            in_specs=[whole(keep), first, first, whole(own_small), whole(own_small)],
            out_specs=[pl.BlockSpec((width // 2, columns), lambda i, m: (0, 0))] * 2,
            scratch_shapes=[pltpu.VMEM((width // 2, 128), F32)],
        ),
        out_shape=[jax.ShapeDtypeStruct((width // 2, columns), BF16)] * 2,
        compiler_params=pltpu.CompilerParams(vmem_limit_bytes=40 << 20),
        cost_estimate=work(4),
        name="up_slabs",
    )(meta, keep, send, got, own_small, got_small)


def head_kernel(meta_ref, turned_ref, *refs, count):
    query_refs, kv_refs = refs[:count], refs[count : 2 * count]
    refs = refs[2 * count :]
    block = turned_ref.shape[0]
    out_ref = refs[-1]

    def put(value, rows, low):
        columns = slice(low, low + value.shape[1])
        if len(refs) == 2:
            value = value + refs[0][rows, columns].astype(F32)
        out_ref[rows, columns] = value.astype(BF16)
        return low + value.shape[1]

    query = jnp.concatenate([ref[...] for ref in query_refs], axis=0)
    turned = turned_ref[...]
    ones = jnp.ones((16, turned.shape[1]), BF16)
    for left, rows in ((turned, slice(0, block)), (ones, slice(block, block + 16))):
        low = 0
        for ref in kv_refs:
            low = put(matmul(left, ref[...]), rows, low)
        put(right_trans(left, query), rows, low)


def head_slab(meta, turned, query, kv, count, got=None):
    width, rows = turned.shape
    block = width // count
    columns = 3 * width // ZS
    whole = pl.BlockSpec((block + 16, columns), lambda i, m: (0, 0))
    return pl.pallas_call(
        partial(head_kernel, count=len(query)),
        grid_spec=pltpu.PrefetchScalarGridSpec(
            num_scalar_prefetch=1,
            grid=(1,),
            in_specs=[pl.BlockSpec((block, rows), lambda i, m: (m[0] * 2 + m[1], 0))]
            + [pl.BlockSpec(item.shape, lambda i, m: (0, 0)) for item in [*query, *kv]]
            + ([] if got is None else [whole]),
            out_specs=whole,
        ),
        out_shape=jax.ShapeDtypeStruct((block + 16, columns), BF16),
        compiler_params=pltpu.CompilerParams(vmem_limit_bytes=24 << 20),
        cost_estimate=work(2),
        name="head_slab",
    )(meta, turned, *query, *kv, *(() if got is None else (got,)))


def token_kernel(*refs, count):
    query_refs, kv_refs = refs[:count], refs[count : 2 * count]
    weight_ref, out_ref = refs[2 * count :]
    kv = jnp.concatenate([ref[...] for ref in kv_refs], axis=1)
    query = jnp.concatenate([ref[...] for ref in query_refs], axis=0).T
    split = kv.shape[1]
    out_ref[...] = (
        right_trans(kv, weight_ref[:, :split]) + right_trans(query, weight_ref[:, split:])
    ).astype(BF16)


def token_part(query, kv, weight):
    return pl.pallas_call(
        partial(token_kernel, count=len(query)),
        out_shape=jax.ShapeDtypeStruct((kv[0].shape[0], weight.shape[0]), BF16),
        compiler_params=pltpu.CompilerParams(vmem_limit_bytes=32 << 20),
        cost_estimate=work(2),
        name="token_part",
    )(*query, *kv, weight)


def down_finish_kernel(meta_ref, *refs):
    block = refs[0].shape[0]
    c_at, x_at = meta_ref[0], meta_ref[1]
    for at in range(4):
        place = (c_at ^ (at >> 1)) * 2 + (x_at ^ (at & 1))
        start = pl.multiple_of(place * block, 8)
        refs[4][pl.ds(start, block), :] = refs[at][...].astype(F32)


def down_finish(meta, pieces):
    block, width = pieces[0].shape
    in_vmem = pl.BlockSpec(memory_space=pltpu.VMEM)
    return pl.pallas_call(
        down_finish_kernel,
        grid_spec=pltpu.PrefetchScalarGridSpec(
            num_scalar_prefetch=1, grid=(), in_specs=[in_vmem] * 4, out_specs=in_vmem
        ),
        out_shape=jax.ShapeDtypeStruct((4 * block, width), F32),
        compiler_params=pltpu.CompilerParams(vmem_limit_bytes=32 << 20),
        cost_estimate=work(4),
        name="down_finish",
    )(meta, *pieces)


def up_finish_kernel(meta_ref, *refs):
    pieces = refs[:4]
    up_ref, out_ref, small_ref = refs[4:]
    block = pieces[0].shape[0]
    quarter = up_ref.shape[1] // 4
    side = out_ref.shape[1] // 2
    c_at, x_at = meta_ref[0], meta_ref[1]
    for at in range(4):
        start = pl.multiple_of((x_at ^ (at & 1)) * block, 8)
        rows = pl.ds(start, block)
        core = c_at ^ (at >> 1)
        for half in range(2):
            lanes = pl.ds(pl.multiple_of((2 * half + core) * quarter, 128), quarter)
            up_ref[rows, lanes] = pieces[at][:, half * quarter : (half + 1) * quarter].astype(F32)
        out_ref[rows, pl.ds(pl.multiple_of(core * side, 128), side)] = (
            pieces[at][:, 2 * quarter : 2 * quarter + side].astype(F32)
        )
        if at < 2:
            small_ref[rows, :] = pieces[at][:, 2 * quarter + side :].astype(F32)


def up_finish(meta, pieces, hidden, width):
    block = pieces[0].shape[0]
    in_vmem = pl.BlockSpec(memory_space=pltpu.VMEM)
    shapes = [(2 * block, hidden), (2 * block, width), (2 * block, 128)]
    return pl.pallas_call(
        up_finish_kernel,
        grid_spec=pltpu.PrefetchScalarGridSpec(
            num_scalar_prefetch=1,
            grid=(),
            in_specs=[in_vmem] * 4,
            out_specs=[in_vmem] * 3,
        ),
        out_shape=[jax.ShapeDtypeStruct(shape, F32) for shape in shapes],
        compiler_params=pltpu.CompilerParams(vmem_limit_bytes=40 << 20),
        cost_estimate=work(5),
        name="up_finish",
    )(meta, *pieces)


def head_finish_kernel(meta_ref, own_ref, got_ref, query_ref, key_ref, value_ref, bias_ref, *, part):
    block = own_ref.shape[1] - 16
    head_dim = part // 3
    for at, source in enumerate((own_ref, got_ref)):
        start = pl.multiple_of((meta_ref[0] ^ at) * block, 8)
        rows = pl.ds(start, block)
        keys, values, queries = [], [], []
        for z in range(ZS):
            item = source[(z & 1) * 2 + (z >> 1)].astype(F32)
            for head in range(3):
                low = head * 2 * head_dim
                keys.append(item[:, low : low + head_dim])
                values.append(item[:, low + head_dim : low + 2 * head_dim])
            queries.append(item[:, 2 * part :])
        key = jnp.concatenate(keys, axis=1)
        value = jnp.concatenate(values, axis=1)
        query = jnp.concatenate(queries, axis=1)
        query_ref[rows, :] = query[:block]
        key_ref[rows, :] = key[:block]
        value_ref[rows, :] = value[:block]
        if at == 0:
            bias_ref[0:8, :] = query[block : block + 8]
            bias_ref[8:16, :] = value[block : block + 8]


def head_finish(meta, own, got):
    _, block, columns = own.shape
    rows = 2 * (block - 16)
    width = ZS * columns // 3
    in_vmem = pl.BlockSpec(memory_space=pltpu.VMEM)
    return pl.pallas_call(
        partial(head_finish_kernel, part=columns // 3),
        grid_spec=pltpu.PrefetchScalarGridSpec(
            num_scalar_prefetch=1, grid=(), in_specs=[in_vmem] * 2, out_specs=[in_vmem] * 4
        ),
        out_shape=[jax.ShapeDtypeStruct((rows, width), F32)] * 3
        + [jax.ShapeDtypeStruct((16, width), F32)],
        compiler_params=pltpu.CompilerParams(vmem_limit_bytes=40 << 20),
        cost_estimate=work(4),
        name="head_finish",
    )(meta, own, got)


def in_order(index, own, other, axis):
    return jnp.where(
        index == 0,
        jnp.concatenate([own, other], axis=axis),
        jnp.concatenate([other, own], axis=axis),
    )


def part_of(value, index, count, axis):
    size = value.shape[axis] // count
    return lax.dynamic_slice_in_dim(value, index * size, size, axis)


def body(
    inputs,
    lengths,
    cotangent,
    query_weight,
    query_bias,
    key_weight,
    value_weight,
    value_bias,
    output_weight,
    output_bias,
    first_gain,
    first_shift,
    up_weight,
    up_bias,
    down_weight,
    down_bias,
    second_gain,
    second_shift,
    *,
    sizes,
):
    count_o, count_w = sizes
    w_at = lax.axis_index("w")
    z_at = lax.axis_index("z")
    c_at = lax.axis_index("c")
    x_at = lax.axis_index("x")
    o_at = lax.axis_index("o")
    tokens = inputs[0]
    local_rows, width = tokens.shape
    head_dim = width // HEADS
    heads = HEADS // ZS
    part = heads * head_dim
    length = lengths[0]

    hold = lax.optimization_barrier

    def head_slice(weight):
        return lax.dynamic_slice_in_dim(weight, z_at * part, part, 1).astype(BF16)

    low_tokens = tokens.astype(BF16)
    token_all = lax.all_gather(low_tokens, "z", axis=0, tiled=True)
    own_rows = query_weight.shape[0]
    key_own = head_slice(key_weight)
    value_own = head_slice(value_weight)
    own_kv = []
    for head in range(heads):
        cut = slice(head * head_dim, (head + 1) * head_dim)
        own_kv += [key_own[:, cut], value_own[:, cut]]
    attn_own = jnp.concatenate(own_kv + [head_slice(query_weight)], axis=1)
    small = jnp.concatenate(
        [
            item.astype(BF16)
            for item in (
                query_bias,
                value_bias,
                output_bias,
                first_gain,
                first_shift,
                down_bias,
                second_gain,
                second_shift,
                up_bias,
            )
        ]
    ).reshape(-1, 3 * part)
    attn_pack = jnp.concatenate([attn_own, small], axis=0)
    if count_w == 2:
        attn_got = swap(attn_pack, "w")
        attn_full = in_order(w_at, attn_own, attn_got[:own_rows], 0)
        small_all = in_order(w_at, small[None], attn_got[None, own_rows:], 0)
    else:
        attn_all = lax.all_gather(attn_pack, "w", axis=0, tiled=False)
        attn_full = attn_all[:, :own_rows].reshape(width, 3 * part)
        small_all = attn_all[:, own_rows:]
    small_all = small_all.astype(F32).reshape(count_w, -1, own_rows)
    vec = jnp.transpose(small_all[:, :8], (1, 0, 2)).reshape(8, width)
    up_offset = small_all[:, 8:].reshape(1, -1)
    attn_pack, output_weight, up_weight, down_weight = hold(
        (attn_pack, output_weight, up_weight, down_weight)
    )
    low_weights = [item.astype(BF16) for item in (output_weight, up_weight, down_weight)]
    low_out, low_up, low_down = low_weights
    if count_w == 2:
        up_half = part_of(low_up, c_at, 2, 1)
        weight_pack = jnp.concatenate(
            [part_of(low_out, c_at, 2, 0)]
            + [up_half[:, at : at + width] for at in range(0, up_half.shape[1], width)]
            + [part_of(low_down, c_at, 2, 0)],
            axis=0,
        )
        attn_got, weight_pack = hold((attn_got, weight_pack))
        weight_got = swap(weight_pack, "w")
    else:
        weight_got = [lax.all_gather(item, "w", axis=0, tiled=True) for item in low_weights]

    own_bias = lax.dynamic_slice_in_dim(vec[:2], z_at * part, part, 1)
    value_bias_own = own_bias[1].reshape(heads, 1, head_dim)
    kv_bias = jnp.concatenate([jnp.zeros_like(value_bias_own), value_bias_own], axis=1)
    bias_row = jnp.concatenate([kv_bias.reshape(1, 2 * part), own_bias[:1]], axis=1)
    groups = ((0, heads),)
    queries, *key_values, turned = project(
        token_all, attn_full, bias_row, [count for _, count in groups]
    )
    places = []
    for at in range(4 * count_o):
        o_of = o_at ^ (at >> 2)
        places.append(o_of * 16 + (x_at ^ (at & 1)) * 2 + (c_at ^ ((at >> 1) & 1)))
    meta = jnp.stack([length, z_at] + places).astype(jnp.int32)
    near = ((0, 1), (1, 0), (2, 3), (3, 2))
    far = ((0, 2), (2, 0), (1, 3), (3, 1))
    cross = ((0, 3), (3, 0), (1, 2), (2, 1))

    def exchange(pieces):
        return [pieces[0]] + [
            lax.ppermute(item, "z", perm) for item, perm in zip(pieces[1:], (near, far, cross))
        ]

    kv_groups = []
    for item in key_values:
        kv_blocks = [item]
        for axis in ("x", "c", "o")[: 3 if count_o == 2 else 2]:
            kv_blocks = kv_blocks + [swap(item, axis) for item in kv_blocks]
        kv_groups.append(kv_blocks)
    attended, mixed, logs = [], [], []
    for (first, _), kv_blocks in zip(groups, kv_groups):
        out, *made = attend_forward(meta, queries, kv_blocks, first, head_dim)
        attended.append(out)
        mixed.append(exchange(made[:ZS]))
        logs.append(made[ZS])
    if count_w == 2:
        attended[0], weight_got = hold((attended[0], weight_got))
        weights = [*low_weights, weight_got, swap(weight_got, "c")]
    else:
        weights = weight_got

    split = count_w == 2 and count_o == 1
    my_index = o_at * 16 + z_at * 4 + x_at * 2 + c_at
    rest = jnp.clip(length - my_index * local_rows, 0, local_rows)
    core = c_at if split else jnp.zeros_like(c_at)
    spots = jnp.stack([rest, w_at, core, z_at]).astype(jnp.int32)
    outputs, resid_grad, *made = middle(
        spots, mixed, groups, tokens, cotangent[0], vec, up_offset, weights
    )
    head_grads = exchange(made[:ZS])
    send, keep, small_own = made[ZS:]
    hidden = up_offset.shape[1]

    def add_pair(kept, got):
        return (kept.astype(F32) + got.astype(F32)).astype(BF16)

    def unite(value, got, bit):
        return in_order(bit, value, got, 0)

    near_bit, far_bit = z_at & 1, z_at >> 1
    spot = jnp.stack([c_at, x_at]).astype(jnp.int32)
    token = [spot]

    def arrive(*values):
        token[0], *values = hold((token[0], *values))
        return values[0] if len(values) == 1 else values

    def backward(at):
        return attend_backward(
            meta,
            queries,
            head_grads,
            attended[at],
            logs[at],
            kv_groups[at],
            groups[at][0],
            head_dim,
        )

    def to_near(value):
        return lax.ppermute(value, "z", near)

    def to_far(value):
        return lax.ppermute(value, "z", far)

    def head_part(at, got=None):
        return head_slab(at, turned, [query_low], [kv_low], 2 * count_w, got)

    def pick(w, c):
        return jnp.stack([jnp.asarray(w), jnp.asarray(c)]).astype(jnp.int32)

    if split:
        got, small_got = swap(send, "c"), swap(small_own, "c")
        down_far = down_slab(pick(1 - w_at, 0), keep, send, got)
        up_sent, up_kept = up_slabs(
            jnp.stack([x_at]).astype(jnp.int32), keep, send, got, small_own, small_got
        )
        down_near = down_slab(pick(1 * w_at, 0), keep, send, got)
        down_far, up_sent, down_near, *head_grads = hold(
            (down_far, up_sent, down_near, *head_grads)
        )
        query_low, *pairs = backward(0)
        down_got, up_got, query_low, *pairs = arrive(
            swap(down_far, "w"), swap(up_sent, "x"), query_low, *pairs
        )
        pair_got = swap(pairs[1], "c")
        down_sum = add_pair(down_near, down_got)
        down_got = swap(part_of(down_sum, 1 - x_at, 2, 0), "x")
        up_sum = add_pair(up_kept, up_got).reshape(2, own_rows // 2, -1)
        up_got = swap(lax.dynamic_index_in_dim(up_sum, 1 - w_at, 0, keepdims=False), "w")
        pair_got = arrive(pair_got)
        half_rows = pair_got.shape[0] // 2
        pair_sent = add_pair(pairs[0][half_rows:], pair_got[half_rows:])
        pair_kept = add_pair(pairs[0][:half_rows], pair_got[:half_rows])
        pair_sent, pair_kept = arrive(pair_sent, pair_kept)
        pair_got = swap(pair_sent, "x")
        down_got = arrive(down_got)
        down_sum = add_pair(part_of(down_sum, x_at, 2, 0), down_got)
        down_got = to_near(part_of(down_sum, 1 - near_bit, 2, 0))
        up_got = arrive(up_got)
        up_sum = add_pair(lax.dynamic_index_in_dim(up_sum, w_at, 0, keepdims=False), up_got)
        up_got = to_near(part_of(up_sum, 1 - near_bit, 2, 0))
        down_got = arrive(down_got)
        down_sum = add_pair(part_of(down_sum, near_bit, 2, 0), down_got)
        down_got = to_far(part_of(down_sum, 1 - far_bit, 2, 0))
        up_got = arrive(up_got)
        up_sum = add_pair(part_of(up_sum, near_bit, 2, 0), up_got)
        up_got = to_far(part_of(up_sum, 1 - far_bit, 2, 0))
        down_got = arrive(down_got)
        down_sum = add_pair(part_of(down_sum, far_bit, 2, 0), down_got)
        down_got = to_far(down_sum)
        pair_got = arrive(pair_got)
        kv_low = add_pair(pair_kept, pair_got)
        token_sum = token_part([query_low], [kv_low], attn_full)
        token_grad = lax.psum_scatter(token_sum, "z", scatter_dimension=0, tiled=True)
        head_far = swap(head_part(pick(1 - w_at, 1 - c_at)), "c")
        head_near = swap(head_part(pick(1 * w_at, 1 - c_at)), "c")
        head_far = arrive(head_far)
        head_sent = swap(head_part(pick(1 - w_at, c_at), head_far), "w")
        head_near = arrive(head_near)
        head_sum = head_part(pick(1 * w_at, c_at), head_near)
        up_got = arrive(up_got)
        up_sum = add_pair(part_of(up_sum, far_bit, 2, 0), up_got)
        up_got = to_far(up_sum)
        down_got = arrive(down_got)
        down_sum = unite(down_sum, down_got, far_bit)
        down_got = to_near(down_sum)
        head_sent = arrive(head_sent)
        head_sum = add_pair(head_sum, head_sent)
        head_got = swap(head_sum, "x")
        up_got = arrive(up_got)
        up_sum = unite(up_sum, up_got, far_bit)
        up_got = to_near(up_sum)
        down_got = arrive(down_got)
        down_sum = unite(down_sum, down_got, near_bit)
        down_x = swap(down_sum, "x")
        down_c = swap(down_sum, "c")
        head_got = arrive(head_got)
        head_sum = add_pair(head_sum, head_got)
        head_got = to_far(head_sum)
        up_got = arrive(up_got)
        up_sum = unite(up_sum, up_got, near_bit)
        up_x = swap(up_sum, "x")
        up_c = swap(up_sum, "c")
        down_x = arrive(down_x)
        down_pieces = [down_sum, down_x, down_c, swap(down_x, "c")]
        head_got = arrive(head_got)
        head_two = unite(head_sum[None], head_got[None], far_bit)
        head_got = to_near(head_two)
        total_down = down_finish(spot, down_pieces)
        up_x = arrive(up_x)
        up_pieces = [up_sum, up_x, up_c, swap(up_x, "c")]
        head_got = arrive(head_got)
        head_four = unite(head_two, head_got, near_bit)
        head_other = swap(head_four, "c")
        total_up, total_out, table = up_finish(token[0], up_pieces, hidden, width)
        groups = own_rows // 128
        small_total = table[: 8 * groups].reshape(groups, 8, 128)
        vectors = [small_total[:, at].reshape(own_rows) for at in range(6)]
        lines = hidden // count_w // 128
        total_up_bias = table[8 * groups : 8 * groups + lines].reshape(-1)
    else:
        query_low, *pairs = backward(0)
        if count_o == 2:
            pairs = [add_pair(pairs[at], swap(pairs[at + 2], "o")) for at in range(2)]
        pair = add_pair(pairs[0], swap(pairs[1], "c"))
        half_rows = pair.shape[0] // 2
        kv_low = add_pair(pair[:half_rows], swap(pair[half_rows:], "x"))
        token_sum = token_part([query_low], [kv_low], attn_full)
        token_grad = lax.psum_scatter(token_sum, "z", scatter_dimension=0, tiled=True)
        got = [swap(head_part(pick(w, 1 - c_at)), "c") for w in range(count_w)]
        slabs = [head_part(pick(w, c_at), got[w]) for w in range(count_w)]
        slabs = jnp.stack(slabs)
        head_sum = lax.psum_scatter(slabs, "w", scatter_dimension=0, tiled=True)[0]
        head_sum = add_pair(head_sum, swap(head_sum, "x"))
        if count_o == 2:
            head_sum = add_pair(head_sum, swap(head_sum, "o"))
        head_two = unite(head_sum[None], to_far(head_sum)[None], far_bit)
        head_four = unite(head_two, to_near(head_two), near_bit)
        head_other = swap(head_four, "c")
        quarter = hidden // 4
        count = quarter // 256
        act_at = 5 * quarter
        act = [keep[:quarter], send[act_at : act_at + quarter], keep[quarter : 2 * quarter]]
        act += [send[act_at + quarter : act_at + 2 * quarter]]
        act = jnp.concatenate(act, axis=0)

        def rows_of(value, low, at):
            return value[low + at * local_rows : low + (at + 1) * local_rows]

        ffn_at = act_at + 2 * quarter
        ffn = jnp.concatenate([rows_of(send, ffn_at, at) for at in range(width // 256)], axis=1)
        pre = []
        for half in range(2):
            pre += [rows_of(keep, 2 * quarter, half * count + at) for at in range(count)]
            pre += [rows_of(send, 0, half * count + at) for at in range(count)]
        pre = jnp.concatenate(pre, axis=1)
        normed_turned = send[2 * quarter : 2 * quarter + width]
        mixed_turned = send[2 * quarter + width : 2 * quarter + 2 * width]
        side = width // 2
        branch = jnp.concatenate(
            [
                rows_of(keep, 4 * quarter, 0),
                rows_of(keep, 4 * quarter, 1)[:, : side - 256],
                rows_of(send, 2 * quarter + 2 * width, 0),
                rows_of(send, 2 * quarter + 2 * width, 1)[:, : side - 256],
            ],
            axis=1,
        )

        def sum_all(value):
            value = value.astype(BF16)
            value = lax.psum_scatter(value, "w", scatter_dimension=0, tiled=True)
            return lax.psum(value, ("o", "z", "x", "c")).astype(F32)

        total_down = sum_all(matmul(act, ffn))
        total_up = sum_all(matmul(normed_turned, pre))
        total_out = sum_all(matmul(mixed_turned, branch))
        small_own = lax.psum(small_own, ("o", "z", "x", "c", "w"))
        vectors = [part_of(small_own[at], w_at, count_w, 0) for at in range(6)]
        total_up_bias = part_of(small_own[8:12].reshape(-1), w_at, count_w, 0)

    input_grad = resid_grad + token_grad.astype(F32)
    total_query, total_key, total_value, head_bias = head_finish(
        spot, head_four, head_other
    )
    totals = [part_of(head_bias[at], w_at, count_w, 0) for at in (0, 8)] + vectors
    return (
        outputs[None],
        input_grad[None],
        total_query,
        totals[0],
        total_key,
        total_value,
        totals[1],
        total_out,
        totals[2],
        totals[3],
        totals[4],
        total_up,
        total_up_bias,
        total_down,
        totals[5],
        totals[6],
        totals[7],
    )


def solution(mesh):
    count_s = mesh.shape["seq"]
    count_w = mesh.shape["wshard"]
    count_o = count_s // 16
    fine = Mesh(
        mesh.devices.reshape(count_o, ZS, 2, 2, count_w), ("o", "z", "x", "c", "w")
    )
    seq = ("o", "z", "x", "c")
    rows = P("w", seq, None)
    matrix = P("w", None)
    vector = P("w")
    placed = (
        rows,
        vector,
        rows,
        matrix,
        vector,
        matrix,
        matrix,
        vector,
        matrix,
        vector,
        vector,
        vector,
        matrix,
        vector,
        matrix,
        vector,
        vector,
        vector,
    )
    return jax.shard_map(
        partial(body, sizes=(count_o, count_w)),
        mesh=fine,
        in_specs=placed,
        out_specs=(
            rows,
            rows,
            matrix,
            vector,
            matrix,
            matrix,
            vector,
            matrix,
            vector,
            vector,
            vector,
            matrix,
            vector,
            matrix,
            vector,
            vector,
            vector,
        ),
        check_vma=False,
    )
```

time: 454 us -> 365 us (0.80); the launches traced: 446 us -> 364 us
  waiting for transfers between devices: 196 us -> 140 us
  Pallas kernels: 120 us -> 104 us
  starting transfers between devices: 54.9 us -> 39.8 us
    ppermute x30 -> x25, waiting for transfers between devices: 73.1 us -> 39.8 us  [swap(): return lax.ppermute(value, axis, SWAP)]
    all_to_all x2 -> x0, waiting for transfers between devices: 19.5 us -> none  [the longest x1 10.9 us: body(): head_grads = lax.all_to_all(mixed_grad, 'z', 0, 1, tiled=True)]
    ppermute x30 -> x25, starting transfers between devices: 37.8 us -> 22.9 us  [swap(): return lax.ppermute(value, axis, SWAP)]
    pallas_call x11 -> x8, Pallas kernels: 38.3 us -> 28.9 us  [the longest x1 15.9 us: middle(): pl.pallas_call(partial(middle_kernel, groups=groups, shared=len(weights)...]
    pallas_call x4 -> x2, Pallas kernels: 9.89 us -> 2.63 us  [down_slab(): pl.pallas_call(down_kernel, grid_spec=pltpu.PrefetchScalarGridSpec(num_sc...]
    all_to_all x2 -> x0, starting transfers between devices: 7.09 us -> none  [the longest x1 3.63 us: body(): low_mixed = lax.all_to_all(attended.astype(BF16), 'z', 1, 0, tiled=True)]
    ppermute x12 -> x16, starting transfers between devices: 9.72 us -> 16.8 us  [the longest x6 7.23 us: exchange(): lax.ppermute(item, 'z', perm)]
    unnamed x102 -> x124, local copies, waits for them, and re-layouts: 16.5 us -> 21.9 us
  transfers between devices with their start and end apart: 46 -> 43, of which waited for: 18 -> 17; matrix products, arithmetic and copies ran while one was open for 9% -> 11% of each run, Pallas kernels for 21% -> 24%
where the time goes in v3:
time: 365 us; the launch traced here: 364 us
  waiting for transfers between devices  140 us (38%)
  Pallas kernels  104 us (28%)
  starting transfers between devices  39.8 us (11%)
  local copies, waits for them, and re-layouts  33.7 us (9%)
  other arithmetic  31.3 us (9%)
  between operations  15.6 us (4%)
    ppermute x5, waiting for transfers between devices, to_near(): return lax.ppermute(value, 'z', near)  50.8 us
    ppermute x25, waiting for transfers between devices, swap(): return lax.ppermute(value, axis, SWAP)  39.8 us
    pallas_call x1, Pallas kernels, attend_backward(): pl.pallas_call(partial(backward_kernel, blocks=blocks, rows=block_rows //...  37.3 us
    ppermute x5, waiting for transfers between devices, to_far(): return lax.ppermute(value, 'z', far)  29.6 us
    pallas_call x1, Pallas kernels, attend_forward(): pl.pallas_call(partial(forward_kernel, blocks=blocks, rows=block_rows //...  25 us
    ppermute x25, starting transfers between devices, swap(): return lax.ppermute(value, axis, SWAP)  22.9 us
    unnamed x124, local copies, waits for them, and re-layouts  21.9 us
    pallas_call x1, Pallas kernels, middle(): pl.pallas_call(partial(middle_kernel, groups=groups, shared=len(weights)...  15.9 us
  transfers between devices with their start and end apart: 43, of which 17 were waited for; matrix products, arithmetic and copies ran while one was open for 11% of the time, Pallas kernels for 24%

profile of v3, /device:TPU:1, one launch (start us, length us, event | category | flops | bytes accessed | tf_op | source)
XLA Modules:
  0.0 364.2 jit_solution(16577580743334880378)
XLA Ops:
  7.3 2.0 bitcast_convert_fusion
  14.4 2.1 collective-permute-start
  16.5 2.7 convert_element_type.190.refs_5_
  19.2 2.2 convert_element_type.189.refs_4_
  23.3 2.6 convert_element_type.191.refs_6_
  33.6 15.8 %all-gather.2.cloned.1.call-done.tokens_ref = bf16[1024,768]{1,0:T(8,128)(2,1)} async-done(((bf16[256,768]{1,0:T(8,128)(2,1)}), bf16[1024,768]{1,0:T(8,128)(2,1)}) %all-gather.2.cloned.1.call-update) | async-done | bytes 1572880 | tf_op jit(solution)/shard_map/all_gather | solution.py:805
  56.5 16.1 %collective-permute-done.1.refs_1_.refs_5_ = bf16[1024,384]{1,0:T(8,128)(2,1)S(1)} collective-permute-done((bf16[1024,384]{1,0:T(8,128)(2,1)S(1)}, bf16[1024,384]{1,0:T(8,128)(2,1)S(1)}, u32[]{:S(2)}, u32[]{:S(2)}) %collective-permute-start.1) | collective-permute-done | bytes 786464 | tf_op jit(solution)/shard_map/ppermute | solution.py:33
  77.2 25.0 %attend_forward.1 = (f32[192,1024]{1,0:T(8,128)S(1)}, bf16[192,256]{1,0:T(8,128)(2,1)S(1)}, bf16[192,256]{1,0:T(8,128)(2,1)S(1)}, bf16[192,256]{1,0:T(8,128)(2,1...) custom-call(s32[6]{0:T(128)S(1)} %stack.80.meta_ref, bf16[192,1024]{1,0:T(8,128)(2,1)S(1)} %copy-done.23, ...), custom_call_target="tpu_custom_call" | custom-call | flops 24000 | bytes 1 | tf_op jit(solution)/shard_map/attend_forward/pallas_call | solution.py:120
  106.0 2.2 collective-permute-start.6
  110.8 3.5 collective-permute-done.6.refs_3_
  115.8 15.9 %middle.1 = (f32[256,768]{1,0:T(8,128)}, f32[256,768]{1,0:T(8,128)}, bf16[192,256]{1,0:T(8,128)(2,1)}, bf16[192,256]{1,0:T(8,128)(2,1)}, bf16[192,256]{1,0:T(8,1...) custom-call(s32[4]{0:T(128)} %pad_add_fusion.2.meta_ref, ...), custom_call_target="tpu_custom_call" | custom-call | flops 15000 | bytes 1 | tf_op jit(solution)/shard_map/middle/pallas_call | solution.py:450
  139.1 1.9 copy-done.2
  152.3 37.3 %attend_backward.1 = (bf16[192,1024]{1,0:T(8,128)(2,1)S(1)}, bf16[2048,384]{1,0:T(8,128)(2,1)}, bf16[2048,384]{1,0:T(8,128)(2,1)}) custom-call(s32[6]{0:T(128)S(1)} %stack.80.meta_ref, bf16[192,1024]{1,0:T(8,128)(2,1)S(1)} %copy-done.24, f32[192,1024]{1,0:T(8,128)S(1)} %copy-done.26, f32[3,1,1024]{2,1,0:T(1,128)S(1)} %get-tuple-element.134.log_ref, ...), custom_call_target="tpu_custom_call" | custom-call | flops 36000 | bytes 1 | tf_op jit(solution)/shard_map/attend_backward/pallas_call | solution.py:215
  196.1 2.9 add_convert_fusion.3
  199.0 9.2 %collective-permute-done.17 = bf16[384,768]{1,0:T(8,128)(2,1)S(1)} collective-permute-done((bf16[384,768]{1,0:T(8,128)(2,1)S(1)}, bf16[384,768]{1,0:T(8,128)(2,1)S(1)}, u32[]{:S(2)}, u32[]{:S(2)}) %collective-permute-start.17) | collective-permute-done | bytes 589856 | tf_op jit(solution)/shard_map/ppermute | solution.py:33
  210.0 3.4 collective-permute-done.18
  218.6 9.0 %collective-permute-done.20 = bf16[96,2048]{1,0:T(8,128)(2,1)} collective-permute-done((bf16[96,2048]{1,0:T(8,128)(2,1)}, bf16[96,2048]{1,0:T(8,128)(2,1)}, u32[]{:S(2)}, u32[]{:S(2)}) %collective-permute-start.20) | collective-permute-done | bytes 393248 | tf_op jit(solution)/shard_map/ppermute | solution.py:939
  228.7 5.1 %collective-permute-done.22 = bf16[1024,384]{1,0:T(8,128)(2,1)S(1)} collective-permute-done((bf16[1024,384]{1,0:T(8,128)(2,1)}, bf16[1024,384]{1,0:T(8,128)(2,1)S(1)}, u32[]{:S(2)}, u32[]{:S(2)}) %collective-permute-start.22) | collective-permute-done | bytes 786464 | tf_op jit(solution)/shard_map/ppermute | solution.py:33
  236.3 2.6 collective-permute-start.24
  243.3 11.8 %collective-permute-done.25 = bf16[48,2048]{1,0:T(8,128)(2,1)S(1)} collective-permute-done((bf16[48,2048]{1,0:T(8,128)(2,1)S(1)}, bf16[48,2048]{1,0:T(8,128)(2,1)S(1)}, u32[]{:S(2)}, u32[]{:S(2)}) %collective-permute-start.25) | collective-permute-done | bytes 196640 | tf_op jit(solution)/shard_map/ppermute | solution.py:942
  260.0 1.9 maximum_select_fusion.6
  261.9 2.4 collective-permute-start.29
  265.5 3.9 %collective-permute-done.28 = bf16[48,2048]{1,0:T(8,128)(2,1)} collective-permute-done((bf16[48,2048]{1,0:T(8,128)(2,1)}, bf16[48,2048]{1,0:T(8,128)(2,1)}, u32[]{:S(2)}, u32[]{:S(2)}) %collective-permute-start.28) | collective-permute-done | bytes 196640 | tf_op jit(solution)/shard_map/ppermute | solution.py:942
  272.8 13.2 %collective-permute-done.29 = bf16[192,768]{1,0:T(8,128)(2,1)} collective-permute-done((bf16[192,768]{1,0:T(8,128)(2,1)}, bf16[192,768]{1,0:T(8,128)(2,1)}, u32[]{:S(2)}, u32[]{:S(2)}) %collective-permute-start.29) | collective-permute-done | bytes 294944 | tf_op jit(solution)/shard_map/ppermute | solution.py:939
  288.4 20.8 %collective-permute-done.31 = bf16[96,2048]{1,0:T(8,128)(2,1)S(1)} collective-permute-done((bf16[96,2048]{1,0:T(8,128)(2,1)S(1)}, bf16[96,2048]{1,0:T(8,128)(2,1)S(1)}, u32[]{:S(2)}, u32[]{:S(2)}) %collective-permute-start.31) | collective-permute-done | bytes 393248 | tf_op jit(solution)/shard_map/ppermute | solution.py:939
  310.6 13.9 %collective-permute-done.33 = bf16[208,576]{1,0:T(8,128)(2,1)S(1)} collective-permute-done((bf16[208,576]{1,0:T(8,128)(2,1)S(1)}, bf16[208,576]{1,0:T(8,128)(2,1)S(1)}, u32[]{:S(2)}, u32[]{:S(2)}) %collective-permute-start.33) | collective-permute-done | bytes 239648 | tf_op jit(solution)/shard_map/ppermute | solution.py:942
  325.2 3.0 collective-permute-done.34.refs_1_
  330.0 7.8 %collective-permute-done.35 = bf16[2,208,576]{2,1,0:T(8,128)(2,1)S(1)} collective-permute-done((bf16[2,208,576]{2,1,0:T(8,128)(2,1)S(1)}, bf16[2,208,576]{2,1,0:T(8,128)(2,1)S(1)}, u32[]{:S(2)}, u32[]{:S(2)}) %collective-permute-start.35) | collective-permute-done | bytes 479264 | tf_op jit(solution)/shard_map/ppermute | solution.py:939
  339.5 4.3 %down_finish.1 = f32[1536,768]{1,0:T(8,128)} custom-call(s32[2]{0:T(128)S(1)} %pad_add_fusion.3.meta_ref, bf16[384,768]{1,0:T(8,128)(2,1)S(1)} %maximum_select_fusion.3.refs_0_, bf16[384,768]{1,0:T(8,128)(2,1)S(1)} %collective-permute-done.32.refs_1_, bf16[384,768]{1,0:T(8,128)(2,1)} %collective-permute-done.39.refs_2_, ...), custom_call_target="tpu_custom_call" | custom-call | flops 4000 | bytes 1 | tf_op jit(solution)/shard_map/down_finish/pallas_call | solution.py:656
  343.8 5.1 %up_finish.1 = (f32[384,3072]{1,0:T(8,128)}, f32[384,768]{1,0:T(8,128)}, f32[384,128]{1,0:T(8,128)S(1)}) custom-call(s32[2]{0:T(128)S(1)} %pad_add_fusion.3.meta_ref, bf16[192,2048]{1,0:T(8,128)(2,1)S(1)} %maximum_select_fusion.2.refs_0_, bf16[192,2048]{1,0:T(8,128)(2,1)} %collective-permute-done.34.refs_1_, ...), custom_call_target="tpu_custom_call" | custom-call | flops 5000 | bytes 1 | tf_op jit(solution)/shard_map/up_finish/pallas_call | solution.py:693
  350.1 4.1 %head_finish.1 = (f32[384,768]{1,0:T(8,128)}, f32[384,768]{1,0:T(8,128)}, f32[384,768]{1,0:T(8,128)}, f32[16,768]{1,0:T(8,128)S(1)}) custom-call(s32[2]{0:T(128)S(1)} %pad_add_fusion.3.meta_ref, bf16[4,208,576]{2,1,0:T(8,128)(2,1)S(1)} %maximum_select_fusion.own_ref, bf16[4,208,576]{2,1,0:T(8,128)(2,1)} %collective-permute-done.36.got_ref), custom_call_target="tpu_custom_call" | custom-call | flops 4000 | bytes 1 | tf_op jit(solution)/shard_map/head_finish/pallas_call | solution.py:738
  355.4 1.9 add_bitcast_fusion
  (274 shorter events, 93.1 us)
Async XLA Ops:
  7.3 42.1 %all-gather.2.cloned.1.call-start = ((), (), s32[]{:S(2)}) async-start(), calls=%async_computation.1 | async-start | bytes 1966080 | tf_op jit(solution)/shard_map/all_gather | solution.py:805
  9.4 346.0 %reduce-scatter.2.cloned.1.call-start = ((), (), s32[]{:S(2)}) async-start(), calls=%async_computation.2 | async-start | bytes 1966080 | tf_op jit(solution)/shard_map/reduce_scatter | solution.py:993
  14.4 15.3 %collective-permute-start = (bf16[392,576]{1,0:T(8,128)(2,1)}, bf16[392,576]{1,0:T(8,128)(2,1)}, u32[]{:S(2)}, u32[]{:S(2)}) collective-permute-start(bf16[392,576]{1,0:T(8,128)(2,1)} %pad_maximum_fusion.1), channel_id=1, source_target_pairs={{0,1},{1,0},{2,3},{3,2},{4,5},{5,4},{6,7},{7,6},{8,9},{9,8},{10,11... | collective-permute-start | bytes 1354760 | tf_op jit(solution)/shard_map/ppermute | solution.py:33
  29.8 74.0 %collective-permute-start.7 = (bf16[1728,768]{1,0:T(8,128)(2,1)}, bf16[1728,768]{1,0:T(8,128)(2,1)}, u32[]{:S(2)}, u32[]{:S(2)}) collective-permute-start(bf16[1728,768]{1,0:T(8,128)(2,1)} %pad_maximum_fusion), channel_id=1, source_target_pairs={{0,1},{1,0},{2,3},{3,2},{4,5},{5,4},{6,7},{7,6},{8,9},{9,8},{10,11... | collective-permute-start | bytes 7962632 | tf_op jit(solution)/shard_map/ppermute | solution.py:33
  54.2 18.4 %collective-permute-start.1 = (bf16[1024,384]{1,0:T(8,128)(2,1)S(1)}, bf16[1024,384]{1,0:T(8,128)(2,1)S(1)}, u32[]{:S(2)}, u32[]{:S(2)}) collective-permute-start(bf16[1024,384]{1,0:T(8,128)(2,1)S(1)} %get-tuple-element.110.refs_0_.refs_4_), channel_id=1, source_target_pairs={{0,4},{4,0},{1,5},{5,1},{2,6},{6,2},{3,7},{7,3},{8,12},{12,8},{9,1... | collective-permute-start | bytes 2359304 | tf_op jit(solution)/shard_map/ppermute | solution.py:33
  55.4 19.5 %collective-permute-start.2 = (bf16[1024,384]{1,0:T(8,128)(2,1)S(1)}, bf16[1024,384]{1,0:T(8,128)(2,1)S(1)}, u32[]{:S(2)}, u32[]{:S(2)}) collective-permute-start(bf16[1024,384]{1,0:T(8,128)(2,1)S(1)} %get-tuple-element.110.refs_0_.refs_4_), channel_id=1, source_target_pairs={{0,2},{2,0},{1,3},{3,1},{4,6},{6,4},{5,7},{7,5},{8,10},{10,8},{9,1... | collective-permute-start | bytes 2359304 | tf_op jit(solution)/shard_map/ppermute | solution.py:33
  133.6 11.6 %collective-permute-start.10 = (f32[16,768]{1,0:T(8,128)}, f32[16,768]{1,0:T(8,128)S(1)}, u32[]{:S(2)}, u32[]{:S(2)}) collective-permute-start(f32[16,768]{1,0:T(8,128)} %get-tuple-element.125.own_small_ref), channel_id=1, source_target_pairs={{0,2},{2,0},{1,3},{3,1},{4,6},{6,4},{5,7},{7,5},{8,10},{10,8},{9,1... | collective-permute-start | bytes 147464 | tf_op jit(solution)/shard_map/ppermute | solution.py:33
  133.7 16.1 %collective-permute-start.11 = (bf16[192,256]{1,0:T(8,128)(2,1)}, bf16[192,256]{1,0:T(8,128)(2,1)S(1)}, u32[]{:S(2)}, u32[]{:S(2)}) collective-permute-start(bf16[192,256]{1,0:T(8,128)(2,1)} %get-tuple-element.128), channel_id=1, source_target_pairs={{0,8},{8,0},{16,24},{24,16},{1,9},{9,1},{17,25},{25,17},{2,10},{10... | collective-permute-start | bytes 294920 | tf_op jit(solution)/shard_map/ppermute | solution.py:879
  135.2 14.6 %collective-permute-start.12 = (bf16[192,256]{1,0:T(8,128)(2,1)}, bf16[192,256]{1,0:T(8,128)(2,1)S(1)}, u32[]{:S(2)}, u32[]{:S(2)}) collective-permute-start(bf16[192,256]{1,0:T(8,128)(2,1)} %get-tuple-element.129), channel_id=1, source_target_pairs={{0,16},{16,0},{8,24},{24,8},{1,17},{17,1},{9,25},{25,9},{2,18},{18... | collective-permute-start | bytes 294920 | tf_op jit(solution)/shard_map/ppermute | solution.py:879
  136.2 13.6 %collective-permute-start.13 = (bf16[192,256]{1,0:T(8,128)(2,1)}, bf16[192,256]{1,0:T(8,128)(2,1)S(1)}, u32[]{:S(2)}, u32[]{:S(2)}) collective-permute-start(bf16[192,256]{1,0:T(8,128)(2,1)} %get-tuple-element.130), channel_id=1, source_target_pairs={{0,24},{24,0},{8,16},{16,8},{1,25},{25,1},{9,17},{17,9},{2,26},{26... | collective-permute-start | bytes 294920 | tf_op jit(solution)/shard_map/ppermute | solution.py:879
  149.7 39.8 %collective-permute-start.15 = (bf16[384,2048]{1,0:T(8,128)(2,1)S(1)}, bf16[384,2048]{1,0:T(8,128)(2,1)S(1)}, u32[]{:S(2)}, u32[]{:S(2)}) collective-permute-start(bf16[384,2048]{1,0:T(8,128)(2,1)S(1)} %get-tuple-element.132), channel_id=1, source_target_pairs={{0,4},{4,0},{1,5},{5,1},{2,6},{6,2},{3,7},{7,3},{8,12},{12,8},{9,1... | collective-permute-start | bytes 4718600 | tf_op jit(solution)/shard_map/ppermute | solution.py:33
  151.0 38.6 %collective-permute-start.14 = (bf16[768,768]{1,0:T(8,128)(2,1)S(1)}, bf16[768,768]{1,0:T(8,128)(2,1)S(1)}, u32[]{:S(2)}, u32[]{:S(2)}) collective-permute-start(bf16[768,768]{1,0:T(8,128)(2,1)S(1)} %down_slab.2), channel_id=1, source_target_pairs={{0,1},{1,0},{2,3},{3,2},{4,5},{5,4},{6,7},{7,6},{8,9},{9,8},{10,11... | collective-permute-start | bytes 3538952 | tf_op jit(solution)/shard_map/ppermute | solution.py:33
  193.5 14.7 %collective-permute-start.17 = (bf16[384,768]{1,0:T(8,128)(2,1)S(1)}, bf16[384,768]{1,0:T(8,128)(2,1)S(1)}, u32[]{:S(2)}, u32[]{:S(2)}) collective-permute-start(bf16[384,768]{1,0:T(8,128)(2,1)S(1)} %constant_dynamic-slice_fusion.7), channel_id=1, source_target_pairs={{0,4},{4,0},{1,5},{5,1},{2,6},{6,2},{3,7},{7,3},{8,12},{12,8},{9,1... | collective-permute-start | bytes 1769480 | tf_op jit(solution)/shard_map/ppermute | solution.py:33
  194.8 18.7 %collective-permute-start.18 = (bf16[192,2048]{1,0:T(8,128)(2,1)S(1)}, bf16[192,2048]{1,0:T(8,128)(2,1)S(1)}, u32[]{:S(2)}, u32[]{:S(2)}) collective-permute-start(bf16[192,2048]{1,0:T(8,128)(2,1)S(1)} %dynamic-slice_bitcast_fusion), channel_id=1, source_target_pairs={{0,1},{1,0},{2,3},{3,2},{4,5},{5,4},{6,7},{7,6},{8,9},{9,8},{10,11... | collective-permute-start | bytes 2359304 | tf_op jit(solution)/shard_map/ppermute | solution.py:33
  214.5 13.1 %collective-permute-start.20 = (bf16[96,2048]{1,0:T(8,128)(2,1)}, bf16[96,2048]{1,0:T(8,128)(2,1)}, u32[]{:S(2)}, u32[]{:S(2)}) collective-permute-start(bf16[96,2048]{1,0:T(8,128)(2,1)} %constant_dynamic-slice_fusion.5), channel_id=1, source_target_pairs={{0,8},{8,0},{16,24},{24,16},{1,9},{9,1},{17,25},{25,17},{2,10},{10... | collective-permute-start | bytes 1179656 | tf_op jit(solution)/shard_map/ppermute | solution.py:939
  216.1 17.6 %collective-permute-start.22 = (bf16[1024,384]{1,0:T(8,128)(2,1)}, bf16[1024,384]{1,0:T(8,128)(2,1)S(1)}, u32[]{:S(2)}, u32[]{:S(2)}) collective-permute-start(bf16[1024,384]{1,0:T(8,128)(2,1)} %get-tuple-element.162), channel_id=1, source_target_pairs={{0,4},{4,0},{1,5},{5,1},{2,6},{6,2},{3,7},{7,3},{8,12},{12,8},{9,1... | collective-permute-start | bytes 2359304 | tf_op jit(solution)/shard_map/ppermute | solution.py:33
  217.2 11.5 %collective-permute-start.21 = (bf16[96,768]{1,0:T(8,128)(2,1)S(1)}, bf16[96,768]{1,0:T(8,128)(2,1)S(1)}, u32[]{:S(2)}, u32[]{:S(2)}) collective-permute-start(bf16[96,768]{1,0:T(8,128)(2,1)S(1)} %constant_dynamic-slice_fusion.4), channel_id=1, source_target_pairs={{0,16},{16,0},{8,24},{24,8},{1,17},{17,1},{9,25},{25,9},{2,18},{18... | collective-permute-start | bytes 442376 | tf_op jit(solution)/shard_map/ppermute | solution.py:942
  240.1 15.0 %collective-permute-start.25 = (bf16[48,2048]{1,0:T(8,128)(2,1)S(1)}, bf16[48,2048]{1,0:T(8,128)(2,1)S(1)}, u32[]{:S(2)}, u32[]{:S(2)}) collective-permute-start(bf16[48,2048]{1,0:T(8,128)(2,1)S(1)} %constant_dynamic-slice_fusion.3), channel_id=1, source_target_pairs={{0,16},{16,0},{8,24},{24,8},{1,17},{17,1},{9,25},{25,9},{2,18},{18... | collective-permute-start | bytes 589832 | tf_op jit(solution)/shard_map/ppermute | solution.py:942
  241.9 18.1 %collective-permute-start.26 = (bf16[96,768]{1,0:T(8,128)(2,1)}, bf16[96,768]{1,0:T(8,128)(2,1)}, u32[]{:S(2)}, u32[]{:S(2)}) collective-permute-start(bf16[96,768]{1,0:T(8,128)(2,1)} %add_convert_fusion.11), channel_id=1, source_target_pairs={{0,16},{16,0},{8,24},{24,8},{1,17},{17,1},{9,25},{25,9},{2,18},{18... | collective-permute-start | bytes 442376 | tf_op jit(solution)/shard_map/ppermute | solution.py:942
  257.3 12.0 %collective-permute-start.28 = (bf16[48,2048]{1,0:T(8,128)(2,1)}, bf16[48,2048]{1,0:T(8,128)(2,1)}, u32[]{:S(2)}, u32[]{:S(2)}) collective-permute-start(bf16[48,2048]{1,0:T(8,128)(2,1)} %add_convert_fusion.10), channel_id=1, source_target_pairs={{0,16},{16,0},{8,24},{24,8},{1,17},{17,1},{9,25},{25,9},{2,18},{18... | collective-permute-start | bytes 589832 | tf_op jit(solution)/shard_map/ppermute | solution.py:942
  261.9 24.0 %collective-permute-start.29 = (bf16[192,768]{1,0:T(8,128)(2,1)}, bf16[192,768]{1,0:T(8,128)(2,1)}, u32[]{:S(2)}, u32[]{:S(2)}) collective-permute-start(bf16[192,768]{1,0:T(8,128)(2,1)} %maximum_select_fusion.6), channel_id=1, source_target_pairs={{0,8},{8,0},{16,24},{24,16},{1,9},{9,1},{17,25},{25,17},{2,10},{10... | collective-permute-start | bytes 884744 | tf_op jit(solution)/shard_map/ppermute | solution.py:939
  270.7 38.6 %collective-permute-start.31 = (bf16[96,2048]{1,0:T(8,128)(2,1)S(1)}, bf16[96,2048]{1,0:T(8,128)(2,1)S(1)}, u32[]{:S(2)}, u32[]{:S(2)}) collective-permute-start(bf16[96,2048]{1,0:T(8,128)(2,1)S(1)} %maximum_select_fusion.5), channel_id=1, source_target_pairs={{0,8},{8,0},{16,24},{24,16},{1,9},{9,1},{17,25},{25,17},{2,10},{10... | collective-permute-start | bytes 1179656 | tf_op jit(solution)/shard_map/ppermute | solution.py:939
  271.8 16.6 %collective-permute-start.30 = (bf16[208,576]{1,0:T(8,128)(2,1)S(1)}, bf16[208,576]{1,0:T(8,128)(2,1)S(1)}, u32[]{:S(2)}, u32[]{:S(2)}) collective-permute-start(bf16[208,576]{1,0:T(8,128)(2,1)S(1)} %add_convert_fusion.9), channel_id=1, source_target_pairs={{0,4},{4,0},{1,5},{5,1},{2,6},{6,2},{3,7},{7,3},{8,12},{12,8},{9,1... | collective-permute-start | bytes 718856 | tf_op jit(solution)/shard_map/ppermute | solution.py:33
  287.4 23.1 %collective-permute-start.32 = (bf16[384,768]{1,0:T(8,128)(2,1)S(1)}, bf16[384,768]{1,0:T(8,128)(2,1)S(1)}, u32[]{:S(2)}, u32[]{:S(2)}) collective-permute-start(bf16[384,768]{1,0:T(8,128)(2,1)S(1)} %maximum_select_fusion.3.refs_0_), channel_id=1, source_target_pairs={{0,4},{4,0},{1,5},{5,1},{2,6},{6,2},{3,7},{7,3},{8,12},{12,8},{9,1... | collective-permute-start | bytes 1769480 | tf_op jit(solution)/shard_map/ppermute | solution.py:33
  309.4 18.8 %collective-permute-start.34 = (bf16[192,2048]{1,0:T(8,128)(2,1)S(1)}, bf16[192,2048]{1,0:T(8,128)(2,1)}, u32[]{:S(2)}, u32[]{:S(2)}) collective-permute-start(bf16[192,2048]{1,0:T(8,128)(2,1)S(1)} %maximum_select_fusion.2.refs_0_), channel_id=1, source_target_pairs={{0,4},{4,0},{1,5},{5,1},{2,6},{6,2},{3,7},{7,3},{8,12},{12,8},{9,1... | collective-permute-start | bytes 2359304 | tf_op jit(solution)/shard_map/ppermute | solution.py:33
  310.5 14.0 %collective-permute-start.33 = (bf16[208,576]{1,0:T(8,128)(2,1)S(1)}, bf16[208,576]{1,0:T(8,128)(2,1)S(1)}, u32[]{:S(2)}, u32[]{:S(2)}) collective-permute-start(bf16[208,576]{1,0:T(8,128)(2,1)S(1)} %add_convert_fusion.8), channel_id=1, source_target_pairs={{0,16},{16,0},{8,24},{24,8},{1,17},{17,1},{9,25},{25,9},{2,18},{18... | collective-permute-start | bytes 718856 | tf_op jit(solution)/shard_map/ppermute | solution.py:942
  324.6 13.2 %collective-permute-start.35 = (bf16[2,208,576]{2,1,0:T(8,128)(2,1)S(1)}, bf16[2,208,576]{2,1,0:T(8,128)(2,1)S(1)}, u32[]{:S(2)}, u32[]{:S(2)}) collective-permute-start(bf16[2,208,576]{2,1,0:T(8,128)(2,1)S(1)} %maximum_select_fusion.4), channel_id=1, source_target_pairs={{0,8},{8,0},{16,24},{24,16},{1,9},{9,1},{17,25},{25,17},{2,10},{10... | collective-permute-start | bytes 1437704 | tf_op jit(solution)/shard_map/ppermute | solution.py:939
  324.7 19.1 %collective-permute-start.37 = (bf16[192,2048]{1,0:T(8,128)(2,1)S(1)}, bf16[192,2048]{1,0:T(8,128)(2,1)}, u32[]{:S(2)}, u32[]{:S(2)}) collective-permute-start(bf16[192,2048]{1,0:T(8,128)(2,1)S(1)} %maximum_select_fusion.2.refs_0_), channel_id=1, source_target_pairs={{0,2},{2,0},{1,3},{3,1},{4,6},{6,4},{5,7},{7,5},{8,10},{10,8},{9,1... | collective-permute-start | bytes 2359304 | tf_op jit(solution)/shard_map/ppermute | solution.py:33
  328.2 15.6 %collective-permute-start.38 = (bf16[192,2048]{1,0:T(8,128)(2,1)}, bf16[192,2048]{1,0:T(8,128)(2,1)}, u32[]{:S(2)}, u32[]{:S(2)}) collective-permute-start(bf16[192,2048]{1,0:T(8,128)(2,1)} %collective-permute-done.34.refs_1_), channel_id=1, source_target_pairs={{0,2},{2,0},{1,3},{3,1},{4,6},{6,4},{5,7},{7,5},{8,10},{10,8},{9,1... | collective-permute-start | bytes 2359304 | tf_op jit(solution)/shard_map/ppermute | solution.py:33
  329.5 10.0 %collective-permute-start.39 = (bf16[384,768]{1,0:T(8,128)(2,1)S(1)}, bf16[384,768]{1,0:T(8,128)(2,1)}, u32[]{:S(2)}, u32[]{:S(2)}) collective-permute-start(bf16[384,768]{1,0:T(8,128)(2,1)S(1)} %maximum_select_fusion.3.refs_0_), channel_id=1, source_target_pairs={{0,2},{2,0},{1,3},{3,1},{4,6},{6,4},{5,7},{7,5},{8,10},{10,8},{9,1... | collective-permute-start | bytes 1769480 | tf_op jit(solution)/shard_map/ppermute | solution.py:33
  329.5 10.0 %collective-permute-start.40 = (bf16[384,768]{1,0:T(8,128)(2,1)S(1)}, bf16[384,768]{1,0:T(8,128)(2,1)}, u32[]{:S(2)}, u32[]{:S(2)}) collective-permute-start(bf16[384,768]{1,0:T(8,128)(2,1)S(1)} %collective-permute-done.32.refs_1_), channel_id=1, source_target_pairs={{0,2},{2,0},{1,3},{3,1},{4,6},{6,4},{5,7},{7,5},{8,10},{10,8},{9,1... | collective-permute-start | bytes 1769480 | tf_op jit(solution)/shard_map/ppermute | solution.py:33
  338.1 12.0 %collective-permute-start.36 = (bf16[4,208,576]{2,1,0:T(8,128)(2,1)S(1)}, bf16[4,208,576]{2,1,0:T(8,128)(2,1)}, u32[]{:S(2)}, u32[]{:S(2)}) collective-permute-start(bf16[4,208,576]{2,1,0:T(8,128)(2,1)S(1)} %maximum_select_fusion.own_ref), channel_id=1, source_target_pairs={{0,2},{2,0},{1,3},{3,1},{4,6},{6,4},{5,7},{7,5},{8,10},{10,8},{9,1... | collective-permute-start | bytes 2875400 | tf_op jit(solution)/shard_map/ppermute | solution.py:33
  (69 other events, 457.4 us)
Sparse Core Ops, SparseCore 0:
  10.3 39.0 all-gather.1
  260.1 48.1 reduce-scatter.1

commit v4 on v3

--- a/solution.py
+++ b/solution.py
@@ -46,22 +46,29 @@
     return jnp.concatenate([kv, fill.astype(BF16)], axis=1)
 
 
-def forward_kernel(meta_ref, q_ref, *refs, blocks, rows):
-    kv_refs = refs[:blocks]
-    out_ref = refs[blocks]
-    piece_refs = refs[blocks + 1 : blocks + 1 + ZS]
-    log_ref = refs[blocks + 1 + ZS]
-    value_refs = refs[blocks + 2 + ZS : 2 * blocks + 2 + ZS]
-    low_ref = refs[-1]
-    head_dim, query_count = q_ref.shape
+def load_head(kv_refs, rows_ref, turned_ref, low):
+    head_dim = turned_ref.shape[1]
+    for at, ref in enumerate(kv_refs):
+        block, half = at // 2, at % 2
+        size = ref.shape[0]
+        for start in range(0, size, 256):
+            value = ref[start : start + 256, :]
+            place = slice(half * size + start, half * size + start + 256)
+            rows_ref[block, place, :] = value
+            turned_ref[block, :, place] = value.T[low : low + head_dim, :]
+
+
+def forward_kernel(meta_ref, *refs, blocks, rows):
+    query_refs, kv_refs = refs[:2], refs[2 : 2 + 2 * blocks]
+    out_ref, *refs = refs[2 + 2 * blocks :]
+    piece_refs, (log_ref, rows_ref, turned_ref) = refs[:ZS], refs[ZS:]
+    head_dim, query_count = out_ref.shape
     length, z_at = meta_ref[0], meta_ref[1]
-    for block in range(blocks):
-        for part in range(ZS):
-            cut = slice(part * rows, (part + 1) * rows)
-            value_refs[block][:, cut] = kv_refs[block][cut, :].T[head_dim:, :]
+    load_head(kv_refs, rows_ref, turned_ref, head_dim)
+    query = jnp.concatenate([ref[...] for ref in query_refs], axis=1)
     query = jnp.concatenate(
         [
-            q_ref[...],
+            query,
             jnp.zeros((head_dim, query_count), BF16),
             jnp.ones((128, query_count), BF16),
         ],
@@ -70,11 +77,11 @@
 
     def step(group, carry, members):
         top, total, acc = carry
-        start = pl.multiple_of(group * rows, rows)
+        start = pl.multiple_of((group ^ z_at) * rows, rows)
         found = []
         for block in members:
             place = (meta_ref[2 + block] + group * 4) * rows
-            kv = with_mask(kv_refs[block][pl.ds(start, rows), :], place, length)
+            kv = with_mask(rows_ref[block, pl.ds(start, rows), :], place, length)
             found.append(matmul(kv, query))
         new_top = top
         for scores in found:
@@ -86,7 +93,7 @@
             weights = jnp.exp(scores - new_top)
             total = total + jnp.sum(weights, axis=0, keepdims=True)
             acc = acc + matmul(
-                value_refs[block][:, pl.ds(start, rows)], weights.astype(BF16)
+                turned_ref[block, :, pl.ds(start, rows)], weights.astype(BF16)
             )
         return new_top, total, acc
 
@@ -102,65 +109,56 @@
     top, total, acc = carry
     out = acc * (1.0 / total)
     out_ref[...] = out
-    low_ref[...] = out.astype(BF16)
     size = query_count // ZS
     for at in range(ZS):
-        start = pl.multiple_of((z_at ^ at) * size, 128)
-        piece_refs[at][...] = low_ref[:, pl.ds(start, size)]
+        piece_refs[at][...] = out[:, at * size : (at + 1) * size].astype(BF16)
     log_ref[0] = top + jnp.log(total)
 
 
-def attend_forward(meta, queries, kv_blocks, first, head_dim):
+def attend_forward(meta, queries, kv_blocks, heads):
     blocks = len(kv_blocks)
-    block_rows, columns = kv_blocks[0].shape
-    heads = columns // 128
-    query_count = queries.shape[1]
+    half_rows = kv_blocks[0][0].shape[0]
+    part, half_count = queries[0].shape
+    head_dim, query_count = part // heads, 2 * half_count
     size = query_count // ZS
-    head_rows = pl.BlockSpec((head_dim, query_count), lambda i, m: (i, 0))
     return pl.pallas_call(
-        partial(forward_kernel, blocks=blocks, rows=block_rows // ZS),
+        partial(forward_kernel, blocks=blocks, rows=2 * half_rows // ZS),
         grid_spec=pltpu.PrefetchScalarGridSpec(
             num_scalar_prefetch=1,
             grid=(heads,),
-            in_specs=[pl.BlockSpec((head_dim, query_count), lambda i, m: (i + first, 0))]
-            + [pl.BlockSpec((block_rows, 128), lambda i, m: (0, i))] * blocks,
-            out_specs=[head_rows]
+            in_specs=[pl.BlockSpec((head_dim, half_count), lambda i, m: (i, 0))] * 2
+            + [pl.BlockSpec((half_rows, 128), lambda i, m: (0, i))] * (2 * blocks),
+            out_specs=[pl.BlockSpec((head_dim, query_count), lambda i, m: (i, 0))]
             + [pl.BlockSpec((head_dim, size), lambda i, m: (i, 0))] * ZS
             + [pl.BlockSpec((1, 1, query_count), lambda i, m: (i, 0, 0))],
-            scratch_shapes=[pltpu.VMEM((head_dim, block_rows), BF16)] * blocks
-            + [pltpu.VMEM((head_dim, query_count), BF16)],
+            scratch_shapes=[
+                pltpu.VMEM((blocks, 2 * half_rows, 128), BF16),
+                pltpu.VMEM((blocks, head_dim, 2 * half_rows), BF16),
+            ],
         ),
-        out_shape=[jax.ShapeDtypeStruct((heads * head_dim, query_count), F32)]
-        + [jax.ShapeDtypeStruct((heads * head_dim, size), BF16)] * ZS
+        out_shape=[jax.ShapeDtypeStruct((part, query_count), F32)]
+        + [jax.ShapeDtypeStruct((part, size), BF16)] * ZS
         + [jax.ShapeDtypeStruct((heads, 1, query_count), F32)],
         compiler_params=pltpu.CompilerParams(vmem_limit_bytes=40 << 20),
         cost_estimate=work(8 * heads),
         name="attend_forward",
-    )(meta, queries, *kv_blocks)
-
-
-def backward_kernel(meta_ref, q_ref, out_ref, log_ref, *refs, blocks, rows):
-    piece_refs = refs[:ZS]
-    kv_refs = refs[ZS : ZS + blocks]
-    refs = refs[ZS + blocks :]
-    dq_ref = refs[0]
-    pairs = refs[1 : 1 + blocks // 2]
-    key_refs = refs[1 + blocks // 2 : 1 + blocks // 2 + blocks]
-    go_ref, qn_ref, gn_ref, acc_ref = refs[1 + blocks // 2 + blocks :]
-    head_dim, query_count = q_ref.shape
+    )(meta, *queries, *[item for pair in kv_blocks for item in pair])
+
+
+def backward_kernel(meta_ref, *refs, blocks, rows, extra):
+    query_refs, (out_ref, log_ref), refs = refs[:2], refs[2:4], refs[4:]
+    grad_refs, kv_refs = refs[:ZS], refs[ZS : ZS + 2 * blocks]
+    refs = refs[ZS + 2 * blocks + extra :]
+    dq_refs, pairs = refs[:ZS], refs[ZS : ZS + blocks // 2]
+    rows_ref, turned_ref, qn_ref, gn_ref, acc_ref = refs[ZS + blocks // 2 :]
+    head_dim, query_count = out_ref.shape
     length, z_at = meta_ref[0], meta_ref[1]
     block_rows = ZS * rows
-    size = query_count // ZS
-    for at in range(ZS):
-        start = pl.multiple_of((z_at ^ at) * size, 128)
-        go_ref[:, pl.ds(start, size)] = piece_refs[at][...]
+    load_head(kv_refs, rows_ref, turned_ref, 0)
+    query = jnp.concatenate([ref[...] for ref in query_refs], axis=1)
+    grads = jnp.concatenate([ref[...] for ref in grad_refs], axis=1)
     blank = jnp.zeros((head_dim, query_count), BF16)
-    for block in range(blocks):
-        for part in range(ZS):
-            cut = slice(part * rows, (part + 1) * rows)
-            key_refs[block][:, cut] = kv_refs[block][cut, :].T[:head_dim, :]
-    grads = go_ref[...]
-    query = jnp.concatenate([q_ref[...], blank], axis=0)
+    query = jnp.concatenate([query, blank], axis=0)
     grad = jnp.concatenate([blank, grads], axis=0)
     qn_ref[...] = query.T
     gn_ref[...] = grad.T
@@ -169,26 +167,26 @@
     log_sum = log_ref[0]
     acc_ref[...] = jnp.zeros_like(acc_ref)
 
+    def put(block, start, value):
+        pairs[block // 2][pl.ds(start + (block & 1) * block_rows, rows), :] = value
+
     def step(group, members):
-        start = pl.multiple_of(group * rows, rows)
+        start = pl.multiple_of((group ^ z_at) * rows, rows)
         for block in members:
-            kv = kv_refs[block][pl.ds(start, rows), :]
+            kv = rows_ref[block, pl.ds(start, rows), :]
             place = (meta_ref[2 + block] + group * 4) * rows
             scores = matmul(with_mask(kv, place, length), query)
             prob_grad = matmul(kv, grad)
             prob = jnp.exp(scores - log_sum)
             score_grad = (prob * (prob_grad - delta)).astype(BF16)
-            pairs[block // 2][pl.ds(start + (block & 1) * block_rows, rows), :] = (
-                matmul(prob.astype(BF16), gn_ref[...]) + matmul(score_grad, qn_ref[...])
-            ).astype(BF16)
-            acc_ref[...] += matmul(key_refs[block][:, pl.ds(start, rows)], score_grad)
+            value = matmul(prob.astype(BF16), gn_ref[...]) + matmul(score_grad, qn_ref[...])
+            put(block, start, value.astype(BF16))
+            acc_ref[...] += matmul(turned_ref[block, :, pl.ds(start, rows)], score_grad)
 
     def clear(group, members):
-        start = pl.multiple_of(group * rows, rows)
+        start = pl.multiple_of((group ^ z_at) * rows, rows)
         for block in members:
-            pairs[block // 2][pl.ds(start + (block & 1) * block_rows, rows), :] = jnp.zeros(
-                (rows, 128), BF16
-            )
+            put(block, start, jnp.zeros((rows, 128), BF16))
 
     def loop(low, high, fn):
         def one(group, carry):
@@ -202,75 +200,268 @@
         count = touched_groups(length, rows, meta_ref[2 + first] // 16)
         loop(0, count, lambda g: step(g, members))
         loop(count, ZS, lambda g: clear(g, members))
-    dq_ref[...] = (acc_ref[...] * head_dim ** (-0.5)).astype(BF16)
-
-
-def attend_backward(meta, queries, grads, out, log_sum, kv_blocks, first, head_dim):
+    dq = (acc_ref[...] * head_dim ** (-0.5)).astype(BF16)
+    size = query_count // ZS
+    for at in range(ZS):
+        dq_refs[at][...] = dq[:, at * size : (at + 1) * size]
+
+
+def attend_backward(meta, queries, grads, out, log_sum, kv_blocks, first, count, made=()):
     blocks = len(kv_blocks)
-    block_rows, columns = kv_blocks[0].shape
+    half_rows, columns = kv_blocks[0][0].shape
     heads = columns // 128
-    query_count = queries.shape[1]
+    part, half_count = queries[0].shape
+    head_dim, query_count = part // heads, 2 * half_count
     size = query_count // ZS
-    head_rows = pl.BlockSpec((head_dim, query_count), lambda i, m: (i, 0))
+    piece = pl.BlockSpec((head_dim, size), lambda i, m: (i + first, 0))
+    ins = [
+        *queries,
+        out,
+        log_sum,
+        *grads,
+        *[item for pair in kv_blocks for item in pair],
+        *made,
+    ]
     return pl.pallas_call(
-        partial(backward_kernel, blocks=blocks, rows=block_rows // ZS),
+        partial(backward_kernel, blocks=blocks, rows=2 * half_rows // ZS, extra=len(made)),
         grid_spec=pltpu.PrefetchScalarGridSpec(
             num_scalar_prefetch=1,
-            grid=(heads,),
-            in_specs=[
+            grid=(count,),
+            in_specs=[pl.BlockSpec((head_dim, half_count), lambda i, m: (i + first, 0))] * 2
+            + [
                 pl.BlockSpec((head_dim, query_count), lambda i, m: (i + first, 0)),
-                head_rows,
-                pl.BlockSpec((1, 1, query_count), lambda i, m: (i, 0, 0)),
+                pl.BlockSpec((1, 1, query_count), lambda i, m: (i + first, 0, 0)),
             ]
-            + [pl.BlockSpec((head_dim, size), lambda i, m: (i + first, 0))] * ZS
-            + [pl.BlockSpec((block_rows, 128), lambda i, m: (0, i))] * blocks,
-            out_specs=[head_rows]
-            + [pl.BlockSpec((2 * block_rows, 128), lambda i, m: (0, i))] * (blocks // 2),
-            scratch_shapes=[pltpu.VMEM((head_dim, block_rows), BF16)] * blocks
-            + [
-                pltpu.VMEM((head_dim, query_count), BF16),
+            + [piece] * ZS
+            + [pl.BlockSpec((half_rows, 128), lambda i, m: (0, i + first))] * (2 * blocks)
+            + [pl.BlockSpec(memory_space=pl.ANY)] * len(made),
+            out_specs=[piece] * ZS
+            + [pl.BlockSpec((4 * half_rows, 128), lambda i, m: (0, i + first))] * (blocks // 2),
+            scratch_shapes=[
+                pltpu.VMEM((blocks, 2 * half_rows, 128), BF16),
+                pltpu.VMEM((blocks, head_dim, 2 * half_rows), BF16),
                 pltpu.VMEM((query_count, 128), BF16),
                 pltpu.VMEM((query_count, 128), BF16),
                 pltpu.VMEM((head_dim, query_count), F32),
             ],
         ),
-        out_shape=[jax.ShapeDtypeStruct((heads * head_dim, query_count), BF16)]
-        + [jax.ShapeDtypeStruct((2 * block_rows, columns), BF16)] * (blocks // 2),
+        out_shape=[jax.ShapeDtypeStruct((part, size), BF16)] * ZS
+        + [jax.ShapeDtypeStruct((4 * half_rows, columns), BF16)] * (blocks // 2),
+        input_output_aliases={
+            1 + len(ins) - len(made) + at: at for at in range(len(made))
+        },
         compiler_params=pltpu.CompilerParams(vmem_limit_bytes=48 << 20),
-        cost_estimate=work(12 * heads),
+        cost_estimate=work(12 * count),
         name="attend_backward",
-    )(meta, queries, out, log_sum, *grads, *kv_blocks)
-
-
-def project_kernel(tokens_ref, weight_ref, bias_ref, query_ref, *refs):
-    kv_refs, turned_ref = refs[:-1], refs[-1]
+    )(meta, *ins)
+
+
+IN_VMEM = pl.BlockSpec(memory_space=pltpu.VMEM)
+
+
+def small_call(kernel, meta, values, shapes, scratch=(), limit=32, name=None):
+    return pl.pallas_call(
+        kernel,
+        grid_spec=pltpu.PrefetchScalarGridSpec(
+            num_scalar_prefetch=1,
+            grid=(),
+            in_specs=[IN_VMEM] * len(values),
+            out_specs=[IN_VMEM] * len(shapes),
+            scratch_shapes=list(scratch),
+        ),
+        out_shape=[jax.ShapeDtypeStruct(shape, kind) for shape, kind in shapes],
+        compiler_params=pltpu.CompilerParams(vmem_limit_bytes=limit << 20),
+        cost_estimate=work(1),
+        name=name,
+    )(meta, *values)
+
+
+def fold_kernel(meta_ref, kept_ref, got_ref, keep_ref, sent_ref, sum_ref):
+    sum_ref[...] = (kept_ref[...].astype(F32) + got_ref[...].astype(F32)).astype(BF16)
+    rows = keep_ref.shape[0]
+    for at, ref in enumerate((keep_ref, sent_ref)):
+        start = pl.multiple_of((meta_ref[0] ^ at) * rows, 16)
+        ref[...] = sum_ref[pl.ds(start, rows), :]
+
+
+def fold(bit, kept, got):
+    rows, columns = kept.shape
+    half = ((rows // 2, columns), BF16)
+    return small_call(
+        fold_kernel,
+        bit,
+        (kept, got),
+        [half, half],
+        [pltpu.VMEM((rows, columns), BF16)],
+        name="fold",
+    )
+
+
+def unite_kernel(meta_ref, own_ref, got_ref, out_ref):
+    rows = own_ref.shape[0]
+    for at, ref in enumerate((own_ref, got_ref)):
+        start = pl.multiple_of((meta_ref[0] ^ at) * rows, 16)
+        out_ref[pl.ds(start, rows), :] = ref[...]
+
+
+def unite(bit, own, got):
+    rows, columns = own.shape
+    return small_call(
+        unite_kernel, bit, (own, got), [((2 * rows, columns), BF16)], name="unite"
+    )[0]
+
+
+def plus_kernel(meta_ref, one_ref, two_ref, out_ref, *, low):
+    cut = slice(low, low + out_ref.shape[0])
+    out_ref[...] = (one_ref[cut, :].astype(F32) + two_ref[cut, :].astype(F32)).astype(BF16)
+
+
+def plus(meta, one, two, low=0):
+    rows, columns = one.shape
+    return small_call(
+        partial(plus_kernel, low=low),
+        meta,
+        (one, two),
+        [((rows - low, columns), BF16)],
+        name="plus",
+    )[0]
+
+
+def prepare_kernel(meta_ref, *refs):
+    sources, refs = refs[:4], refs[4:]
+    low_ref, pack_ref, low_refs, head_ref = refs[0], refs[1], refs[2:5], refs[5]
+    places, sems = refs[6:10], refs[10]
+    copies = []
+    for at in range(4):
+        copies.append(pltpu.make_async_copy(sources[at], places[at], sems.at[at]))
+        copies[-1].start()
+    z_at, c_at = meta_ref[0], meta_ref[1]
+    width = places[0].shape[1]
+    part = width // ZS
+    head_dim = width // HEADS
+    copies[0].wait()
+    low_ref[...] = places[0][...].astype(BF16)
+    parts = []
+    for kind in range(3):
+        ref = places[kind + 1]
+        copies[kind + 1].wait()
+        value = ref[...]
+        low_refs[kind][...] = value.astype(BF16)
+        half = ref.shape[0] // 2
+        rows = ref[pl.ds(pl.multiple_of(c_at * half, half), half), :]
+        head_ref[kind * half : (kind + 1) * half, :] = rows.astype(BF16)
+        turn = lax.rem(width - z_at * part, width)
+        parts.append(pltpu.roll(value, turn, 1)[:, :part])
+    columns = []
+    for head in range(part // head_dim):
+        cut = slice(head * head_dim, (head + 1) * head_dim)
+        columns += [parts[1][:, cut], parts[2][:, cut]]
+    pack_ref[...] = jnp.concatenate(columns + [parts[0]], axis=1).astype(BF16)
+
+
+def prepare(meta, tokens, weights):
+    rows, width = tokens.shape
+    count = weights[0].shape[0]
+    shapes = [(rows, width), (count, 3 * width // ZS)] + [(count, width)] * 3
+    shapes.append((3 * count // 2, width))
+    return pl.pallas_call(
+        prepare_kernel,
+        grid_spec=pltpu.PrefetchScalarGridSpec(
+            num_scalar_prefetch=1,
+            grid=(),
+            in_specs=[pl.BlockSpec(memory_space=pltpu.MemorySpace.HBM)] * 4,
+            out_specs=[IN_VMEM] * len(shapes),
+            scratch_shapes=[pltpu.VMEM((rows, width), F32)]
+            + [pltpu.VMEM((count, width), F32)] * 3
+            + [pltpu.SemaphoreType.DMA((4,))],
+        ),
+        out_shape=[jax.ShapeDtypeStruct(shape, BF16) for shape in shapes],
+        compiler_params=pltpu.CompilerParams(vmem_limit_bytes=40 << 20),
+        cost_estimate=work(1),
+        name="prepare",
+    )(meta, tokens, *weights)
+
+
+def round_kernel(meta_ref, out_w, up_w, down_w, low_out, low_up, low_down, pack_ref):
+    core = meta_ref[1]
+    for source, target in ((out_w, low_out), (up_w, low_up), (down_w, low_down)):
+        target[...] = source[...].astype(BF16)
+    width = pack_ref.shape[1]
+    low = 0
+    half = out_w.shape[0] // 2
+    rows = pl.ds(pl.multiple_of(core * half, half), half)
+    pack_ref[low : low + half, :] = out_w[rows, :].astype(BF16)
+    low += half
+    count = up_w.shape[1] // 2
+    for block in range(count // width):
+        lanes = pl.ds(pl.multiple_of(core * count + block * width, 128), width)
+        pack_ref[low : low + up_w.shape[0], :] = up_w[:, lanes].astype(BF16)
+        low += up_w.shape[0]
+    half = down_w.shape[0] // 2
+    rows = pl.ds(pl.multiple_of(core * half, half), half)
+    pack_ref[low : low + half, :] = down_w[rows, :].astype(BF16)
+
+
+def round_weights(meta, weights):
+    out_w, up_w, down_w = weights
+    width = out_w.shape[1]
+    total = out_w.shape[0] // 2 + up_w.shape[0] * (up_w.shape[1] // 2 // width)
+    total += down_w.shape[0] // 2
+    return small_call(
+        round_kernel,
+        meta,
+        weights,
+        [(item.shape, BF16) for item in weights] + [((total, width), BF16)],
+        limit=48,
+        name="round_weights",
+    )
+
+
+def project_kernel(meta_ref, first_ref, second_ref, *refs, shared):
+    query_ref, kv_ref, turned_ref, token_ref, bias_ref = refs[-5:]
     part = query_ref.shape[0]
-    tokens = tokens_ref[...]
+    rows, width = first_ref.shape
     split = 2 * part
-    kv = matmul(tokens, weight_ref[:, :split]) + bias_ref[:, :split]
-    kv = kv.astype(BF16)
-    low = 0
-    for ref in kv_refs:
-        ref[...] = kv[:, low : low + ref.shape[1]]
-        low += ref.shape[1]
-    query = matmul(tokens, weight_ref[:, split:]) + bias_ref[:, split:]
+    token_ref[:rows, :] = first_ref[...]
+    token_ref[rows:, :] = second_ref[...]
+    if shared:
+        w_at, z_at = meta_ref[0], meta_ref[1]
+        both = None
+        bias_ref[...] = jnp.zeros_like(bias_ref)
+        for at in range(2):
+            count = refs[at].shape[0]
+            cut = pl.ds(pl.multiple_of((w_at ^ at) * count, 128), count)
+            term = matmul(token_ref[:, cut], refs[at][...])
+            both = term if both is None else both + term
+            bias_ref[0:2, cut] = refs[2 + at][0:2, :].astype(F32)
+        turn = lax.rem(width - z_at * part, width)
+        bias = pltpu.roll(bias_ref[...], turn, 1)[:, :part]
+        head_dim = width // HEADS
+        pieces = []
+        for head in range(part // head_dim):
+            pieces.append(jnp.zeros((1, head_dim), F32))
+            pieces.append(bias[1:2, head * head_dim : (head + 1) * head_dim])
+        both = both + jnp.concatenate(pieces + [bias[0:1, :]], axis=1)
+    else:
+        both = matmul(token_ref[...], refs[0][...]) + refs[1][...]
+    kv_ref[...] = both[:, :split].astype(BF16)
     scale = (part * ZS // HEADS) ** (-0.5)
-    query_ref[...] = (query.astype(BF16) * jnp.array(scale, BF16)).T
-    turned_ref[...] = tokens.T
-
-
-def project(tokens, weight, bias, counts):
-    rows, width = tokens.shape
-    part = weight.shape[1] // 3
-    return pl.pallas_call(
-        project_kernel,
-        out_shape=[jax.ShapeDtypeStruct((part, rows), BF16)]
-        + [jax.ShapeDtypeStruct((rows, 128 * count), BF16) for count in counts]
-        + [jax.ShapeDtypeStruct((width, rows), BF16)],
-        compiler_params=pltpu.CompilerParams(vmem_limit_bytes=40 << 20),
-        cost_estimate=work(2),
+    query_ref[...] = (both[:, split:].astype(BF16) * jnp.array(scale, BF16)).T
+    turned_ref[...] = token_ref[...].T
+
+
+def project(meta, first, second, sources):
+    rows, width = first.shape
+    part = sources[0].shape[1] // 3
+    return small_call(
+        partial(project_kernel, shared=len(sources) == 4),
+        meta,
+        (first, second, *sources),
+        [((part, 2 * rows), BF16), ((2 * rows, 2 * part), BF16), ((width, 2 * rows), BF16)],
+        [pltpu.VMEM((2 * rows, width), BF16), pltpu.VMEM((8, width), F32)],
+        limit=40,
         name="project",
-    )(tokens, weight, bias)
+    )
 
 
 def middle_kernel(meta_ref, tokens_ref, seed_ref, vec_ref, upoff_ref, *refs, groups, shared):
@@ -575,79 +766,152 @@
     )(meta, keep, send, got, own_small, got_small)
 
 
-def head_kernel(meta_ref, turned_ref, *refs, count):
-    query_refs, kv_refs = refs[:count], refs[count : 2 * count]
-    refs = refs[2 * count :]
-    block = turned_ref.shape[0]
+def key_sum_kernel(own_ref, core_ref, got_ref, *out_refs):
+    size = out_refs[0].shape[1]
+    for at, ref in enumerate(out_refs):
+        cut = slice(at * size, (at + 1) * size)
+        kept = (own_ref[cut, :].astype(F32) + core_ref[cut, :].astype(F32)).astype(BF16)
+        ref[...] = (kept.astype(F32) + got_ref[cut, :].astype(F32)).astype(BF16).T
+
+
+def key_sum(own, core, got):
+    rows, columns = got.shape
+    half = pl.BlockSpec((rows, columns), lambda i: (0, 0))
+    return pl.pallas_call(
+        key_sum_kernel,
+        grid=(1,),
+        in_specs=[half] * 3,
+        out_specs=[pl.BlockSpec((columns, rows // ZS), lambda i: (0, 0))] * ZS,
+        out_shape=[jax.ShapeDtypeStruct((columns, rows // ZS), BF16)] * ZS,
+        compiler_params=pltpu.CompilerParams(vmem_limit_bytes=24 << 20),
+        cost_estimate=work(2),
+        name="key_sum",
+    )(own, core, got)
+
+
+def head_kernel(meta_ref, *refs):
+    turned_refs, query_refs, kv_refs = refs[:2], refs[2 : 2 + ZS], refs[2 + ZS : 2 + 2 * ZS]
+    refs = refs[2 + 2 * ZS :]
     out_ref = refs[-1]
-
-    def put(value, rows, low):
-        columns = slice(low, low + value.shape[1])
+    block = turned_refs[0].shape[0]
+
+    def put(value, rows):
         if len(refs) == 2:
-            value = value + refs[0][rows, columns].astype(F32)
-        out_ref[rows, columns] = value.astype(BF16)
-        return low + value.shape[1]
-
-    query = jnp.concatenate([ref[...] for ref in query_refs], axis=0)
-    turned = turned_ref[...]
+            value = value + refs[0][rows, :].astype(F32)
+        out_ref[rows, :] = value.astype(BF16)
+
+    grads = [jnp.concatenate([ref[...] for ref in items], axis=1) for items in (query_refs, kv_refs)]
+    grads = jnp.concatenate(grads, axis=0)
+    turned = jnp.concatenate([ref[...] for ref in turned_refs], axis=1)
+    put(right_trans(turned, grads), slice(0, block))
     ones = jnp.ones((16, turned.shape[1]), BF16)
-    for left, rows in ((turned, slice(0, block)), (ones, slice(block, block + 16))):
-        low = 0
-        for ref in kv_refs:
-            low = put(matmul(left, ref[...]), rows, low)
-        put(right_trans(left, query), rows, low)
-
-
-def head_slab(meta, turned, query, kv, count, got=None):
-    width, rows = turned.shape
+    put(right_trans(ones, grads), slice(block, block + 16))
+
+
+def head_slab(meta, turned, query, kv, count, slabs, got=None, first=0):
+    width, rows = turned[0].shape
     block = width // count
-    columns = 3 * width // ZS
-    whole = pl.BlockSpec((block + 16, columns), lambda i, m: (0, 0))
+    columns = query[0].shape[0] + kv[0].shape[0]
     return pl.pallas_call(
-        partial(head_kernel, count=len(query)),
+        head_kernel,
         grid_spec=pltpu.PrefetchScalarGridSpec(
             num_scalar_prefetch=1,
-            grid=(1,),
-            in_specs=[pl.BlockSpec((block, rows), lambda i, m: (m[0] * 2 + m[1], 0))]
+            grid=(slabs,),
+            in_specs=[pl.BlockSpec((block, rows), lambda i, m: (m[i] * 2 + m[slabs], 0))] * 2
             + [pl.BlockSpec(item.shape, lambda i, m: (0, 0)) for item in [*query, *kv]]
-            + ([] if got is None else [whole]),
-            out_specs=whole,
+            + (
+                []
+                if got is None
+                else [pl.BlockSpec((block + 16, columns), lambda i, m: (first + i, 0))]
+            ),
+            out_specs=pl.BlockSpec((block + 16, columns), lambda i, m: (i, 0)),
         ),
-        out_shape=jax.ShapeDtypeStruct((block + 16, columns), BF16),
+        out_shape=jax.ShapeDtypeStruct((slabs * (block + 16), columns), BF16),
         compiler_params=pltpu.CompilerParams(vmem_limit_bytes=24 << 20),
         cost_estimate=work(2),
         name="head_slab",
-    )(meta, turned, *query, *kv, *(() if got is None else (got,)))
-
-
-def token_kernel(*refs, count):
-    query_refs, kv_refs = refs[:count], refs[count : 2 * count]
-    weight_ref, out_ref = refs[2 * count :]
-    kv = jnp.concatenate([ref[...] for ref in kv_refs], axis=1)
-    query = jnp.concatenate([ref[...] for ref in query_refs], axis=0).T
-    split = kv.shape[1]
-    out_ref[...] = (
-        right_trans(kv, weight_ref[:, :split]) + right_trans(query, weight_ref[:, split:])
-    ).astype(BF16)
-
-
-def token_part(query, kv, weight):
+    )(meta, *turned, *query, *kv, *(() if got is None else (got,)))
+
+
+def token_kernel(meta_ref, resid_ref, *refs, shared):
+    query_refs, kv_refs, refs = refs[:ZS], refs[ZS : 2 * ZS], refs[2 * ZS :]
+    weight_refs, refs = refs[: 5 if shared else 3], refs[5 if shared else 3 :]
+    out_ref, full_ref, turned_ref, sems = refs
+    w_at, c_at, z_at = meta_ref[1], meta_ref[2], meta_ref[3]
+    width = full_ref.shape[1]
+    moves = []
+    if shared:
+        count = weight_refs[0].shape[0]
+        half = count // 2
+        for kind in range(3):
+            start = pl.multiple_of(w_at * count, count)
+            moves.append((weight_refs[kind], full_ref.at[kind, pl.ds(start, count), :]))
+            for ref, core in ((weight_refs[3], c_at), (weight_refs[4], 1 - c_at)):
+                start = pl.multiple_of(((1 - w_at) * 2 + core) * half, half)
+                moves.append(
+                    (
+                        ref.at[pl.ds(kind * half, half), :],
+                        full_ref.at[kind, pl.ds(start, half), :],
+                    )
+                )
+    else:
+        for kind in range(3):
+            moves.append((weight_refs[kind], full_ref.at[kind]))
+    copies = []
+    for at, (source, target) in enumerate(moves):
+        copies.append(pltpu.make_async_copy(source, target, sems.at[at]))
+        copies[-1].start()
+    part = width // ZS
+    head_dim = width // HEADS
+    for at in range(ZS):
+        low = (z_at ^ at) * part
+        turned_ref[0, pl.ds(pl.multiple_of(low, part), part), :] = query_refs[at][...]
+        for head in range(part // head_dim):
+            start = pl.ds(pl.multiple_of(low + head * head_dim, head_dim), head_dim)
+            for kind in (1, 2):
+                row = (2 * head + kind - 1) * head_dim
+                turned_ref[kind, start, :] = kv_refs[at][row : row + head_dim, :]
+    parts = [turned_ref[kind].T for kind in range(3)]
+    for copy in copies:
+        copy.wait()
+    out = resid_ref[...]
+    for kind in range(3):
+        out = out + right_trans(parts[kind], full_ref[kind])
+    out_ref[...] = out
+
+
+def token_gradient(meta, resid, query, kv, weights):
+    rows, width = resid.shape
+    in_vmem = pl.BlockSpec(memory_space=pltpu.VMEM)
+    in_place = pl.BlockSpec(memory_space=pl.ANY)
     return pl.pallas_call(
-        partial(token_kernel, count=len(query)),
-        out_shape=jax.ShapeDtypeStruct((kv[0].shape[0], weight.shape[0]), BF16),
+        partial(token_kernel, shared=len(weights) == 5),
+        grid_spec=pltpu.PrefetchScalarGridSpec(
+            num_scalar_prefetch=1,
+            grid=(),
+            in_specs=[in_vmem] * (1 + 2 * ZS) + [in_place] * len(weights),
+            out_specs=in_vmem,
+            scratch_shapes=[
+                pltpu.VMEM((3, width, width), BF16),
+                pltpu.VMEM((3, width, rows), BF16),
+                pltpu.SemaphoreType.DMA((9,)),
+            ],
+        ),
+        out_shape=jax.ShapeDtypeStruct((rows, width), F32),
         compiler_params=pltpu.CompilerParams(vmem_limit_bytes=32 << 20),
-        cost_estimate=work(2),
-        name="token_part",
-    )(*query, *kv, weight)
+        cost_estimate=work(4),
+        name="token_gradient",
+    )(meta, resid, *query, *kv, *weights)
 
 
 def down_finish_kernel(meta_ref, *refs):
-    block = refs[0].shape[0]
+    block = refs[0].shape[0] // 4
     c_at, x_at = meta_ref[0], meta_ref[1]
     for at in range(4):
-        place = (c_at ^ (at >> 1)) * 2 + (x_at ^ (at & 1))
-        start = pl.multiple_of(place * block, 8)
-        refs[4][pl.ds(start, block), :] = refs[at][...].astype(F32)
+        for z in range(4):
+            place = (c_at ^ (at >> 1)) * 8 + z * 2 + (x_at ^ (at & 1))
+            start = pl.multiple_of(place * block, 8)
+            refs[4][pl.ds(start, block), :] = refs[at][z * block : (z + 1) * block, :].astype(F32)
 
 
 def down_finish(meta, pieces):
@@ -706,19 +970,20 @@
 
 
 def head_finish_kernel(meta_ref, own_ref, got_ref, query_ref, key_ref, value_ref, bias_ref, *, part):
-    block = own_ref.shape[1] - 16
+    size = own_ref.shape[0] // ZS
+    block = size - 16
     head_dim = part // 3
     for at, source in enumerate((own_ref, got_ref)):
         start = pl.multiple_of((meta_ref[0] ^ at) * block, 8)
         rows = pl.ds(start, block)
         keys, values, queries = [], [], []
         for z in range(ZS):
-            item = source[(z & 1) * 2 + (z >> 1)].astype(F32)
+            item = source[((z & 1) * 2 + (z >> 1)) * size :][:size].astype(F32)
             for head in range(3):
-                low = head * 2 * head_dim
+                low = part + head * 2 * head_dim
                 keys.append(item[:, low : low + head_dim])
                 values.append(item[:, low + head_dim : low + 2 * head_dim])
-            queries.append(item[:, 2 * part :])
+            queries.append(item[:, :part])
         key = jnp.concatenate(keys, axis=1)
         value = jnp.concatenate(values, axis=1)
         query = jnp.concatenate(queries, axis=1)
@@ -731,21 +996,17 @@
 
 
 def head_finish(meta, own, got):
-    _, block, columns = own.shape
-    rows = 2 * (block - 16)
+    rows, columns = own.shape
+    rows = 2 * (rows // ZS - 16)
     width = ZS * columns // 3
-    in_vmem = pl.BlockSpec(memory_space=pltpu.VMEM)
-    return pl.pallas_call(
+    return small_call(
         partial(head_finish_kernel, part=columns // 3),
-        grid_spec=pltpu.PrefetchScalarGridSpec(
-            num_scalar_prefetch=1, grid=(), in_specs=[in_vmem] * 2, out_specs=[in_vmem] * 4
-        ),
-        out_shape=[jax.ShapeDtypeStruct((rows, width), F32)] * 3
-        + [jax.ShapeDtypeStruct((16, width), F32)],
-        compiler_params=pltpu.CompilerParams(vmem_limit_bytes=40 << 20),
-        cost_estimate=work(4),
+        meta,
+        (own, got),
+        [((rows, width), F32)] * 3 + [((16, width), F32)],
+        limit=40,
         name="head_finish",
-    )(meta, own, got)
+    )
 
 
 def in_order(index, own, other, axis):
@@ -798,22 +1059,26 @@
 
     hold = lax.optimization_barrier
 
-    def head_slice(weight):
-        return lax.dynamic_slice_in_dim(weight, z_at * part, part, 1).astype(BF16)
-
-    low_tokens = tokens.astype(BF16)
-    token_all = lax.all_gather(low_tokens, "z", axis=0, tiled=True)
+    near = ((0, 1), (1, 0), (2, 3), (3, 2))
+    far = ((0, 2), (2, 0), (1, 3), (3, 1))
+    cross = ((0, 3), (3, 0), (1, 2), (2, 1))
+
+    def exchange(pieces):
+        return [pieces[0]] + [
+            lax.ppermute(item, "z", perm) for item, perm in zip(pieces[1:], (near, far, cross))
+        ]
+
     own_rows = query_weight.shape[0]
-    key_own = head_slice(key_weight)
-    value_own = head_slice(value_weight)
-    own_kv = []
-    for head in range(heads):
-        cut = slice(head * head_dim, (head + 1) * head_dim)
-        own_kv += [key_own[:, cut], value_own[:, cut]]
-    attn_own = jnp.concatenate(own_kv + [head_slice(query_weight)], axis=1)
-    small = jnp.concatenate(
+    big_weights = (output_weight, up_weight, down_weight)
+    sides = jnp.stack([z_at, c_at]).astype(jnp.int32)
+    low_tokens, attn_own, *low_heads, head_pack = prepare(
+        sides, tokens, (query_weight, key_weight, value_weight)
+    )
+    line_tokens = [low_tokens, lax.ppermute(low_tokens, "z", near)]
+    line_tokens.append(lax.ppermute(low_tokens, "z", far))
+    small = jnp.stack(
         [
-            item.astype(BF16)
+            item.reshape(-1, own_rows)[row]
             for item in (
                 query_bias,
                 value_bias,
@@ -825,77 +1090,64 @@
                 second_shift,
                 up_bias,
             )
+            for row in range(item.shape[0] // own_rows)
         ]
-    ).reshape(-1, 3 * part)
-    attn_pack = jnp.concatenate([attn_own, small], axis=0)
+    ).astype(BF16)
     if count_w == 2:
-        attn_got = swap(attn_pack, "w")
-        attn_full = in_order(w_at, attn_own, attn_got[:own_rows], 0)
-        small_all = in_order(w_at, small[None], attn_got[None, own_rows:], 0)
+        attn_got, small_got = swap(attn_own, "w"), swap(small, "w")
+        *low_weights, weight_pack = round_weights(sides, big_weights)
+        attn_got, small_got, weight_pack, *line_tokens[1:3] = hold(
+            (attn_got, small_got, weight_pack, *line_tokens[1:3])
+        )
+        weight_got = swap(weight_pack, "w")
+        sources = (attn_own, attn_got, small, small_got)
     else:
-        attn_all = lax.all_gather(attn_pack, "w", axis=0, tiled=False)
-        attn_full = attn_all[:, :own_rows].reshape(width, 3 * part)
-        small_all = attn_all[:, own_rows:]
-    small_all = small_all.astype(F32).reshape(count_w, -1, own_rows)
-    vec = jnp.transpose(small_all[:, :8], (1, 0, 2)).reshape(8, width)
-    up_offset = small_all[:, 8:].reshape(1, -1)
-    attn_pack, output_weight, up_weight, down_weight = hold(
-        (attn_pack, output_weight, up_weight, down_weight)
-    )
-    low_weights = [item.astype(BF16) for item in (output_weight, up_weight, down_weight)]
-    low_out, low_up, low_down = low_weights
-    if count_w == 2:
-        up_half = part_of(low_up, c_at, 2, 1)
-        weight_pack = jnp.concatenate(
-            [part_of(low_out, c_at, 2, 0)]
-            + [up_half[:, at : at + width] for at in range(0, up_half.shape[1], width)]
-            + [part_of(low_down, c_at, 2, 0)],
-            axis=0,
-        )
-        attn_got, weight_pack = hold((attn_got, weight_pack))
-        weight_got = swap(weight_pack, "w")
-    else:
+        attn_full = lax.all_gather(attn_own, "w", axis=0, tiled=True)
+        small_all = lax.all_gather(small, "w", axis=0, tiled=False)
+        low_weights = [item.astype(BF16) for item in big_weights]
         weight_got = [lax.all_gather(item, "w", axis=0, tiled=True) for item in low_weights]
-
-    own_bias = lax.dynamic_slice_in_dim(vec[:2], z_at * part, part, 1)
-    value_bias_own = own_bias[1].reshape(heads, 1, head_dim)
-    kv_bias = jnp.concatenate([jnp.zeros_like(value_bias_own), value_bias_own], axis=1)
-    bias_row = jnp.concatenate([kv_bias.reshape(1, 2 * part), own_bias[:1]], axis=1)
-    groups = ((0, heads),)
-    queries, *key_values, turned = project(
-        token_all, attn_full, bias_row, [count for _, count in groups]
-    )
+        head_weights = [lax.all_gather(item, "w", axis=0, tiled=True) for item in low_heads]
+        pair = jnp.transpose(small_all[:, :2], (1, 0, 2)).reshape(2, width).astype(F32)
+        own_bias = lax.dynamic_slice_in_dim(pair, z_at * part, part, 1)
+        value_bias_own = own_bias[1].reshape(heads, 1, head_dim)
+        kv_bias = jnp.concatenate([jnp.zeros_like(value_bias_own), value_bias_own], axis=1)
+        bias_row = jnp.concatenate([kv_bias.reshape(1, 2 * part), own_bias[:1]], axis=1)
+        sources = (attn_full, bias_row)
+
+    line_tokens.append(lax.ppermute(line_tokens[2], "z", near))
+    corner = jnp.stack([w_at, z_at]).astype(jnp.int32)
+    made = [project(corner, *line_tokens[:2], sources)]
+    made[0], *line_tokens[2:] = hold((made[0], *line_tokens[2:]))
+    made.append(project(corner, *line_tokens[2:], sources))
+    queries = [item[0] for item in made]
+    turned = [item[2] for item in made]
+    kv_blocks = [[item[1] for item in made]]
+    for axis in ("x", "c", "o")[: 3 if count_o == 2 else 2]:
+        kv_blocks = kv_blocks + [[swap(item, axis) for item in pair] for pair in kv_blocks]
     places = []
     for at in range(4 * count_o):
         o_of = o_at ^ (at >> 2)
         places.append(o_of * 16 + (x_at ^ (at & 1)) * 2 + (c_at ^ ((at >> 1) & 1)))
     meta = jnp.stack([length, z_at] + places).astype(jnp.int32)
-    near = ((0, 1), (1, 0), (2, 3), (3, 2))
-    far = ((0, 2), (2, 0), (1, 3), (3, 1))
-    cross = ((0, 3), (3, 0), (1, 2), (2, 1))
-
-    def exchange(pieces):
-        return [pieces[0]] + [
-            lax.ppermute(item, "z", perm) for item, perm in zip(pieces[1:], (near, far, cross))
-        ]
-
-    kv_groups = []
-    for item in key_values:
-        kv_blocks = [item]
-        for axis in ("x", "c", "o")[: 3 if count_o == 2 else 2]:
-            kv_blocks = kv_blocks + [swap(item, axis) for item in kv_blocks]
-        kv_groups.append(kv_blocks)
-    attended, mixed, logs = [], [], []
-    for (first, _), kv_blocks in zip(groups, kv_groups):
-        out, *made = attend_forward(meta, queries, kv_blocks, first, head_dim)
-        attended.append(out)
-        mixed.append(exchange(made[:ZS]))
-        logs.append(made[ZS])
+    kv_blocks = [
+        [pltpu.with_memory_space_constraint(item, pltpu.MemorySpace.HBM) for item in pair]
+        for pair in kv_blocks
+    ]
+    attended, *made = attend_forward(meta, queries, kv_blocks, heads)
+    logs = made[ZS]
     if count_w == 2:
-        attended[0], weight_got = hold((attended[0], weight_got))
+        attended, weight_got, head_pack, small_own, small_got = hold(
+            (attended, weight_got, head_pack, small, small_got)
+        )
+        small_all = in_order(w_at, small_own[None], small_got[None], 0)
         weights = [*low_weights, weight_got, swap(weight_got, "c")]
+        head_got = swap(head_pack, "w")
     else:
         weights = weight_got
+    mixed = exchange(made[:ZS])
+    small_all = small_all.astype(F32)
+    vec = jnp.transpose(small_all[:, :8], (1, 0, 2)).reshape(8, width)
+    up_offset = small_all[:, 8:].reshape(1, -1)
 
     split = count_w == 2 and count_o == 1
     my_index = o_at * 16 + z_at * 4 + x_at * 2 + c_at
@@ -903,19 +1155,20 @@
     core = c_at if split else jnp.zeros_like(c_at)
     spots = jnp.stack([rest, w_at, core, z_at]).astype(jnp.int32)
     outputs, resid_grad, *made = middle(
-        spots, mixed, groups, tokens, cotangent[0], vec, up_offset, weights
+        spots, [mixed], ((0, heads),), tokens, cotangent[0], vec, up_offset, weights
     )
     head_grads = exchange(made[:ZS])
     send, keep, small_own = made[ZS:]
     hidden = up_offset.shape[1]
 
+    near_bit, far_bit = z_at & 1, z_at >> 1
+
     def add_pair(kept, got):
         return (kept.astype(F32) + got.astype(F32)).astype(BF16)
 
-    def unite(value, got, bit):
+    def join(value, got, bit):
         return in_order(bit, value, got, 0)
 
-    near_bit, far_bit = z_at & 1, z_at >> 1
     spot = jnp.stack([c_at, x_at]).astype(jnp.int32)
     token = [spot]
 
@@ -923,16 +1176,9 @@
         token[0], *values = hold((token[0], *values))
         return values[0] if len(values) == 1 else values
 
-    def backward(at):
+    def backward(first, count, made=()):
         return attend_backward(
-            meta,
-            queries,
-            head_grads,
-            attended[at],
-            logs[at],
-            kv_groups[at],
-            groups[at][0],
-            head_dim,
+            meta, queries, head_grads, attended, logs, kv_blocks, first, count, made
         )
 
     def to_near(value):
@@ -941,8 +1187,9 @@
     def to_far(value):
         return lax.ppermute(value, "z", far)
 
-    def head_part(at, got=None):
-        return head_slab(at, turned, [query_low], [kv_low], 2 * count_w, got)
+    def head_part(ws, core, got=None, first=0):
+        at = jnp.stack([jnp.asarray(item) for item in (*ws, core)]).astype(jnp.int32)
+        return head_slab(at, turned, query_low, kv_low, 2 * count_w, len(ws), got, first)
 
     def pick(w, c):
         return jnp.stack([jnp.asarray(w), jnp.asarray(c)]).astype(jnp.int32)
@@ -957,80 +1204,92 @@
         down_far, up_sent, down_near, *head_grads = hold(
             (down_far, up_sent, down_near, *head_grads)
         )
-        query_low, *pairs = backward(0)
-        down_got, up_got, query_low, *pairs = arrive(
-            swap(down_far, "w"), swap(up_sent, "x"), query_low, *pairs
+        made = backward(0, heads - 1)
+        down_got, *made = arrive(swap(down_far, "w"), *made)
+        down_sum = add_pair(down_near, down_got)
+        down_got = to_near(part_of(down_sum, 1 - near_bit, 2, 0))
+        down_sum, *head_grads = arrive(down_sum, *head_grads)
+        made = backward(heads - 1, 1, made)
+        down_got, up_got, head_got, *made = arrive(
+            down_got, swap(up_sent, "x"), head_got, *made
         )
+        query_low, pairs = made[:ZS], made[ZS:]
+        head_weights = [*low_heads, head_got, swap(head_got, "c")]
         pair_got = swap(pairs[1], "c")
-        down_sum = add_pair(down_near, down_got)
-        down_got = swap(part_of(down_sum, 1 - x_at, 2, 0), "x")
+        query_got = exchange(query_low)
+        down_sum = add_pair(part_of(down_sum, near_bit, 2, 0), down_got)
+        down_got = to_far(part_of(down_sum, 1 - far_bit, 2, 0))
         up_sum = add_pair(up_kept, up_got).reshape(2, own_rows // 2, -1)
         up_got = swap(lax.dynamic_index_in_dim(up_sum, 1 - w_at, 0, keepdims=False), "w")
         pair_got = arrive(pair_got)
         half_rows = pair_got.shape[0] // 2
         pair_sent = add_pair(pairs[0][half_rows:], pair_got[half_rows:])
-        pair_kept = add_pair(pairs[0][:half_rows], pair_got[:half_rows])
-        pair_sent, pair_kept = arrive(pair_sent, pair_kept)
-        pair_got = swap(pair_sent, "x")
+        pair_sent = arrive(pair_sent)
+        key_got = swap(pair_sent, "x")
         down_got = arrive(down_got)
-        down_sum = add_pair(part_of(down_sum, x_at, 2, 0), down_got)
-        down_got = to_near(part_of(down_sum, 1 - near_bit, 2, 0))
+        down_sum = add_pair(part_of(down_sum, far_bit, 2, 0), down_got)
+        down_got = swap(part_of(down_sum, 1 - x_at, 2, 0), "x")
         up_got = arrive(up_got)
         up_sum = add_pair(lax.dynamic_index_in_dim(up_sum, w_at, 0, keepdims=False), up_got)
         up_got = to_near(part_of(up_sum, 1 - near_bit, 2, 0))
+        key_got, *query_got = arrive(key_got, *query_got)
+        kv_low = key_sum(pairs[0], pair_got, key_got)
+        head_far = swap(head_part((1 - w_at,), 1 - c_at), "c")
+        kv_got = exchange(kv_low)
+        head_near = swap(head_part((1 * w_at,), 1 - c_at), "c")
         down_got = arrive(down_got)
-        down_sum = add_pair(part_of(down_sum, near_bit, 2, 0), down_got)
-        down_got = to_far(part_of(down_sum, 1 - far_bit, 2, 0))
+        down_sum = add_pair(part_of(down_sum, x_at, 2, 0), down_got)
+        down_got = to_far(down_sum)
+        head_far = arrive(head_far)
+        head_sent = swap(head_part((1 - w_at,), c_at, head_far), "w")
+        head_near = arrive(head_near)
+        head_sum = head_part((1 * w_at,), c_at, head_near)
         up_got = arrive(up_got)
         up_sum = add_pair(part_of(up_sum, near_bit, 2, 0), up_got)
         up_got = to_far(part_of(up_sum, 1 - far_bit, 2, 0))
-        down_got = arrive(down_got)
-        down_sum = add_pair(part_of(down_sum, far_bit, 2, 0), down_got)
-        down_got = to_far(down_sum)
-        pair_got = arrive(pair_got)
-        kv_low = add_pair(pair_kept, pair_got)
-        token_sum = token_part([query_low], [kv_low], attn_full)
-        token_grad = lax.psum_scatter(token_sum, "z", scatter_dimension=0, tiled=True)
-        head_far = swap(head_part(pick(1 - w_at, 1 - c_at)), "c")
-        head_near = swap(head_part(pick(1 * w_at, 1 - c_at)), "c")
-        head_far = arrive(head_far)
-        head_sent = swap(head_part(pick(1 - w_at, c_at), head_far), "w")
-        head_near = arrive(head_near)
-        head_sum = head_part(pick(1 * w_at, c_at), head_near)
+        head_sent = arrive(head_sent)
+        head_sum = add_pair(head_sum, head_sent)
+        head_got = swap(head_sum, "x")
+        kv_got = arrive(*kv_got)
+        input_grad = token_gradient(
+            spots, resid_grad, query_got, kv_got, head_weights
+        )
         up_got = arrive(up_got)
         up_sum = add_pair(part_of(up_sum, far_bit, 2, 0), up_got)
         up_got = to_far(up_sum)
         down_got = arrive(down_got)
-        down_sum = unite(down_sum, down_got, far_bit)
+        down_sum = join(down_sum[None], down_got[None], far_bit)
         down_got = to_near(down_sum)
-        head_sent = arrive(head_sent)
-        head_sum = add_pair(head_sum, head_sent)
-        head_got = swap(head_sum, "x")
-        up_got = arrive(up_got)
-        up_sum = unite(up_sum, up_got, far_bit)
-        up_got = to_near(up_sum)
-        down_got = arrive(down_got)
-        down_sum = unite(down_sum, down_got, near_bit)
-        down_x = swap(down_sum, "x")
-        down_c = swap(down_sum, "c")
         head_got = arrive(head_got)
         head_sum = add_pair(head_sum, head_got)
         head_got = to_far(head_sum)
         up_got = arrive(up_got)
-        up_sum = unite(up_sum, up_got, near_bit)
+        up_sum = join(up_sum, up_got, far_bit)
+        up_got = to_near(up_sum)
+        down_got = arrive(down_got)
+        down_sum = join(down_sum[None], down_got[None], near_bit)
+        down_sum = down_sum.reshape(-1, width)
+        down_x = swap(down_sum, "x")
+        down_c = swap(down_sum, "c")
+        head_got = arrive(head_got)
+        head_two = join(head_sum, head_got, far_bit)
+        head_got = to_near(head_two)
+        up_got = arrive(up_got)
+        up_sum = join(up_sum, up_got, near_bit)
         up_x = swap(up_sum, "x")
         up_c = swap(up_sum, "c")
-        down_x = arrive(down_x)
+        down_x, input_grad = arrive(down_x, input_grad)
         down_pieces = [down_sum, down_x, down_c, swap(down_x, "c")]
         head_got = arrive(head_got)
-        head_two = unite(head_sum[None], head_got[None], far_bit)
-        head_got = to_near(head_two)
+        head_four = join(head_two, head_got, near_bit)
+        head_other = swap(head_four, "c")
         total_down = down_finish(spot, down_pieces)
-        up_x = arrive(up_x)
+        up_x, total_down = arrive(up_x, total_down)
         up_pieces = [up_sum, up_x, up_c, swap(up_x, "c")]
-        head_got = arrive(head_got)
-        head_four = unite(head_two, head_got, near_bit)
-        head_other = swap(head_four, "c")
+        total_query, total_key, total_value, head_bias = head_finish(
+            spot, head_four, head_other
+        )
+        total_query, total_key, total_value = arrive(total_query, total_key, total_value)
         total_up, total_out, table = up_finish(token[0], up_pieces, hidden, width)
         groups = own_rows // 128
         small_total = table[: 8 * groups].reshape(groups, 8, 128)
@@ -1038,24 +1297,37 @@
         lines = hidden // count_w // 128
         total_up_bias = table[8 * groups : 8 * groups + lines].reshape(-1)
     else:
-        query_low, *pairs = backward(0)
+        made = backward(0, heads)
+        query_low, pairs = made[:ZS], made[ZS:]
         if count_o == 2:
-            pairs = [add_pair(pairs[at], swap(pairs[at + 2], "o")) for at in range(2)]
-        pair = add_pair(pairs[0], swap(pairs[1], "c"))
-        half_rows = pair.shape[0] // 2
-        kv_low = add_pair(pair[:half_rows], swap(pair[half_rows:], "x"))
-        token_sum = token_part([query_low], [kv_low], attn_full)
-        token_grad = lax.psum_scatter(token_sum, "z", scatter_dimension=0, tiled=True)
-        got = [swap(head_part(pick(w, 1 - c_at)), "c") for w in range(count_w)]
-        slabs = [head_part(pick(w, c_at), got[w]) for w in range(count_w)]
-        slabs = jnp.stack(slabs)
-        head_sum = lax.psum_scatter(slabs, "w", scatter_dimension=0, tiled=True)[0]
-        head_sum = add_pair(head_sum, swap(head_sum, "x"))
+            pairs = [plus(spot, pairs[at], swap(pairs[at + 2], "o")) for at in range(2)]
+        pair_got = swap(pairs[1], "c")
+        half_rows = pair_got.shape[0] // 2
+        key_got = swap(plus(spot, pairs[0], pair_got, half_rows), "x")
+        kv_low = key_sum(pairs[0], pair_got, key_got)
+        if count_w == 2:
+            head_weights = [*low_heads, head_got, swap(head_got, "c")]
+        input_grad = token_gradient(
+            spots.at[2].set(c_at.astype(jnp.int32)),
+            resid_grad,
+            exchange(query_low),
+            exchange(kv_low),
+            head_weights,
+        )
+        every_w = tuple(range(count_w))
+        slabs = head_part(every_w, c_at, swap(head_part(every_w, 1 - c_at), "c"))
+        head_sum = lax.psum_scatter(slabs, "w", scatter_dimension=0, tiled=True)
+        head_sum = plus(spot, head_sum, swap(head_sum, "x"))
         if count_o == 2:
-            head_sum = add_pair(head_sum, swap(head_sum, "o"))
-        head_two = unite(head_sum[None], to_far(head_sum)[None], far_bit)
-        head_four = unite(head_two, to_near(head_two), near_bit)
-        head_other = swap(head_four, "c")
+            head_sum = plus(spot, head_sum, swap(head_sum, "o"))
+        n_bit, f_bit = [
+            jnp.stack([bit, bit]).astype(jnp.int32) for bit in (near_bit, far_bit)
+        ]
+        head_sum = unite(f_bit, head_sum, to_far(head_sum))
+        head_sum = unite(n_bit, head_sum, to_near(head_sum))
+        total_query, total_key, total_value, head_bias = head_finish(
+            spot, head_sum, swap(head_sum, "c")
+        )
         quarter = hidden // 4
         count = quarter // 256
         act_at = 5 * quarter
@@ -1098,10 +1370,6 @@
         vectors = [part_of(small_own[at], w_at, count_w, 0) for at in range(6)]
         total_up_bias = part_of(small_own[8:12].reshape(-1), w_at, count_w, 0)
 
-    input_grad = resid_grad + token_grad.astype(F32)
-    total_query, total_key, total_value, head_bias = head_finish(
-        spot, head_four, head_other
-    )
     totals = [part_of(head_bias[at], w_at, count_w, 0) for at in (0, 8)] + vectors
     return (
         outputs[None],

time: 365 us -> 352 us (0.964); the launches traced: 364 us -> 346 us
  waiting for transfers between devices: 140 us -> 76.2 us
  starting transfers between devices: 39.8 us -> 79.9 us
  Pallas kernels: 104 us -> 126 us
  other arithmetic: 31.3 us -> 12.9 us
  local copies, waits for them, and re-layouts: 33.7 us -> 48.1 us
  between operations: 15.6 us -> 2.82 us
    ppermute x5, waiting for transfers between devices: 50.8 us -> 1.29 us  [to_near(): return lax.ppermute(value, 'z', near)]
    ppermute x25 -> x31, starting transfers between devices: 22.9 us -> 51 us  [swap(): return lax.ppermute(value, axis, SWAP)]
    ppermute x25 -> x31, waiting for transfers between devices: 39.8 us -> 17.3 us  [swap(): return lax.ppermute(value, axis, SWAP)]
    pallas_call x9 -> x14, Pallas kernels: 73.8 us -> 93.8 us  [the longest x2 40.4 us: attend_backward(): pl.pallas_call(partial(backward_kernel, blocks=blocks, rows=2 * half_rows...]
    all_gather x1 -> x0, waiting for transfers between devices: 15.8 us -> none  [body(): token_all = lax.all_gather(low_tokens, 'z', axis=0, tiled=True)]
    unnamed x124 -> x194, local copies, waits for them, and re-layouts: 21.9 us -> 37.2 us
    ppermute x5, waiting for transfers between devices: 29.6 us -> 43.6 us  [to_far(): return lax.ppermute(value, 'z', far)]
    convert_element_type x13 -> x1, other arithmetic: 9.51 us -> 0.01 us  [body(): small_all = small_all.astype(F32)]
  transfers between devices with their start and end apart: 43 -> 56, of which waited for: 17 -> 14; matrix products, arithmetic and copies ran while one was open for 11% -> 7% of each run, Pallas kernels for 24% -> 29%
where the time goes in v4:
time: 352 us; the launch traced here: 346 us
  Pallas kernels  126 us (36%)
  starting transfers between devices  79.9 us (23%)
  waiting for transfers between devices  76.2 us (22%)
  local copies, waits for them, and re-layouts  48.1 us (14%)
  other arithmetic  12.9 us (4%)
    ppermute x31, starting transfers between devices, swap(): return lax.ppermute(value, axis, SWAP)  51 us
    ppermute x5, waiting for transfers between devices, to_far(): return lax.ppermute(value, 'z', far)  43.6 us
    pallas_call x2, Pallas kernels, attend_backward(): pl.pallas_call(partial(backward_kernel, blocks=blocks, rows=2 * half_rows...  40.4 us
    unnamed x194, local copies, waits for them, and re-layouts  37.2 us
    pallas_call x1, Pallas kernels, attend_forward(): pl.pallas_call(partial(forward_kernel, blocks=blocks, rows=2 * half_rows...  25.1 us
    ppermute x31, waiting for transfers between devices, swap(): return lax.ppermute(value, axis, SWAP)  17.3 us
    pallas_call x1, Pallas kernels, middle(): pl.pallas_call(partial(middle_kernel, groups=groups, shared=len(weights)...  15.9 us
    ppermute x12, starting transfers between devices, exchange(): lax.ppermute(item, 'z', perm)  14.8 us
  transfers between devices with their start and end apart: 56, of which 14 were waited for; matrix products, arithmetic and copies ran while one was open for 7% of the time, Pallas kernels for 29%

profile of v4, /device:TPU:1, one launch (start us, length us, event | category | flops | bytes accessed | tf_op | source)
XLA Modules:
  0.0 345.5 jit_solution(15998168790391839630)
XLA Ops:
  5.8 2.8 prepare.1
  18.3 7.3 %round_weights.1 = (bf16[384,768]{1,0:T(8,128)(2,1)S(1)}, bf16[384,3072]{1,0:T(8,128)(2,1)S(1)}, bf16[1536,768]{1,0:T(8,128)(2,1)}, bf16[1728,768]{1,0:T(8,128)(2,1)}) custom-call(s32[2]{0:T(128)S(1)} %get-tuple-element.344.meta_ref, f32[384,768]{1,0:T(8,128)S(1)} %copy-done.38, f32[384,3072]{1,0:T(8,128)} %up_w.1, f32[1536,768]{1,0:T(8,128)} %down_w.1), custom_call_target="tpu_custom_call" | custom-call | flops 1000 | bytes 1 | tf_op jit(solution)/shard_map/round_weights/pallas_call | solution.py:263
  27.1 5.0 %collective-permute-done.2.second_ref = bf16[256,768]{1,0:T(8,128)(2,1)S(1)} collective-permute-done((bf16[256,768]{1,0:T(8,128)(2,1)S(1)}, bf16[256,768]{1,0:T(8,128)(2,1)S(1)}, u32[]{:S(2)}, u32[]{:S(2)}) %collective-permute-start.2) | collective-permute-done | bytes 393248 | tf_op jit(solution)/shard_map/ppermute | solution.py:1077
  38.3 3.0 collective-permute-done.4.second_ref
  41.3 2.6 project.3
  46.3 4.3 %collective-permute-start.8 = (bf16[512,384]{1,0:T(8,128)(2,1)S(1)}, bf16[512,384]{1,0:T(8,128)(2,1)S(1)}, u32[]{:S(2)}, u32[]{:S(2)}) collective-permute-start(bf16[512,384]{1,0:T(8,128)(2,1)S(1)} %get-tuple-element.189.refs_3_.refs_9_), channel_id=1, source_target_pairs={{0,2},{2,0},{1,3},{3,1},{4,6},{6,4},{5,7},{7,5},{8,10},{10,8},{9,1... | collective-permute-start | bytes 1179656 | tf_op jit(solution)/shard_map/ppermute | solution.py:33
  51.9 8.7 %collective-permute-start.10 = (bf16[512,384]{1,0:T(8,128)(2,1)S(1)}, bf16[512,384]{1,0:T(8,128)(2,1)}, u32[]{:S(2)}, u32[]{:S(2)}) collective-permute-start(bf16[512,384]{1,0:T(8,128)(2,1)S(1)} %collective-permute-done.6.refs_5_.refs_11_), channel_id=1, source_target_pairs={{0,2},{2,0},{1,3},{3,1},{4,6},{6,4},{5,7},{7,5},{8,10},{10,8},{9,1... | collective-permute-start | bytes 1179656 | tf_op jit(solution)/shard_map/ppermute | solution.py:33
  60.6 4.2 %collective-permute-start.9 = (bf16[512,384]{1,0:T(8,128)(2,1)S(1)}, bf16[512,384]{1,0:T(8,128)(2,1)}, u32[]{:S(2)}, u32[]{:S(2)}) collective-permute-start(bf16[512,384]{1,0:T(8,128)(2,1)S(1)} %collective-permute-done.5.refs_4_.refs_10_), channel_id=1, source_target_pairs={{0,2},{2,0},{1,3},{3,1},{4,6},{6,4},{5,7},{7,5},{8,10},{10,8},{9,1... | collective-permute-start | bytes 1179656 | tf_op jit(solution)/shard_map/ppermute | solution.py:33
  66.4 25.1 %attend_forward.1 = (f32[192,1024]{1,0:T(8,128)S(1)}, bf16[192,256]{1,0:T(8,128)(2,1)S(1)}, bf16[192,256]{1,0:T(8,128)(2,1)S(1)}, bf16[192,256]{1,0:T(8,128)(2,1...) custom-call(s32[6]{0:T(128)S(1)} %stack.94.meta_ref, bf16[192,512]{1,0:T(8,128)(2,1)S(1)} %get-tuple-element.184.refs_0_, ...), custom_call_target="tpu_custom_call" | custom-call | flops 24000 | bytes 1 | tf_op jit(solution)/shard_map/attend_forward/pallas_call | solution.py:124
  98.8 5.9 %collective-permute-done.13.refs_2_ = bf16[192,256]{1,0:T(8,128)(2,1)S(1)} collective-permute-done((bf16[192,256]{1,0:T(8,128)(2,1)S(1)}, bf16[192,256]{1,0:T(8,128)(2,1)S(1)}, u32[]{:S(2)}, u32[]{:S(2)}) %collective-permute-start.13) | collective-permute-done | bytes 98336 | tf_op jit(solution)/shard_map/ppermute | solution.py:1068
  105.4 15.9 %middle.1 = (f32[256,768]{1,0:T(8,128)}, f32[256,768]{1,0:T(8,128)}, bf16[192,256]{1,0:T(8,128)(2,1)}, bf16[192,256]{1,0:T(8,128)(2,1)}, bf16[192,256]{1,0:T(8,1...) custom-call(s32[4]{0:T(128)} %pad_add_fusion.2.meta_ref, ...), custom_call_target="tpu_custom_call" | custom-call | flops 15000 | bytes 1 | tf_op jit(solution)/shard_map/middle/pallas_call | solution.py:641
  133.4 2.3 down_slab.2
  136.7 2.9 up_slabs.1
  150.7 26.0 %attend_backward.2 = (bf16[192,256]{1,0:T(8,128)(2,1)S(1)}, bf16[192,256]{1,0:T(8,128)(2,1)S(1)}, bf16[192,256]{1,0:T(8,128)(2,1)S(1)}, bf16[192,256]{1,0:T(8,12...) custom-call(s32[6]{0:T(128)S(1)} %stack.94.meta_ref, ...), custom_call_target="tpu_custom_call" | custom-call | flops 24000 | bytes 1 | tf_op jit(solution)/shard_map/attend_backward/pallas_call | solution.py:225
  180.9 14.4 %attend_backward.3 = (bf16[192,256]{1,0:T(8,128)(2,1)S(1)}, bf16[192,256]{1,0:T(8,128)(2,1)S(1)}, bf16[192,256]{1,0:T(8,128)(2,1)S(1)}, bf16[192,256]{1,0:T(8,12...) custom-call(s32[6]{0:T(128)S(1)} %stack.94.meta_ref, ...), custom_call_target="tpu_custom_call", output_to_operand_aliasing={{0}: (17, {}), {1}: (18, {}), {2}: (19, {}), {3}: (20, {}),... | custom-call | flops 12000 | bytes 1 | tf_op jit(solution)/shard_map/attend_backward/pallas_call | solution.py:225
  199.2 2.5 add_convert_fusion
  210.2 16.2 %collective-permute-done.26 = bf16[192,768]{1,0:T(8,128)(2,1)} collective-permute-done((bf16[192,768]{1,0:T(8,128)(2,1)}, bf16[192,768]{1,0:T(8,128)(2,1)}, u32[]{:S(2)}, u32[]{:S(2)}) %collective-permute-start.26) | collective-permute-done | bytes 294944 | tf_op jit(solution)/shard_map/ppermute | solution.py:1188
  233.9 11.0 %collective-permute-done.28.got_ref = bf16[1024,384]{1,0:T(8,128)(2,1)S(1)} collective-permute-done((bf16[1024,384]{1,0:T(8,128)(2,1)S(1)}, bf16[1024,384]{1,0:T(8,128)(2,1)S(1)}, u32[]{:S(2)}, u32[]{:S(2)}) %collective-permute-start.28) | collective-permute-done | bytes 786464 | tf_op jit(solution)/shard_map/ppermute | solution.py:33
  247.6 2.4 collective-permute-start.34
  263.5 2.3 head_slab.7
  265.9 2.7 collective-permute-done.36
  270.7 2.9 collective-permute-start.48
  273.8 12.3 %collective-permute-done.40 = bf16[48,2048]{1,0:T(8,128)(2,1)S(1)} collective-permute-done((bf16[48,2048]{1,0:T(8,128)(2,1)S(1)}, bf16[48,2048]{1,0:T(8,128)(2,1)S(1)}, u32[]{:S(2)}, u32[]{:S(2)}) %collective-permute-start.40) | collective-permute-done | bytes 196640 | tf_op jit(solution)/shard_map/ppermute | solution.py:1188
  288.9 6.8 %collective-permute-done.43 = bf16[48,2048]{1,0:T(8,128)(2,1)S(1)} collective-permute-done((bf16[48,2048]{1,0:T(8,128)(2,1)S(1)}, bf16[48,2048]{1,0:T(8,128)(2,1)S(1)}, u32[]{:S(2)}, u32[]{:S(2)}) %collective-permute-start.43) | collective-permute-done | bytes 196640 | tf_op jit(solution)/shard_map/ppermute | solution.py:1188
  295.8 2.5 collective-permute-start.46
  299.8 8.2 %collective-permute-done.45 = bf16[208,576]{1,0:T(8,128)(2,1)S(1)} collective-permute-done((bf16[208,576]{1,0:T(8,128)(2,1)S(1)}, bf16[208,576]{1,0:T(8,128)(2,1)S(1)}, u32[]{:S(2)}, u32[]{:S(2)}) %collective-permute-start.45) | collective-permute-done | bytes 239648 | tf_op jit(solution)/shard_map/ppermute | solution.py:1188
  308.9 3.8 %token_gradient.1 = f32[256,768]{1,0:T(8,128)} custom-call(s32[4]{0:T(128)S(1)} %copy-done.68, f32[256,768]{1,0:T(8,128)S(1)} %copy-done.41, bf16[192,256]{1,0:T(8,128)(2,1)S(1)} %get-tuple-element.298.refs_2_.refs_0_, bf16[192,256]{1,0:T(8,128)(2,1)S(1)} %copy-done.62, bf16[192,256]{1,0:T(8,128)(2,1)S(1)} %copy-done.64, bf16[192,256]{1,0:T(8,128)(2,1)S(1)} %copy-done.66, ...), custom_call_target="tpu_custom_call" | custom-call | flops 4000 | bytes 1 | tf_op jit(solution)/shard_map/token_gradient/pallas_call | solution.py:887
  312.7 9.5 %collective-permute-start.51 = (bf16[384,768]{1,0:T(8,128)(2,1)S(1)}, bf16[384,768]{1,0:T(8,128)(2,1)}, u32[]{:S(2)}, u32[]{:S(2)}) collective-permute-start(bf16[384,768]{1,0:T(8,128)(2,1)S(1)} %bitcast.47), channel_id=1, source_target_pairs={{0,2},{2,0},{1,3},{3,1},{4,6},{6,4},{5,7},{7,5},{8,10},{10,8},{9,1... | collective-permute-start | bytes 1769480 | tf_op jit(solution)/shard_map/ppermute | solution.py:33
  324.6 3.3 collective-permute-start.53
  328.0 4.3 %down_finish.1 = f32[1536,768]{1,0:T(8,128)} custom-call(s32[2]{0:T(128)S(1)} %copy-done.69, bf16[384,768]{1,0:T(8,128)(2,1)S(1)} %bitcast.48, bf16[384,768]{1,0:T(8,128)(2,1)S(1)} %collective-permute-done.47.refs_1_, bf16[384,768]{1,0:T(8,128)(2,1)} %collective-permute-done.51.refs_2_, bf16[384,768]{1,0:T(8,128)(2,1)} %collective-permute-done.52.refs_3_), custom_call_target="tpu_custom_call" | custom-call | flops 4000 | bytes 1 | tf_op jit(solution)/shard_map/down_finish/pallas_call | solution.py:920
  334.8 2.7 head_finish.1
  338.8 5.1 %up_finish.1 = (f32[384,3072]{1,0:T(8,128)}, f32[384,768]{1,0:T(8,128)}, f32[384,128]{1,0:T(8,128)S(1)}) custom-call(s32[2]{0:T(128)S(1)} %copy-done.69, bf16[192,2048]{1,0:T(8,128)(2,1)S(1)} %maximum_select_fusion.1.refs_0_, bf16[192,2048]{1,0:T(8,128)(2,1)} %collective-permute-done.50.refs_1_, bf16[192,2048]{1,0:T(8,128)(2,1)} %collective-permute-done.54.refs_2_, ...), custom_call_target="tpu_custom_call" | custom-call | flops 5000 | bytes 1 | tf_op jit(solution)/shard_map/up_finish/pallas_call | solution.py:957
  (362 shorter events, 113.7 us)
Async XLA Ops:
  12.0 20.9 %collective-permute-start = (bf16[384,576]{1,0:T(8,128)(2,1)S(1)}, bf16[384,576]{1,0:T(8,128)(2,1)S(1)}, u32[]{:S(2)}, u32[]{:S(2)}) collective-permute-start(bf16[384,576]{1,0:T(8,128)(2,1)S(1)} %get-tuple-element.175.refs_0_), channel_id=1, source_target_pairs={{0,1},{1,0},{2,3},{3,2},{4,5},{5,4},{6,7},{7,6},{8,9},{9,8},{10,11... | collective-permute-start | bytes 1327112 | tf_op jit(solution)/shard_map/ppermute | solution.py:33
  14.0 18.1 %collective-permute-start.2 = (bf16[256,768]{1,0:T(8,128)(2,1)S(1)}, bf16[256,768]{1,0:T(8,128)(2,1)S(1)}, u32[]{:S(2)}, u32[]{:S(2)}) collective-permute-start(bf16[256,768]{1,0:T(8,128)(2,1)S(1)} %get-tuple-element.174.first_ref), channel_id=1, source_target_pairs={{0,8},{8,0},{16,24},{24,16},{1,9},{9,1},{17,25},{25,17},{2,10},{10... | collective-permute-start | bytes 1179656 | tf_op jit(solution)/shard_map/ppermute | solution.py:1077
  15.3 17.5 %collective-permute-start.3 = (bf16[256,768]{1,0:T(8,128)(2,1)S(1)}, bf16[256,768]{1,0:T(8,128)(2,1)}, u32[]{:S(2)}, u32[]{:S(2)}) collective-permute-start(bf16[256,768]{1,0:T(8,128)(2,1)S(1)} %get-tuple-element.174.first_ref), channel_id=1, source_target_pairs={{0,16},{16,0},{8,24},{24,8},{1,17},{17,1},{9,25},{25,9},{2,18},{18... | collective-permute-start | bytes 1179656 | tf_op jit(solution)/shard_map/ppermute | solution.py:1078
  32.9 59.6 %collective-permute-start.11 = (bf16[1728,768]{1,0:T(8,128)(2,1)}, bf16[1728,768]{1,0:T(8,128)(2,1)}, u32[]{:S(2)}, u32[]{:S(2)}) collective-permute-start(bf16[1728,768]{1,0:T(8,128)(2,1)} %get-tuple-element.191), channel_id=1, source_target_pairs={{0,1},{1,0},{2,3},{3,2},{4,5},{5,4},{6,7},{7,6},{8,9},{9,8},{10,11... | collective-permute-start | bytes 7962632 | tf_op jit(solution)/shard_map/ppermute | solution.py:33
  46.1 14.5 %collective-permute-start.5 = (bf16[512,384]{1,0:T(8,128)(2,1)S(1)}, bf16[512,384]{1,0:T(8,128)(2,1)S(1)}, u32[]{:S(2)}, u32[]{:S(2)}) collective-permute-start(bf16[512,384]{1,0:T(8,128)(2,1)S(1)} %get-tuple-element.188.refs_2_.refs_8_), channel_id=1, source_target_pairs={{0,4},{4,0},{1,5},{5,1},{2,6},{6,2},{3,7},{7,3},{8,12},{12,8},{9,1... | collective-permute-start | bytes 1179656 | tf_op jit(solution)/shard_map/ppermute | solution.py:33
  46.3 19.2 %collective-permute-start.8 = (bf16[512,384]{1,0:T(8,128)(2,1)S(1)}, bf16[512,384]{1,0:T(8,128)(2,1)S(1)}, u32[]{:S(2)}, u32[]{:S(2)}) collective-permute-start(bf16[512,384]{1,0:T(8,128)(2,1)S(1)} %get-tuple-element.189.refs_3_.refs_9_), channel_id=1, source_target_pairs={{0,2},{2,0},{1,3},{3,1},{4,6},{6,4},{5,7},{7,5},{8,10},{10,8},{9,1... | collective-permute-start | bytes 1179656 | tf_op jit(solution)/shard_map/ppermute | solution.py:33
  50.6 14.9 %collective-permute-start.7 = (bf16[512,384]{1,0:T(8,128)(2,1)S(1)}, bf16[512,384]{1,0:T(8,128)(2,1)S(1)}, u32[]{:S(2)}, u32[]{:S(2)}) collective-permute-start(bf16[512,384]{1,0:T(8,128)(2,1)S(1)} %get-tuple-element.188.refs_2_.refs_8_), channel_id=1, source_target_pairs={{0,2},{2,0},{1,3},{3,1},{4,6},{6,4},{5,7},{7,5},{8,10},{10,8},{9,1... | collective-permute-start | bytes 1179656 | tf_op jit(solution)/shard_map/ppermute | solution.py:33
  123.2 17.5 %collective-permute-start.18 = (bf16[192,256]{1,0:T(8,128)(2,1)}, bf16[192,256]{1,0:T(8,128)(2,1)S(1)}, u32[]{:S(2)}, u32[]{:S(2)}) collective-permute-start(bf16[192,256]{1,0:T(8,128)(2,1)} %get-tuple-element.209), channel_id=1, source_target_pairs={{0,8},{8,0},{16,24},{24,16},{1,9},{9,1},{17,25},{25,17},{2,10},{10... | collective-permute-start | bytes 294920 | tf_op jit(solution)/shard_map/ppermute | solution.py:1068
  124.9 16.5 %collective-permute-start.19 = (bf16[192,256]{1,0:T(8,128)(2,1)}, bf16[192,256]{1,0:T(8,128)(2,1)S(1)}, u32[]{:S(2)}, u32[]{:S(2)}) collective-permute-start(bf16[192,256]{1,0:T(8,128)(2,1)} %get-tuple-element.210), channel_id=1, source_target_pairs={{0,16},{16,0},{8,24},{24,8},{1,17},{17,1},{9,25},{25,9},{2,18},{18... | collective-permute-start | bytes 294920 | tf_op jit(solution)/shard_map/ppermute | solution.py:1068
  124.9 17.1 %collective-permute-start.20 = (bf16[192,256]{1,0:T(8,128)(2,1)}, bf16[192,256]{1,0:T(8,128)(2,1)S(1)}, u32[]{:S(2)}, u32[]{:S(2)}) collective-permute-start(bf16[192,256]{1,0:T(8,128)(2,1)} %get-tuple-element.211), channel_id=1, source_target_pairs={{0,24},{24,0},{8,16},{16,8},{1,25},{25,1},{9,17},{17,9},{2,26},{26... | collective-permute-start | bytes 294920 | tf_op jit(solution)/shard_map/ppermute | solution.py:1068
  142.7 34.0 %collective-permute-start.21 = (bf16[768,768]{1,0:T(8,128)(2,1)}, bf16[768,768]{1,0:T(8,128)(2,1)}, u32[]{:S(2)}, u32[]{:S(2)}) collective-permute-start(bf16[768,768]{1,0:T(8,128)(2,1)} %down_slab.2), channel_id=1, source_target_pairs={{0,1},{1,0},{2,3},{3,2},{4,5},{5,4},{6,7},{7,6},{8,9},{9,8},{10,11... | collective-permute-start | bytes 3538952 | tf_op jit(solution)/shard_map/ppermute | solution.py:33
  143.4 53.2 %collective-permute-start.23 = (bf16[384,2048]{1,0:T(8,128)(2,1)}, bf16[384,2048]{1,0:T(8,128)(2,1)}, u32[]{:S(2)}, u32[]{:S(2)}) collective-permute-start(bf16[384,2048]{1,0:T(8,128)(2,1)} %get-tuple-element.229), channel_id=1, source_target_pairs={{0,4},{4,0},{1,5},{5,1},{2,6},{6,2},{3,7},{7,3},{8,12},{12,8},{9,1... | collective-permute-start | bytes 4718600 | tf_op jit(solution)/shard_map/ppermute | solution.py:33
  145.2 51.4 %collective-permute-start.24 = (bf16[576,768]{1,0:T(8,128)(2,1)}, bf16[576,768]{1,0:T(8,128)(2,1)S(1)}, u32[]{:S(2)}, u32[]{:S(2)}) collective-permute-start(bf16[576,768]{1,0:T(8,128)(2,1)} %copy-done.70), channel_id=1, source_target_pairs={{0,1},{1,0},{2,3},{3,2},{4,5},{5,4},{6,7},{7,6},{8,9},{9,8},{10,11... | collective-permute-start | bytes 2654216 | tf_op jit(solution)/shard_map/ppermute | solution.py:33
  179.2 17.4 %collective-permute-start.22 = (bf16[384,768]{1,0:T(8,128)(2,1)S(1)}, bf16[384,768]{1,0:T(8,128)(2,1)S(1)}, u32[]{:S(2)}, u32[]{:S(2)}) collective-permute-start(bf16[384,768]{1,0:T(8,128)(2,1)S(1)} %constant_dynamic-slice_fusion.6), channel_id=1, source_target_pairs={{0,8},{8,0},{16,24},{24,16},{1,9},{9,1},{17,25},{25,17},{2,10},{10... | collective-permute-start | bytes 1769480 | tf_op jit(solution)/shard_map/ppermute | solution.py:1185
  202.8 23.6 %collective-permute-start.27 = (bf16[192,2048]{1,0:T(8,128)(2,1)}, bf16[192,2048]{1,0:T(8,128)(2,1)}, u32[]{:S(2)}, u32[]{:S(2)}) collective-permute-start(bf16[192,2048]{1,0:T(8,128)(2,1)} %dynamic-slice_bitcast_fusion), channel_id=1, source_target_pairs={{0,1},{1,0},{2,3},{3,2},{4,5},{5,4},{6,7},{7,6},{8,9},{9,8},{10,11... | collective-permute-start | bytes 2359304 | tf_op jit(solution)/shard_map/ppermute | solution.py:33
  206.2 20.1 %collective-permute-start.26 = (bf16[192,768]{1,0:T(8,128)(2,1)}, bf16[192,768]{1,0:T(8,128)(2,1)}, u32[]{:S(2)}, u32[]{:S(2)}) collective-permute-start(bf16[192,768]{1,0:T(8,128)(2,1)} %constant_dynamic-slice_fusion.5), channel_id=1, source_target_pairs={{0,16},{16,0},{8,24},{24,8},{1,17},{17,1},{9,25},{25,9},{2,18},{18... | collective-permute-start | bytes 884744 | tf_op jit(solution)/shard_map/ppermute | solution.py:1188
  206.3 25.6 %collective-permute-start.29 = (bf16[192,256]{1,0:T(8,128)(2,1)S(1)}, bf16[192,256]{1,0:T(8,128)(2,1)S(1)}, u32[]{:S(2)}, u32[]{:S(2)}) collective-permute-start(bf16[192,256]{1,0:T(8,128)(2,1)S(1)} %get-tuple-element.261.refs_3_), channel_id=1, source_target_pairs={{0,8},{8,0},{16,24},{24,16},{1,9},{9,1},{17,25},{25,17},{2,10},{10... | collective-permute-start | bytes 294920 | tf_op jit(solution)/shard_map/ppermute | solution.py:1068
  207.2 25.5 %collective-permute-start.30 = (bf16[192,256]{1,0:T(8,128)(2,1)S(1)}, bf16[192,256]{1,0:T(8,128)(2,1)S(1)}, u32[]{:S(2)}, u32[]{:S(2)}) collective-permute-start(bf16[192,256]{1,0:T(8,128)(2,1)S(1)} %copy-done.24), channel_id=1, source_target_pairs={{0,16},{16,0},{8,24},{24,8},{1,17},{17,1},{9,25},{25,9},{2,18},{18... | collective-permute-start | bytes 294920 | tf_op jit(solution)/shard_map/ppermute | solution.py:1068
  208.8 24.5 %collective-permute-start.31 = (bf16[192,256]{1,0:T(8,128)(2,1)S(1)}, bf16[192,256]{1,0:T(8,128)(2,1)S(1)}, u32[]{:S(2)}, u32[]{:S(2)}) collective-permute-start(bf16[192,256]{1,0:T(8,128)(2,1)S(1)} %copy-done.28), channel_id=1, source_target_pairs={{0,24},{24,0},{8,16},{16,8},{1,25},{25,1},{9,17},{17,9},{2,26},{26... | collective-permute-start | bytes 294920 | tf_op jit(solution)/shard_map/ppermute | solution.py:1068
  226.4 18.6 %collective-permute-start.28 = (bf16[1024,384]{1,0:T(8,128)(2,1)S(1)}, bf16[1024,384]{1,0:T(8,128)(2,1)S(1)}, u32[]{:S(2)}, u32[]{:S(2)}) collective-permute-start(bf16[1024,384]{1,0:T(8,128)(2,1)S(1)} %add_convert_fusion.2), channel_id=1, source_target_pairs={{0,4},{4,0},{1,5},{5,1},{2,6},{6,2},{3,7},{7,3},{8,12},{12,8},{9,1... | collective-permute-start | bytes 2359304 | tf_op jit(solution)/shard_map/ppermute | solution.py:33
  228.4 23.1 %collective-permute-start.32 = (bf16[96,768]{1,0:T(8,128)(2,1)}, bf16[96,768]{1,0:T(8,128)(2,1)}, u32[]{:S(2)}, u32[]{:S(2)}) collective-permute-start(bf16[96,768]{1,0:T(8,128)(2,1)} %constant_dynamic-slice_fusion.4), channel_id=1, source_target_pairs={{0,4},{4,0},{1,5},{5,1},{2,6},{6,2},{3,7},{7,3},{8,12},{12,8},{9,1... | collective-permute-start | bytes 442376 | tf_op jit(solution)/shard_map/ppermute | solution.py:33
  232.6 29.4 %collective-permute-start.35 = (bf16[96,2048]{1,0:T(8,128)(2,1)}, bf16[96,2048]{1,0:T(8,128)(2,1)}, u32[]{:S(2)}, u32[]{:S(2)}) collective-permute-start(bf16[96,2048]{1,0:T(8,128)(2,1)} %constant_dynamic-slice_fusion.3), channel_id=1, source_target_pairs={{0,8},{8,0},{16,24},{24,16},{1,9},{9,1},{17,25},{25,17},{2,10},{10... | collective-permute-start | bytes 1179656 | tf_op jit(solution)/shard_map/ppermute | solution.py:1185
  251.5 19.2 %collective-permute-start.37 = (bf16[384,256]{1,0:T(8,128)(2,1)}, bf16[384,256]{1,0:T(8,128)(2,1)S(1)}, u32[]{:S(2)}, u32[]{:S(2)}) collective-permute-start(bf16[384,256]{1,0:T(8,128)(2,1)} %copy-done.21), channel_id=1, source_target_pairs={{0,8},{8,0},{16,24},{24,16},{1,9},{9,1},{17,25},{25,17},{2,10},{10... | collective-permute-start | bytes 589832 | tf_op jit(solution)/shard_map/ppermute | solution.py:1068
  251.5 22.0 %collective-permute-start.38 = (bf16[384,256]{1,0:T(8,128)(2,1)}, bf16[384,256]{1,0:T(8,128)(2,1)S(1)}, u32[]{:S(2)}, u32[]{:S(2)}) collective-permute-start(bf16[384,256]{1,0:T(8,128)(2,1)} %copy-done.19), channel_id=1, source_target_pairs={{0,16},{16,0},{8,24},{24,8},{1,17},{17,1},{9,25},{25,9},{2,18},{18... | collective-permute-start | bytes 589832 | tf_op jit(solution)/shard_map/ppermute | solution.py:1068
  254.9 18.9 %collective-permute-start.39 = (bf16[384,256]{1,0:T(8,128)(2,1)}, bf16[384,256]{1,0:T(8,128)(2,1)S(1)}, u32[]{:S(2)}, u32[]{:S(2)}) collective-permute-start(bf16[384,256]{1,0:T(8,128)(2,1)} %copy-done.17), channel_id=1, source_target_pairs={{0,24},{24,0},{8,16},{16,8},{1,25},{25,1},{9,17},{17,9},{2,26},{26... | collective-permute-start | bytes 589832 | tf_op jit(solution)/shard_map/ppermute | solution.py:1068
  261.9 24.3 %collective-permute-start.41 = (bf16[96,768]{1,0:T(8,128)(2,1)S(1)}, bf16[96,768]{1,0:T(8,128)(2,1)S(1)}, u32[]{:S(2)}, u32[]{:S(2)}) collective-permute-start(bf16[96,768]{1,0:T(8,128)(2,1)S(1)} %add_convert_fusion.9), channel_id=1, source_target_pairs={{0,16},{16,0},{8,24},{24,8},{1,17},{17,1},{9,25},{25,9},{2,18},{18... | collective-permute-start | bytes 442376 | tf_op jit(solution)/shard_map/ppermute | solution.py:1188
  268.6 17.6 %collective-permute-start.40 = (bf16[48,2048]{1,0:T(8,128)(2,1)S(1)}, bf16[48,2048]{1,0:T(8,128)(2,1)S(1)}, u32[]{:S(2)}, u32[]{:S(2)}) collective-permute-start(bf16[48,2048]{1,0:T(8,128)(2,1)S(1)} %constant_dynamic-slice_fusion.2), channel_id=1, source_target_pairs={{0,16},{16,0},{8,24},{24,8},{1,17},{17,1},{9,25},{25,9},{2,18},{18... | collective-permute-start | bytes 589832 | tf_op jit(solution)/shard_map/ppermute | solution.py:1188
  270.7 38.2 %collective-permute-start.48 = (bf16[576,768]{1,0:T(8,128)(2,1)S(1)}, bf16[576,768]{1,0:T(8,128)(2,1)S(1)}, u32[]{:S(2)}, u32[]{:S(2)}) collective-permute-start(bf16[576,768]{1,0:T(8,128)(2,1)S(1)} %copy-done.40), channel_id=1, source_target_pairs={{0,2},{2,0},{1,3},{3,1},{4,6},{6,4},{5,7},{7,5},{8,10},{10,8},{9,1... | collective-permute-start | bytes 2654216 | tf_op jit(solution)/shard_map/ppermute | solution.py:33
  288.1 19.9 %collective-permute-start.45 = (bf16[208,576]{1,0:T(8,128)(2,1)S(1)}, bf16[208,576]{1,0:T(8,128)(2,1)S(1)}, u32[]{:S(2)}, u32[]{:S(2)}) collective-permute-start(bf16[208,576]{1,0:T(8,128)(2,1)S(1)} %add_convert_fusion.6), channel_id=1, source_target_pairs={{0,16},{16,0},{8,24},{24,8},{1,17},{17,1},{9,25},{25,9},{2,18},{18... | collective-permute-start | bytes 718856 | tf_op jit(solution)/shard_map/ppermute | solution.py:1188
  299.5 22.7 %collective-permute-start.47 = (bf16[384,768]{1,0:T(8,128)(2,1)S(1)}, bf16[384,768]{1,0:T(8,128)(2,1)S(1)}, u32[]{:S(2)}, u32[]{:S(2)}) collective-permute-start(bf16[384,768]{1,0:T(8,128)(2,1)S(1)} %bitcast.46), channel_id=1, source_target_pairs={{0,4},{4,0},{1,5},{5,1},{2,6},{6,2},{3,7},{7,3},{8,12},{12,8},{9,1... | collective-permute-start | bytes 1769480 | tf_op jit(solution)/shard_map/ppermute | solution.py:33
  308.5 23.7 %collective-permute-start.50 = (bf16[192,2048]{1,0:T(8,128)(2,1)S(1)}, bf16[192,2048]{1,0:T(8,128)(2,1)}, u32[]{:S(2)}, u32[]{:S(2)}) collective-permute-start(bf16[192,2048]{1,0:T(8,128)(2,1)S(1)} %maximum_select_fusion.1.refs_0_), channel_id=1, source_target_pairs={{0,4},{4,0},{1,5},{5,1},{2,6},{6,2},{3,7},{7,3},{8,12},{12,8},{9,1... | collective-permute-start | bytes 2359304 | tf_op jit(solution)/shard_map/ppermute | solution.py:33
  312.7 15.2 %collective-permute-start.51 = (bf16[384,768]{1,0:T(8,128)(2,1)S(1)}, bf16[384,768]{1,0:T(8,128)(2,1)}, u32[]{:S(2)}, u32[]{:S(2)}) collective-permute-start(bf16[384,768]{1,0:T(8,128)(2,1)S(1)} %bitcast.47), channel_id=1, source_target_pairs={{0,2},{2,0},{1,3},{3,1},{4,6},{6,4},{5,7},{7,5},{8,10},{10,8},{9,1... | collective-permute-start | bytes 1769480 | tf_op jit(solution)/shard_map/ppermute | solution.py:33
  (121 other events, 864.7 us)

commit v5 on v4

--- a/solution.py
+++ b/solution.py
@@ -10,6 +10,7 @@
 HEADS = 12
 ZS = 4
 NEG_FILL = -1e30
+VMEM_LIMIT = 60 << 20
 SWAP = ((0, 1), (1, 0))
 F32 = jnp.float32
 BF16 = jnp.bfloat16
@@ -139,7 +140,7 @@
         out_shape=[jax.ShapeDtypeStruct((part, query_count), F32)]
         + [jax.ShapeDtypeStruct((part, size), BF16)] * ZS
         + [jax.ShapeDtypeStruct((heads, 1, query_count), F32)],
-        compiler_params=pltpu.CompilerParams(vmem_limit_bytes=40 << 20),
+        compiler_params=pltpu.CompilerParams(vmem_limit_bytes=VMEM_LIMIT),
         cost_estimate=work(8 * heads),
         name="attend_forward",
     )(meta, *queries, *[item for pair in kv_blocks for item in pair])
@@ -250,7 +251,7 @@
         input_output_aliases={
             1 + len(ins) - len(made) + at: at for at in range(len(made))
         },
-        compiler_params=pltpu.CompilerParams(vmem_limit_bytes=48 << 20),
+        compiler_params=pltpu.CompilerParams(vmem_limit_bytes=VMEM_LIMIT),
         cost_estimate=work(12 * count),
         name="attend_backward",
     )(meta, *ins)
@@ -376,7 +377,7 @@
             + [pltpu.SemaphoreType.DMA((4,))],
         ),
         out_shape=[jax.ShapeDtypeStruct(shape, BF16) for shape in shapes],
-        compiler_params=pltpu.CompilerParams(vmem_limit_bytes=40 << 20),
+        compiler_params=pltpu.CompilerParams(vmem_limit_bytes=VMEM_LIMIT),
         cost_estimate=work(1),
         name="prepare",
     )(meta, tokens, *weights)
@@ -412,7 +413,7 @@
         meta,
         weights,
         [(item.shape, BF16) for item in weights] + [((total, width), BF16)],
-        limit=48,
+        limit=60,
         name="round_weights",
     )
 
@@ -662,7 +663,7 @@
             jax.ShapeDtypeStruct((hidden + 2 * rows, 256), BF16),
             jax.ShapeDtypeStruct((16, width), F32),
         ],
-        compiler_params=pltpu.CompilerParams(vmem_limit_bytes=56 << 20),
+        compiler_params=pltpu.CompilerParams(vmem_limit_bytes=VMEM_LIMIT),
         cost_estimate=work(15),
         name="middle",
     )(meta, tokens, seed, vec, upoff, *flat, *weights)

time: 352 us -> 339 us (0.963)
  Pallas kernels: 126 us -> 103 us
  waiting for transfers between devices: 76.2 us -> 95.1 us
  local copies, waits for them, and re-layouts: 48.1 us -> 31 us
  starting transfers between devices: 79.9 us -> 89.3 us
    ppermute x31, waiting for transfers between devices: 17.3 us -> 35.8 us  [swap(): return lax.ppermute(value, axis, SWAP)]
    unnamed x194 -> x162, local copies, waits for them, and re-layouts: 37.2 us -> 19.6 us
    pallas_call x2, Pallas kernels: 40.4 us -> 25.1 us  [attend_backward(): pl.pallas_call(partial(backward_kernel, blocks=blocks, rows=2 * half_rows...]
    pallas_call x1, Pallas kernels: 25.1 us -> 15.1 us  [attend_forward(): pl.pallas_call(partial(forward_kernel, blocks=blocks, rows=2 * half_rows...]
    ppermute x31, starting transfers between devices: 51 us -> 58.6 us  [swap(): return lax.ppermute(value, axis, SWAP)]
  transfers between devices with their start and end apart: 56 -> 56, of which waited for: 14 -> 15; matrix products, arithmetic and copies ran while one was open for 7% -> 7% of each run, Pallas kernels for 29% -> 23%
where the time goes in v5:
time: 339 us; the launch traced here: 333 us
  Pallas kernels  103 us (30%)
  waiting for transfers between devices  95.1 us (28%)
  starting transfers between devices  89.3 us (26%)
  local copies, waits for them, and re-layouts  31 us (9%)
  other arithmetic  12.4 us (4%)
    ppermute x31, starting transfers between devices, swap(): return lax.ppermute(value, axis, SWAP)  58.6 us
    ppermute x5, waiting for transfers between devices, to_far(): return lax.ppermute(value, 'z', far)  43.3 us
    ppermute x31, waiting for transfers between devices, swap(): return lax.ppermute(value, axis, SWAP)  35.8 us
    pallas_call x2, Pallas kernels, attend_backward(): pl.pallas_call(partial(backward_kernel, blocks=blocks, rows=2 * half_rows...  25.1 us
    unnamed x162, local copies, waits for them, and re-layouts  19.6 us
    pallas_call x1, Pallas kernels, middle(): pl.pallas_call(partial(middle_kernel, groups=groups, shared=len(weights)...  15.9 us
    ppermute x12, starting transfers between devices, exchange(): lax.ppermute(item, 'z', perm)  15.7 us
    pallas_call x1, Pallas kernels, attend_forward(): pl.pallas_call(partial(forward_kernel, blocks=blocks, rows=2 * half_rows...  15.1 us
  transfers between devices with their start and end apart: 56, of which 15 were waited for; matrix products, arithmetic and copies ran while one was open for 7% of the time, Pallas kernels for 23%

profile of v5, /device:TPU:1, one launch (start us, length us, event | category | flops | bytes accessed | tf_op | source)
XLA Modules:
  0.0 333.1 jit_solution(1482752801130419869)
XLA Ops:
  1.3 5.0 %prepare.1 = (bf16[256,768]{1,0:T(8,128)(2,1)}, bf16[384,576]{1,0:T(8,128)(2,1)}, bf16[384,768]{1,0:T(8,128)(2,1)}, bf16[384,768]{1,0:T(8,128)(2,1)}, bf16[384,7...) custom-call(s32[2]{0:T(128)} %get-tuple-element.344.meta_ref, f32[256,768]{1,0:T(8,128)} %bitcast.51, f32[384,768]{1,0:T(8,128)} %refs_1_.1, ...), custom_call_target="tpu_custom_call" | custom-call | flops 1000 | bytes 1 | tf_op jit(solution)/shard_map/prepare/pallas_call | solution.py:368
  12.8 8.3 %round_weights.1 = (bf16[384,768]{1,0:T(8,128)(2,1)}, bf16[384,3072]{1,0:T(8,128)(2,1)}, bf16[1536,768]{1,0:T(8,128)(2,1)}, bf16[1728,768]{1,0:T(8,128)(2,1)}) custom-call(s32[2]{0:T(128)} %get-tuple-element.344.meta_ref, f32[384,768]{1,0:T(8,128)} %out_w.1, f32[384,3072]{1,0:T(8,128)} %up_w.1, f32[1536,768]{1,0:T(8,128)} %down_w.1), custom_call_target="tpu_custom_call" | custom-call | flops 1000 | bytes 1 | tf_op jit(solution)/shard_map/round_weights/pallas_call | solution.py:264
  21.0 5.6 %collective-permute-done.2.second_ref = bf16[256,768]{1,0:T(8,128)(2,1)S(1)} collective-permute-done((bf16[256,768]{1,0:T(8,128)(2,1)}, bf16[256,768]{1,0:T(8,128)(2,1)S(1)}, u32[]{:S(2)}, u32[]{:S(2)}) %collective-permute-start.2) | collective-permute-done | bytes 393248 | tf_op jit(solution)/shard_map/ppermute | solution.py:1078
  32.5 3.1 collective-permute-done.4.second_ref
  40.2 4.4 %collective-permute-start.8 = (bf16[512,384]{1,0:T(8,128)(2,1)S(1)}, bf16[512,384]{1,0:T(8,128)(2,1)S(1)}, u32[]{:S(2)}, u32[]{:S(2)}) collective-permute-start(bf16[512,384]{1,0:T(8,128)(2,1)S(1)} %get-tuple-element.189.refs_3_.refs_9_), channel_id=1, source_target_pairs={{0,2},{2,0},{1,3},{3,1},{4,6},{6,4},{5,7},{7,5},{8,10},{10,8},{9,1... | collective-permute-start | bytes 1179656 | tf_op jit(solution)/shard_map/ppermute | solution.py:34
  45.8 8.7 %collective-permute-start.10 = (bf16[512,384]{1,0:T(8,128)(2,1)S(1)}, bf16[512,384]{1,0:T(8,128)(2,1)S(1)}, u32[]{:S(2)}, u32[]{:S(2)}) collective-permute-start(bf16[512,384]{1,0:T(8,128)(2,1)S(1)} %collective-permute-done.6.refs_5_.refs_11_), channel_id=1, source_target_pairs={{0,2},{2,0},{1,3},{3,1},{4,6},{6,4},{5,7},{7,5},{8,10},{10,8},{9,1... | collective-permute-start | bytes 1179656 | tf_op jit(solution)/shard_map/ppermute | solution.py:34
  54.5 4.2 %collective-permute-start.9 = (bf16[512,384]{1,0:T(8,128)(2,1)S(1)}, bf16[512,384]{1,0:T(8,128)(2,1)S(1)}, u32[]{:S(2)}, u32[]{:S(2)}) collective-permute-start(bf16[512,384]{1,0:T(8,128)(2,1)S(1)} %collective-permute-done.5.refs_4_.refs_10_), channel_id=1, source_target_pairs={{0,2},{2,0},{1,3},{3,1},{4,6},{6,4},{5,7},{7,5},{8,10},{10,8},{9,1... | collective-permute-start | bytes 1179656 | tf_op jit(solution)/shard_map/ppermute | solution.py:34
  61.1 15.1 %attend_forward.1 = (f32[192,1024]{1,0:T(8,128)}, bf16[192,256]{1,0:T(8,128)(2,1)}, bf16[192,256]{1,0:T(8,128)(2,1)}, bf16[192,256]{1,0:T(8,128)(2,1)}, bf16[192,256]{1,0:T(8,128)(2,1)}, /*index=5*/f32[3,1,1024]{2,1,0:T(1,128)}) custom-call(s32[6]{0:T(128)} %stack.94.meta_ref, bf16[192,512]{1,0:T(8,128)(2,1)} %copy-done.30, bf16[192,512]{1,0:T(8,128)(2,1)} %copy-done.31, ...), custom_call_target="tpu_custom_call" | custom-call | flops 24000 | bytes 1 | tf_op jit(solution)/shard_map/attend_forward/pallas_call | solution.py:125
  76.3 5.5 %collective-permute-done.11.refs_7_ = bf16[1728,768]{1,0:T(8,128)(2,1)} collective-permute-done((bf16[1728,768]{1,0:T(8,128)(2,1)}, bf16[1728,768]{1,0:T(8,128)(2,1)}, u32[]{:S(2)}, u32[]{:S(2)}) %collective-permute-start.11) | collective-permute-done | bytes 2654240 | tf_op jit(solution)/shard_map/ppermute | solution.py:34
  81.8 5.2 %collective-permute-start.15 = (bf16[1728,768]{1,0:T(8,128)(2,1)}, bf16[1728,768]{1,0:T(8,128)(2,1)}, u32[]{:S(2)}, u32[]{:S(2)}) collective-permute-start(bf16[1728,768]{1,0:T(8,128)(2,1)} %collective-permute-done.11.refs_7_), channel_id=1, source_target_pairs={{0,2},{2,0},{1,3},{3,1},{4,6},{6,4},{5,7},{7,5},{8,10},{10,8},{9,1... | collective-permute-start | bytes 7962632 | tf_op jit(solution)/shard_map/ppermute | solution.py:34
  87.5 2.5 collective-permute-start.12
  93.4 6.2 %collective-permute-done.13.refs_2_ = bf16[192,256]{1,0:T(8,128)(2,1)S(1)} collective-permute-done((bf16[192,256]{1,0:T(8,128)(2,1)}, bf16[192,256]{1,0:T(8,128)(2,1)S(1)}, u32[]{:S(2)}, u32[]{:S(2)}) %collective-permute-start.13) | collective-permute-done | bytes 98336 | tf_op jit(solution)/shard_map/ppermute | solution.py:1069
  100.3 15.9 %middle.1 = (f32[256,768]{1,0:T(8,128)}, f32[256,768]{1,0:T(8,128)}, bf16[192,256]{1,0:T(8,128)(2,1)}, bf16[192,256]{1,0:T(8,128)(2,1)}, bf16[192,256]{1,0:T(8,1...) custom-call(s32[4]{0:T(128)} %pad_add_fusion.2.meta_ref, ...), custom_call_target="tpu_custom_call" | custom-call | flops 15000 | bytes 1 | tf_op jit(solution)/shard_map/middle/pallas_call | solution.py:642
  131.8 2.9 up_slabs.1
  138.8 15.7 %attend_backward.2 = (bf16[192,256]{1,0:T(8,128)(2,1)}, bf16[192,256]{1,0:T(8,128)(2,1)}, bf16[192,256]{1,0:T(8,128)(2,1)}, bf16[192,256]{1,0:T(8,128)(2,1)}, bf...) custom-call(s32[6]{0:T(128)} %stack.94.meta_ref, bf16[192,512]{1,0:T(8,128)(2,1)} %copy-done.30, ...), custom_call_target="tpu_custom_call" | custom-call | flops 24000 | bytes 1 | tf_op jit(solution)/shard_map/attend_backward/pallas_call | solution.py:226
  154.5 9.0 %collective-permute-done.21 = bf16[768,768]{1,0:T(8,128)(2,1)} collective-permute-done((bf16[768,768]{1,0:T(8,128)(2,1)}, bf16[768,768]{1,0:T(8,128)(2,1)}, u32[]{:S(2)}, u32[]{:S(2)}) %collective-permute-start.21) | collective-permute-done | bytes 1179680 | tf_op jit(solution)/shard_map/ppermute | solution.py:34
  168.0 9.4 %attend_backward.3 = (bf16[192,256]{1,0:T(8,128)(2,1)}, bf16[192,256]{1,0:T(8,128)(2,1)}, bf16[192,256]{1,0:T(8,128)(2,1)}, bf16[192,256]{1,0:T(8,128)(2,1)}, bf...) custom-call(s32[6]{0:T(128)} %stack.94.meta_ref, ...), custom_call_target="tpu_custom_call", output_to_operand_aliasing={{0}: (17, {}), {1}: (18, {}), {2}: (19, {}), {3}: (20, {}),... | custom-call | flops 12000 | bytes 1 | tf_op jit(solution)/shard_map/attend_backward/pallas_call | solution.py:226
  177.4 4.9 %collective-permute-done.24.refs_11_ = bf16[576,768]{1,0:T(8,128)(2,1)S(1)} collective-permute-done((bf16[576,768]{1,0:T(8,128)(2,1)}, bf16[576,768]{1,0:T(8,128)(2,1)S(1)}, u32[]{:S(2)}, u32[]{:S(2)}) %collective-permute-start.24) | collective-permute-done | bytes 884768 | tf_op jit(solution)/shard_map/ppermute | solution.py:34
  187.5 3.7 %collective-permute-start.27 = (bf16[192,2048]{1,0:T(8,128)(2,1)}, bf16[192,2048]{1,0:T(8,128)(2,1)}, u32[]{:S(2)}, u32[]{:S(2)}) collective-permute-start(bf16[192,2048]{1,0:T(8,128)(2,1)} %dynamic-slice_bitcast_fusion), channel_id=1, source_target_pairs={{0,1},{1,0},{2,3},{3,2},{4,5},{5,4},{6,7},{7,6},{8,9},{9,8},{10,11... | collective-permute-start | bytes 2359304 | tf_op jit(solution)/shard_map/ppermute | solution.py:34
  197.5 16.3 %collective-permute-done.26 = bf16[192,768]{1,0:T(8,128)(2,1)} collective-permute-done((bf16[192,768]{1,0:T(8,128)(2,1)}, bf16[192,768]{1,0:T(8,128)(2,1)}, u32[]{:S(2)}, u32[]{:S(2)}) %collective-permute-start.26) | collective-permute-done | bytes 294944 | tf_op jit(solution)/shard_map/ppermute | solution.py:1189
  221.5 11.0 %collective-permute-done.28.got_ref = bf16[1024,384]{1,0:T(8,128)(2,1)S(1)} collective-permute-done((bf16[1024,384]{1,0:T(8,128)(2,1)S(1)}, bf16[1024,384]{1,0:T(8,128)(2,1)S(1)}, u32[]{:S(2)}, u32[]{:S(2)}) %collective-permute-start.28) | collective-permute-done | bytes 786464 | tf_op jit(solution)/shard_map/ppermute | solution.py:34
  253.4 2.7 collective-permute-done.36
  258.2 2.9 collective-permute-start.48
  261.7 12.0 %collective-permute-done.40 = bf16[48,2048]{1,0:T(8,128)(2,1)S(1)} collective-permute-done((bf16[48,2048]{1,0:T(8,128)(2,1)S(1)}, bf16[48,2048]{1,0:T(8,128)(2,1)S(1)}, u32[]{:S(2)}, u32[]{:S(2)}) %collective-permute-start.40) | collective-permute-done | bytes 196640 | tf_op jit(solution)/shard_map/ppermute | solution.py:1189
  276.4 6.8 %collective-permute-done.43 = bf16[48,2048]{1,0:T(8,128)(2,1)S(1)} collective-permute-done((bf16[48,2048]{1,0:T(8,128)(2,1)S(1)}, bf16[48,2048]{1,0:T(8,128)(2,1)S(1)}, u32[]{:S(2)}, u32[]{:S(2)}) %collective-permute-start.43) | collective-permute-done | bytes 196640 | tf_op jit(solution)/shard_map/ppermute | solution.py:1189
  287.4 8.2 %collective-permute-done.45 = bf16[208,576]{1,0:T(8,128)(2,1)S(1)} collective-permute-done((bf16[208,576]{1,0:T(8,128)(2,1)S(1)}, bf16[208,576]{1,0:T(8,128)(2,1)S(1)}, u32[]{:S(2)}, u32[]{:S(2)}) %collective-permute-start.45) | collective-permute-done | bytes 239648 | tf_op jit(solution)/shard_map/ppermute | solution.py:1189
  296.8 3.8 %token_gradient.1 = f32[256,768]{1,0:T(8,128)} custom-call(s32[4]{0:T(128)S(1)} %copy-done.50, f32[256,768]{1,0:T(8,128)S(1)} %copy-done.36, bf16[192,256]{1,0:T(8,128)(2,1)S(1)} %copy-done.11, bf16[192,256]{1,0:T(8,128)(2,1)S(1)} %copy-done.44, bf16[192,256]{1,0:T(8,128)(2,1)S(1)} %copy-done.46, bf16[192,256]{1,0:T(8,128)(2,1)S(1)} %copy-done.48, ...), custom_call_target="tpu_custom_call" | custom-call | flops 4000 | bytes 1 | tf_op jit(solution)/shard_map/token_gradient/pallas_call | solution.py:888
  300.6 9.5 %collective-permute-start.51 = (bf16[384,768]{1,0:T(8,128)(2,1)S(1)}, bf16[384,768]{1,0:T(8,128)(2,1)}, u32[]{:S(2)}, u32[]{:S(2)}) collective-permute-start(bf16[384,768]{1,0:T(8,128)(2,1)S(1)} %bitcast.45), channel_id=1, source_target_pairs={{0,2},{2,0},{1,3},{3,1},{4,6},{6,4},{5,7},{7,5},{8,10},{10,8},{9,1... | collective-permute-start | bytes 1769480 | tf_op jit(solution)/shard_map/ppermute | solution.py:34
  312.2 3.3 collective-permute-start.53
  315.5 4.3 %down_finish.1 = f32[1536,768]{1,0:T(8,128)} custom-call(s32[2]{0:T(128)S(1)} %pad_add_fusion.5.meta_ref, bf16[384,768]{1,0:T(8,128)(2,1)S(1)} %bitcast.46, bf16[384,768]{1,0:T(8,128)(2,1)S(1)} %collective-permute-done.47.refs_1_, bf16[384,768]{1,0:T(8,128)(2,1)} %collective-permute-done.51.refs_2_, bf16[384,768]{1,0:T(8,128)(2,1)} %collective-permute-done.52.refs_3_), custom_call_target="tpu_custom_call" | custom-call | flops 4000 | bytes 1 | tf_op jit(solution)/shard_map/down_finish/pallas_call | solution.py:921
  322.4 2.7 head_finish.1
  326.4 5.1 %up_finish.1 = (f32[384,3072]{1,0:T(8,128)}, f32[384,768]{1,0:T(8,128)}, f32[384,128]{1,0:T(8,128)S(1)}) custom-call(s32[2]{0:T(128)S(1)} %pad_add_fusion.5.meta_ref, bf16[192,2048]{1,0:T(8,128)(2,1)S(1)} %maximum_select_fusion.1.refs_0_, bf16[192,2048]{1,0:T(8,128)(2,1)} %collective-permute-done.50.refs_1_, ...), custom_call_target="tpu_custom_call" | custom-call | flops 5000 | bytes 1 | tf_op jit(solution)/shard_map/up_finish/pallas_call | solution.py:958
  (330 shorter events, 106.4 us)
Async XLA Ops:
  6.3 20.3 %collective-permute-start = (bf16[384,576]{1,0:T(8,128)(2,1)}, bf16[384,576]{1,0:T(8,128)(2,1)S(1)}, u32[]{:S(2)}, u32[]{:S(2)}) collective-permute-start(bf16[384,576]{1,0:T(8,128)(2,1)} %get-tuple-element.175.refs_0_), channel_id=1, source_target_pairs={{0,1},{1,0},{2,3},{3,2},{4,5},{5,4},{6,7},{7,6},{8,9},{9,8},{10,11... | collective-permute-start | bytes 1327112 | tf_op jit(solution)/shard_map/ppermute | solution.py:34
  8.5 18.2 %collective-permute-start.2 = (bf16[256,768]{1,0:T(8,128)(2,1)}, bf16[256,768]{1,0:T(8,128)(2,1)S(1)}, u32[]{:S(2)}, u32[]{:S(2)}) collective-permute-start(bf16[256,768]{1,0:T(8,128)(2,1)} %get-tuple-element.174.first_ref), channel_id=1, source_target_pairs={{0,8},{8,0},{16,24},{24,16},{1,9},{9,1},{17,25},{25,17},{2,10},{10... | collective-permute-start | bytes 1179656 | tf_op jit(solution)/shard_map/ppermute | solution.py:1078
  9.8 16.9 %collective-permute-start.3 = (bf16[256,768]{1,0:T(8,128)(2,1)}, bf16[256,768]{1,0:T(8,128)(2,1)S(1)}, u32[]{:S(2)}, u32[]{:S(2)}) collective-permute-start(bf16[256,768]{1,0:T(8,128)(2,1)} %get-tuple-element.174.first_ref), channel_id=1, source_target_pairs={{0,16},{16,0},{8,24},{24,8},{1,17},{17,1},{9,25},{25,9},{2,18},{18... | collective-permute-start | bytes 1179656 | tf_op jit(solution)/shard_map/ppermute | solution.py:1079
  26.7 55.1 %collective-permute-start.11 = (bf16[1728,768]{1,0:T(8,128)(2,1)}, bf16[1728,768]{1,0:T(8,128)(2,1)}, u32[]{:S(2)}, u32[]{:S(2)}) collective-permute-start(bf16[1728,768]{1,0:T(8,128)(2,1)} %get-tuple-element.191), channel_id=1, source_target_pairs={{0,1},{1,0},{2,3},{3,2},{4,5},{5,4},{6,7},{7,6},{8,9},{9,8},{10,11... | collective-permute-start | bytes 7962632 | tf_op jit(solution)/shard_map/ppermute | solution.py:34
  40.2 19.8 %collective-permute-start.8 = (bf16[512,384]{1,0:T(8,128)(2,1)S(1)}, bf16[512,384]{1,0:T(8,128)(2,1)S(1)}, u32[]{:S(2)}, u32[]{:S(2)}) collective-permute-start(bf16[512,384]{1,0:T(8,128)(2,1)S(1)} %get-tuple-element.189.refs_3_.refs_9_), channel_id=1, source_target_pairs={{0,2},{2,0},{1,3},{3,1},{4,6},{6,4},{5,7},{7,5},{8,10},{10,8},{9,1... | collective-permute-start | bytes 1179656 | tf_op jit(solution)/shard_map/ppermute | solution.py:34
  44.6 15.3 %collective-permute-start.7 = (bf16[512,384]{1,0:T(8,128)(2,1)S(1)}, bf16[512,384]{1,0:T(8,128)(2,1)S(1)}, u32[]{:S(2)}, u32[]{:S(2)}) collective-permute-start(bf16[512,384]{1,0:T(8,128)(2,1)S(1)} %get-tuple-element.188.refs_2_.refs_8_), channel_id=1, source_target_pairs={{0,2},{2,0},{1,3},{3,1},{4,6},{6,4},{5,7},{7,5},{8,10},{10,8},{9,1... | collective-permute-start | bytes 1179656 | tf_op jit(solution)/shard_map/ppermute | solution.py:34
  81.8 17.8 %collective-permute-start.15 = (bf16[1728,768]{1,0:T(8,128)(2,1)}, bf16[1728,768]{1,0:T(8,128)(2,1)}, u32[]{:S(2)}, u32[]{:S(2)}) collective-permute-start(bf16[1728,768]{1,0:T(8,128)(2,1)} %collective-permute-done.11.refs_7_), channel_id=1, source_target_pairs={{0,2},{2,0},{1,3},{3,1},{4,6},{6,4},{5,7},{7,5},{8,10},{10,8},{9,1... | collective-permute-start | bytes 7962632 | tf_op jit(solution)/shard_map/ppermute | solution.py:34
  117.8 18.0 %collective-permute-start.18 = (bf16[192,256]{1,0:T(8,128)(2,1)}, bf16[192,256]{1,0:T(8,128)(2,1)S(1)}, u32[]{:S(2)}, u32[]{:S(2)}) collective-permute-start(bf16[192,256]{1,0:T(8,128)(2,1)} %get-tuple-element.209), channel_id=1, source_target_pairs={{0,8},{8,0},{16,24},{24,16},{1,9},{9,1},{17,25},{25,17},{2,10},{10... | collective-permute-start | bytes 294920 | tf_op jit(solution)/shard_map/ppermute | solution.py:1069
  119.6 16.2 %collective-permute-start.19 = (bf16[192,256]{1,0:T(8,128)(2,1)}, bf16[192,256]{1,0:T(8,128)(2,1)S(1)}, u32[]{:S(2)}, u32[]{:S(2)}) collective-permute-start(bf16[192,256]{1,0:T(8,128)(2,1)} %get-tuple-element.210), channel_id=1, source_target_pairs={{0,16},{16,0},{8,24},{24,8},{1,17},{17,1},{9,25},{25,9},{2,18},{18... | collective-permute-start | bytes 294920 | tf_op jit(solution)/shard_map/ppermute | solution.py:1069
  119.6 16.3 %collective-permute-start.20 = (bf16[192,256]{1,0:T(8,128)(2,1)}, bf16[192,256]{1,0:T(8,128)(2,1)S(1)}, u32[]{:S(2)}, u32[]{:S(2)}) collective-permute-start(bf16[192,256]{1,0:T(8,128)(2,1)} %get-tuple-element.211), channel_id=1, source_target_pairs={{0,24},{24,0},{8,16},{16,8},{1,25},{25,1},{9,17},{17,9},{2,26},{26... | collective-permute-start | bytes 294920 | tf_op jit(solution)/shard_map/ppermute | solution.py:1069
  135.9 27.6 %collective-permute-start.21 = (bf16[768,768]{1,0:T(8,128)(2,1)}, bf16[768,768]{1,0:T(8,128)(2,1)}, u32[]{:S(2)}, u32[]{:S(2)}) collective-permute-start(bf16[768,768]{1,0:T(8,128)(2,1)} %down_slab.2), channel_id=1, source_target_pairs={{0,1},{1,0},{2,3},{3,2},{4,5},{5,4},{6,7},{7,6},{8,9},{9,8},{10,11... | collective-permute-start | bytes 3538952 | tf_op jit(solution)/shard_map/ppermute | solution.py:34
  136.9 45.4 %collective-permute-start.23 = (bf16[384,2048]{1,0:T(8,128)(2,1)}, bf16[384,2048]{1,0:T(8,128)(2,1)}, u32[]{:S(2)}, u32[]{:S(2)}) collective-permute-start(bf16[384,2048]{1,0:T(8,128)(2,1)} %get-tuple-element.229), channel_id=1, source_target_pairs={{0,4},{4,0},{1,5},{5,1},{2,6},{6,2},{3,7},{7,3},{8,12},{12,8},{9,1... | collective-permute-start | bytes 4718600 | tf_op jit(solution)/shard_map/ppermute | solution.py:34
  138.2 44.2 %collective-permute-start.24 = (bf16[576,768]{1,0:T(8,128)(2,1)}, bf16[576,768]{1,0:T(8,128)(2,1)S(1)}, u32[]{:S(2)}, u32[]{:S(2)}) collective-permute-start(bf16[576,768]{1,0:T(8,128)(2,1)} %get-tuple-element.230), channel_id=1, source_target_pairs={{0,1},{1,0},{2,3},{3,2},{4,5},{5,4},{6,7},{7,6},{8,9},{9,8},{10,11... | collective-permute-start | bytes 2654216 | tf_op jit(solution)/shard_map/ppermute | solution.py:34
  166.1 16.2 %collective-permute-start.22 = (bf16[384,768]{1,0:T(8,128)(2,1)S(1)}, bf16[384,768]{1,0:T(8,128)(2,1)}, u32[]{:S(2)}, u32[]{:S(2)}) collective-permute-start(bf16[384,768]{1,0:T(8,128)(2,1)S(1)} %constant_dynamic-slice_fusion.6), channel_id=1, source_target_pairs={{0,8},{8,0},{16,24},{24,16},{1,9},{9,1},{17,25},{25,17},{2,10},{10... | collective-permute-start | bytes 1769480 | tf_op jit(solution)/shard_map/ppermute | solution.py:1186
  187.5 26.4 %collective-permute-start.27 = (bf16[192,2048]{1,0:T(8,128)(2,1)}, bf16[192,2048]{1,0:T(8,128)(2,1)}, u32[]{:S(2)}, u32[]{:S(2)}) collective-permute-start(bf16[192,2048]{1,0:T(8,128)(2,1)} %dynamic-slice_bitcast_fusion), channel_id=1, source_target_pairs={{0,1},{1,0},{2,3},{3,2},{4,5},{5,4},{6,7},{7,6},{8,9},{9,8},{10,11... | collective-permute-start | bytes 2359304 | tf_op jit(solution)/shard_map/ppermute | solution.py:34
  193.6 20.3 %collective-permute-start.26 = (bf16[192,768]{1,0:T(8,128)(2,1)}, bf16[192,768]{1,0:T(8,128)(2,1)}, u32[]{:S(2)}, u32[]{:S(2)}) collective-permute-start(bf16[192,768]{1,0:T(8,128)(2,1)} %constant_dynamic-slice_fusion.5), channel_id=1, source_target_pairs={{0,16},{16,0},{8,24},{24,8},{1,17},{17,1},{9,25},{25,9},{2,18},{18... | collective-permute-start | bytes 884744 | tf_op jit(solution)/shard_map/ppermute | solution.py:1189
  193.7 25.8 %collective-permute-start.29 = (bf16[192,256]{1,0:T(8,128)(2,1)S(1)}, bf16[192,256]{1,0:T(8,128)(2,1)S(1)}, u32[]{:S(2)}, u32[]{:S(2)}) collective-permute-start(bf16[192,256]{1,0:T(8,128)(2,1)S(1)} %copy-done.22), channel_id=1, source_target_pairs={{0,8},{8,0},{16,24},{24,16},{1,9},{9,1},{17,25},{25,17},{2,10},{10... | collective-permute-start | bytes 294920 | tf_op jit(solution)/shard_map/ppermute | solution.py:1069
  194.6 25.6 %collective-permute-start.30 = (bf16[192,256]{1,0:T(8,128)(2,1)S(1)}, bf16[192,256]{1,0:T(8,128)(2,1)S(1)}, u32[]{:S(2)}, u32[]{:S(2)}) collective-permute-start(bf16[192,256]{1,0:T(8,128)(2,1)S(1)} %copy-done.23), channel_id=1, source_target_pairs={{0,16},{16,0},{8,24},{24,8},{1,17},{17,1},{9,25},{25,9},{2,18},{18... | collective-permute-start | bytes 294920 | tf_op jit(solution)/shard_map/ppermute | solution.py:1069
  196.2 24.7 %collective-permute-start.31 = (bf16[192,256]{1,0:T(8,128)(2,1)S(1)}, bf16[192,256]{1,0:T(8,128)(2,1)S(1)}, u32[]{:S(2)}, u32[]{:S(2)}) collective-permute-start(bf16[192,256]{1,0:T(8,128)(2,1)S(1)} %copy-done.26), channel_id=1, source_target_pairs={{0,24},{24,0},{8,16},{16,8},{1,25},{25,1},{9,17},{17,9},{2,26},{26... | collective-permute-start | bytes 294920 | tf_op jit(solution)/shard_map/ppermute | solution.py:1069
  213.9 18.6 %collective-permute-start.28 = (bf16[1024,384]{1,0:T(8,128)(2,1)S(1)}, bf16[1024,384]{1,0:T(8,128)(2,1)S(1)}, u32[]{:S(2)}, u32[]{:S(2)}) collective-permute-start(bf16[1024,384]{1,0:T(8,128)(2,1)S(1)} %add_convert_fusion.2), channel_id=1, source_target_pairs={{0,4},{4,0},{1,5},{5,1},{2,6},{6,2},{3,7},{7,3},{8,12},{12,8},{9,1... | collective-permute-start | bytes 2359304 | tf_op jit(solution)/shard_map/ppermute | solution.py:34
  216.3 22.7 %collective-permute-start.32 = (bf16[96,768]{1,0:T(8,128)(2,1)}, bf16[96,768]{1,0:T(8,128)(2,1)}, u32[]{:S(2)}, u32[]{:S(2)}) collective-permute-start(bf16[96,768]{1,0:T(8,128)(2,1)} %constant_dynamic-slice_fusion.4), channel_id=1, source_target_pairs={{0,4},{4,0},{1,5},{5,1},{2,6},{6,2},{3,7},{7,3},{8,12},{12,8},{9,1... | collective-permute-start | bytes 442376 | tf_op jit(solution)/shard_map/ppermute | solution.py:34
  220.1 29.3 %collective-permute-start.35 = (bf16[96,2048]{1,0:T(8,128)(2,1)}, bf16[96,2048]{1,0:T(8,128)(2,1)}, u32[]{:S(2)}, u32[]{:S(2)}) collective-permute-start(bf16[96,2048]{1,0:T(8,128)(2,1)} %constant_dynamic-slice_fusion.3), channel_id=1, source_target_pairs={{0,8},{8,0},{16,24},{24,16},{1,9},{9,1},{17,25},{25,17},{2,10},{10... | collective-permute-start | bytes 1179656 | tf_op jit(solution)/shard_map/ppermute | solution.py:1186
  239.0 19.2 %collective-permute-start.37 = (bf16[384,256]{1,0:T(8,128)(2,1)}, bf16[384,256]{1,0:T(8,128)(2,1)S(1)}, u32[]{:S(2)}, u32[]{:S(2)}) collective-permute-start(bf16[384,256]{1,0:T(8,128)(2,1)} %copy-done.20), channel_id=1, source_target_pairs={{0,8},{8,0},{16,24},{24,16},{1,9},{9,1},{17,25},{25,17},{2,10},{10... | collective-permute-start | bytes 589832 | tf_op jit(solution)/shard_map/ppermute | solution.py:1069
  239.0 22.0 %collective-permute-start.38 = (bf16[384,256]{1,0:T(8,128)(2,1)}, bf16[384,256]{1,0:T(8,128)(2,1)S(1)}, u32[]{:S(2)}, u32[]{:S(2)}) collective-permute-start(bf16[384,256]{1,0:T(8,128)(2,1)} %copy-done.18), channel_id=1, source_target_pairs={{0,16},{16,0},{8,24},{24,8},{1,17},{17,1},{9,25},{25,9},{2,18},{18... | collective-permute-start | bytes 589832 | tf_op jit(solution)/shard_map/ppermute | solution.py:1069
  242.3 19.3 %collective-permute-start.39 = (bf16[384,256]{1,0:T(8,128)(2,1)}, bf16[384,256]{1,0:T(8,128)(2,1)S(1)}, u32[]{:S(2)}, u32[]{:S(2)}) collective-permute-start(bf16[384,256]{1,0:T(8,128)(2,1)} %copy-done.16), channel_id=1, source_target_pairs={{0,24},{24,0},{8,16},{16,8},{1,25},{25,1},{9,17},{17,9},{2,26},{26... | collective-permute-start | bytes 589832 | tf_op jit(solution)/shard_map/ppermute | solution.py:1069
  249.4 24.3 %collective-permute-start.41 = (bf16[96,768]{1,0:T(8,128)(2,1)S(1)}, bf16[96,768]{1,0:T(8,128)(2,1)S(1)}, u32[]{:S(2)}, u32[]{:S(2)}) collective-permute-start(bf16[96,768]{1,0:T(8,128)(2,1)S(1)} %add_convert_fusion.9), channel_id=1, source_target_pairs={{0,16},{16,0},{8,24},{24,8},{1,17},{17,1},{9,25},{25,9},{2,18},{18... | collective-permute-start | bytes 442376 | tf_op jit(solution)/shard_map/ppermute | solution.py:1189
  256.1 17.6 %collective-permute-start.40 = (bf16[48,2048]{1,0:T(8,128)(2,1)S(1)}, bf16[48,2048]{1,0:T(8,128)(2,1)S(1)}, u32[]{:S(2)}, u32[]{:S(2)}) collective-permute-start(bf16[48,2048]{1,0:T(8,128)(2,1)S(1)} %constant_dynamic-slice_fusion.2), channel_id=1, source_target_pairs={{0,16},{16,0},{8,24},{24,8},{1,17},{17,1},{9,25},{25,9},{2,18},{18... | collective-permute-start | bytes 589832 | tf_op jit(solution)/shard_map/ppermute | solution.py:1189
  258.2 38.5 %collective-permute-start.48 = (bf16[576,768]{1,0:T(8,128)(2,1)S(1)}, bf16[576,768]{1,0:T(8,128)(2,1)S(1)}, u32[]{:S(2)}, u32[]{:S(2)}) collective-permute-start(bf16[576,768]{1,0:T(8,128)(2,1)S(1)} %copy-done.35), channel_id=1, source_target_pairs={{0,2},{2,0},{1,3},{3,1},{4,6},{6,4},{5,7},{7,5},{8,10},{10,8},{9,1... | collective-permute-start | bytes 2654216 | tf_op jit(solution)/shard_map/ppermute | solution.py:34
  275.6 20.0 %collective-permute-start.45 = (bf16[208,576]{1,0:T(8,128)(2,1)S(1)}, bf16[208,576]{1,0:T(8,128)(2,1)S(1)}, u32[]{:S(2)}, u32[]{:S(2)}) collective-permute-start(bf16[208,576]{1,0:T(8,128)(2,1)S(1)} %add_convert_fusion.6), channel_id=1, source_target_pairs={{0,16},{16,0},{8,24},{24,8},{1,17},{17,1},{9,25},{25,9},{2,18},{18... | collective-permute-start | bytes 718856 | tf_op jit(solution)/shard_map/ppermute | solution.py:1189
  287.0 23.1 %collective-permute-start.47 = (bf16[384,768]{1,0:T(8,128)(2,1)S(1)}, bf16[384,768]{1,0:T(8,128)(2,1)S(1)}, u32[]{:S(2)}, u32[]{:S(2)}) collective-permute-start(bf16[384,768]{1,0:T(8,128)(2,1)S(1)} %bitcast.44), channel_id=1, source_target_pairs={{0,4},{4,0},{1,5},{5,1},{2,6},{6,2},{3,7},{7,3},{8,12},{12,8},{9,1... | collective-permute-start | bytes 1769480 | tf_op jit(solution)/shard_map/ppermute | solution.py:34
  296.0 23.7 %collective-permute-start.50 = (bf16[192,2048]{1,0:T(8,128)(2,1)S(1)}, bf16[192,2048]{1,0:T(8,128)(2,1)}, u32[]{:S(2)}, u32[]{:S(2)}) collective-permute-start(bf16[192,2048]{1,0:T(8,128)(2,1)S(1)} %maximum_select_fusion.1.refs_0_), channel_id=1, source_target_pairs={{0,4},{4,0},{1,5},{5,1},{2,6},{6,2},{3,7},{7,3},{8,12},{12,8},{9,1... | collective-permute-start | bytes 2359304 | tf_op jit(solution)/shard_map/ppermute | solution.py:34
  300.6 14.9 %collective-permute-start.51 = (bf16[384,768]{1,0:T(8,128)(2,1)S(1)}, bf16[384,768]{1,0:T(8,128)(2,1)}, u32[]{:S(2)}, u32[]{:S(2)}) collective-permute-start(bf16[384,768]{1,0:T(8,128)(2,1)S(1)} %bitcast.45), channel_id=1, source_target_pairs={{0,2},{2,0},{1,3},{3,1},{4,6},{6,4},{5,7},{7,5},{8,10},{10,8},{9,1... | collective-permute-start | bytes 1769480 | tf_op jit(solution)/shard_map/ppermute | solution.py:34
  (105 other events, 838.6 us)
